TPU v7x, 32 devices: a whole 2x2x4 slice. The times are simulated.
32 devices in a mesh: dp: 16 (over z, x, core), tensor: 2 (over y).
Axes of the slice: x: 2, y: 2, z: 4, core: 2. Of those that a mesh axis runs over, the one named last changes fastest.
Arguments:
- x_input: bfloat16 [16, 768, 1536], P('dp', 'tensor'), may hold values from -6 to 6
- cond_tokens: bfloat16 [16, 130, 1536], P('dp'), may hold values from -6 to 6
- teacher: bfloat16 [16, 768, 1536], P('dp', 'tensor'), may hold values from -6 to 6
- valid_mask: int32 [16, 768], P('dp', 'tensor'), may hold values from 0 to 1, as said below
- norm_gains: bfloat16 [3, 1536], P(None, 'dp'), may hold values from 0.099609375 to 1.8984375
- w_query: bfloat16 [1536, 1536], P('dp', 'tensor'), may hold values from -0.15625 to 0.15625
- w_key: bfloat16 [1536, 1536], P('dp', 'tensor'), may hold values from -0.15625 to 0.15625
- w_value: bfloat16 [1536, 1536], P('dp', 'tensor'), may hold values from -0.15625 to 0.15625
- w_out: bfloat16 [1536, 1536], P('tensor', 'dp'), may hold values from -3 to 3
- c_query: bfloat16 [1536, 1536], P('dp', 'tensor'), may hold values from -0.15625 to 0.15625
- c_key: bfloat16 [1536, 1536], P('dp', 'tensor'), may hold values from -0.15625 to 0.15625
- c_value: bfloat16 [1536, 1536], P('dp', 'tensor'), may hold values from -0.15625 to 0.15625
- c_out: bfloat16 [1536, 1536], P('tensor', 'dp'), may hold values from -1.25 to 1.25
- w_gate: bfloat16 [1536, 6144], P('dp', 'tensor'), may hold values from -0.15625 to 0.15625
- w_up: bfloat16 [1536, 6144], P('dp', 'tensor'), may hold values from -0.15625 to 0.15625
- w_down: bfloat16 [6144, 1536], P('tensor', 'dp'), may hold values from -0.078125 to 0.078125
Outputs:
- output: bfloat16 [16, 768, 1536], P('dp', 'tensor')
- mean_loss: float32 [], replicated
- grad_input: float32 [16, 768, 1536], P('dp', 'tensor')
- grad_cond: float32 [16, 130, 1536], P('dp')
- grad_w_query: float32 [1536, 1536], P('dp', 'tensor')
- grad_w_key: float32 [1536, 1536], P('dp', 'tensor')
- grad_w_value: float32 [1536, 1536], P('dp', 'tensor')
- grad_w_out: float32 [1536, 1536], P('tensor', 'dp')
- grad_c_query: float32 [1536, 1536], P('dp', 'tensor')
- grad_c_key: float32 [1536, 1536], P('dp', 'tensor')
- grad_c_value: float32 [1536, 1536], P('dp', 'tensor')
- grad_c_out: float32 [1536, 1536], P('tensor', 'dp')
- grad_w_gate: float32 [1536, 6144], P('dp', 'tensor')
- grad_w_up: float32 [1536, 6144], P('dp', 'tensor')
- grad_w_down: float32 [6144, 1536], P('tensor', 'dp')
- grad_norm_gains: float32 [3, 1536], P(None, 'dp')
Inputs may be any that keep to these rules, and one draw needn't show every extreme that they name: `valid_mask`: the valid tokens of each latent form a prefix of it, and every latent has a valid token.
All inputs are finite; a program needn't handle non-finite values.
Results may differ from a plain program's by a relative error of at most 0.017.
Values may be sent and summed in bfloat16 or wider, within the bound.
No kernel may reach another device: no remote copies, remote signals or barrier semaphores. Data moves between devices by JAX's collectives and lax.ppermute only.
A program may use at most 256 MiB of HBM per device.

v0:
```python
import math

import jax
import jax.numpy as jnp
from jax import lax
from jax.sharding import PartitionSpec as P

HEAD_DIM = 64


EPSILON = 1e-05


def matmul(left_side, right_side):
    return jnp.dot(left_side, right_side, preferred_element_type=jnp.float32)


def contract_rows(left_side, right_side):
    return lax.dot_general(
        left_side, right_side, (((0,), (0,)), ((), ())), preferred_element_type=jnp.float32
    )


def times_transposed(left_side, right_side):
    return lax.dot_general(
        left_side, right_side, (((1,), (1,)), ((), ())), preferred_element_type=jnp.float32
    )


def norm_stats(values):
    row_mean = jnp.mean(values, axis=-1, keepdims=True)
    centred = values - row_mean
    row_var = jnp.mean(centred * centred, axis=-1, keepdims=True)
    inverse = lax.rsqrt(row_var + EPSILON)
    return (centred * inverse, inverse)


def norm_back(grad_normed, normed, inverse, gain_row):
    scaled = grad_normed * gain_row
    mean_scaled = jnp.mean(scaled, axis=-1, keepdims=True)
    mean_product = jnp.mean(scaled * normed, axis=-1, keepdims=True)
    grad_values = inverse * (scaled - mean_scaled - normed * mean_product)
    return (grad_values, jnp.sum(grad_normed * normed, axis=0))


def rotary_tables(length):
    half_dim = HEAD_DIM // 2
    freqs = jnp.exp(jnp.arange(half_dim, dtype=jnp.float32) * (-math.log(10000.0) / half_dim))
    angles = jnp.arange(length, dtype=jnp.float32)[:, None] * freqs[None, :]
    return (jnp.cos(angles)[:, None, :], jnp.sin(angles)[:, None, :])


def rotate(values, rot_cos, rot_sin):
    half_dim = HEAD_DIM // 2
    lower = values[..., :half_dim]
    upper = values[..., half_dim:]
    return jnp.concatenate(
        [lower * rot_cos - upper * rot_sin, upper * rot_cos + lower * rot_sin], axis=-1
    )


def rotate_back(values, rot_cos, rot_sin):
    half_dim = HEAD_DIM // 2
    lower = values[..., :half_dim]
    upper = values[..., half_dim:]
    return jnp.concatenate(
        [lower * rot_cos + upper * rot_sin, upper * rot_cos - lower * rot_sin], axis=-1
    )


def attend_forward(queries, keys_in, values_in):
    scale_factor = HEAD_DIM ** (-0.5)
    scores = (
        jnp.einsum("qhd,khd->hqk", queries, keys_in, preferred_element_type=jnp.float32)
        * scale_factor
    )
    row_max = jnp.max(scores, axis=-1, keepdims=True)
    shifted = jnp.exp(scores - row_max)
    row_total = jnp.sum(shifted, axis=-1, keepdims=True)
    soft_probs = (shifted / row_total).astype(jnp.bfloat16)
    mixed = jnp.einsum("hqk,khd->qhd", soft_probs, values_in, preferred_element_type=jnp.float32)
    return (mixed, row_max + jnp.log(row_total))


def attend_back(queries, keys_in, values_in, log_total, grad_mixed):
    scale_factor = HEAD_DIM ** (-0.5)
    scores = (
        jnp.einsum("qhd,khd->hqk", queries, keys_in, preferred_element_type=jnp.float32)
        * scale_factor
    )
    soft_probs = jnp.exp(scores - log_total)
    grad_values = jnp.einsum(
        "hqk,qhd->khd",
        soft_probs.astype(jnp.bfloat16),
        grad_mixed,
        preferred_element_type=jnp.float32,
    )
    grad_probs = jnp.einsum(
        "qhd,khd->hqk", grad_mixed, values_in, preferred_element_type=jnp.float32
    )
    weighted = jnp.sum(soft_probs * grad_probs, axis=-1, keepdims=True)
    grad_scores = (soft_probs * (grad_probs - weighted)).astype(jnp.bfloat16)
    grad_queries = (
        jnp.einsum("hqk,khd->qhd", grad_scores, keys_in, preferred_element_type=jnp.float32)
        * scale_factor
    )
    grad_keys = (
        jnp.einsum("hqk,qhd->khd", grad_scores, queries, preferred_element_type=jnp.float32)
        * scale_factor
    )
    return (grad_queries, grad_keys, grad_values)


def body(
    x_input,
    cond_tokens,
    teacher,
    valid_mask,
    norm_gains,
    w_query,
    w_key,
    w_value,
    w_out,
    c_query,
    c_key,
    c_value,
    c_out,
    w_gate,
    w_up,
    w_down,
):
    bf_type = jnp.bfloat16

    def fetch_attention():
        return (
            lax.all_gather(w_query, "dp", axis=0, tiled=True),
            lax.all_gather(w_key, "dp", axis=0, tiled=True),
            lax.all_gather(w_value, "dp", axis=0, tiled=True),
            lax.all_gather(w_out, "dp", axis=1, tiled=True),
            lax.all_gather(c_query, "dp", axis=0, tiled=True),
            lax.all_gather(c_key, "dp", axis=0, tiled=True),
            lax.all_gather(c_value, "dp", axis=0, tiled=True),
            lax.all_gather(c_out, "dp", axis=1, tiled=True),
            lax.all_gather(norm_gains, "dp", axis=1, tiled=True),
        )

    def fetch_mlp():
        return (
            lax.all_gather(w_gate, "dp", axis=0, tiled=True),
            lax.all_gather(w_up, "dp", axis=0, tiled=True),
            lax.all_gather(w_down, "dp", axis=1, tiled=True),
        )

    def gather_rows(values):
        return lax.all_gather(values, "tensor", axis=0, tiled=True)

    def scatter_rows(values):
        return lax.psum_scatter(values, "tensor", scatter_dimension=0, tiled=True)

    def gather_grads(values):
        return lax.all_gather(values, "tensor", axis=0, tiled=True)

    def scatter_grads(values):
        return lax.psum_scatter(values, "tensor", scatter_dimension=0, tiled=True)

    local_rows = x_input[0].astype(jnp.float32)
    cond_rows = cond_tokens[0]
    mask_float = valid_mask[0].astype(jnp.float32)
    width = local_rows.shape[1]
    token_total = float(lax.axis_size("dp") * lax.axis_size("tensor") * local_rows.shape[0])
    weight_q, weight_k, weight_v, weight_o, cross_q, cross_k, cross_v, cross_o, gains_bf = (
        fetch_attention()
    )
    gains = gains_bf.astype(jnp.float32)
    normed_one, inverse_one = norm_stats(local_rows)
    input_one = gather_rows((normed_one * gains[0]).astype(bf_type))
    length = input_one.shape[0]
    ctx_len = cond_rows.shape[0]
    rot_cos, rot_sin = rotary_tables(length)
    query_rot = rotate(
        matmul(input_one, weight_q).reshape(length, -1, HEAD_DIM), rot_cos, rot_sin
    ).astype(bf_type)
    key_rot = rotate(
        matmul(input_one, weight_k).reshape(length, -1, HEAD_DIM), rot_cos, rot_sin
    ).astype(bf_type)
    value_self = matmul(input_one, weight_v).astype(bf_type).reshape(length, -1, HEAD_DIM)
    mixed_self, log_self = attend_forward(query_rot, key_rot, value_self)
    mixed_self = mixed_self.reshape(length, -1).astype(bf_type)
    hidden_one = local_rows + scatter_rows(matmul(mixed_self, weight_o))
    normed_two, inverse_two = norm_stats(hidden_one)
    input_two = gather_rows((normed_two * gains[1]).astype(bf_type))
    query_cross = matmul(input_two, cross_q).astype(bf_type).reshape(length, -1, HEAD_DIM)
    key_cross = matmul(cond_rows, cross_k).astype(bf_type).reshape(ctx_len, -1, HEAD_DIM)
    value_cross = matmul(cond_rows, cross_v).astype(bf_type).reshape(ctx_len, -1, HEAD_DIM)
    mixed_cross, log_cross = attend_forward(query_cross, key_cross, value_cross)
    mixed_cross = mixed_cross.reshape(length, -1).astype(bf_type)
    hidden_two = hidden_one + scatter_rows(matmul(mixed_cross, cross_o))
    weight_gate, weight_up, weight_down = fetch_mlp()
    normed_three, inverse_three = norm_stats(hidden_two)
    input_three = gather_rows((normed_three * gains[2]).astype(bf_type))
    gate_pre = matmul(input_three, weight_gate)
    up_pre = matmul(input_three, weight_up)
    gate_sigmoid = jax.nn.sigmoid(gate_pre)
    gate_silu = gate_pre * gate_sigmoid
    hidden_ff = (gate_silu * up_pre).astype(bf_type)
    block_out = hidden_two + scatter_rows(matmul(hidden_ff, weight_down))
    error_diff = block_out - teacher[0].astype(jnp.float32)
    local_error = jnp.sum(mask_float[:, None] * error_diff * error_diff)
    valid_count, error_total = lax.psum((jnp.sum(mask_float), local_error), ("dp", "tensor"))
    mean_loss = error_total / (width * valid_count)
    grad_out = 2.0 * token_total / valid_count * mask_float[:, None] * error_diff
    weight_gate, weight_up, weight_down = fetch_mlp()
    branch_three = gather_grads(grad_out.astype(bf_type))
    grad_hidden = times_transposed(branch_three, weight_down)
    grad_down = contract_rows(hidden_ff, branch_three)
    grad_gate = (
        grad_hidden * up_pre * gate_sigmoid * (1.0 + gate_pre * (1.0 - gate_sigmoid))
    ).astype(bf_type)
    grad_upper = (grad_hidden * gate_silu).astype(bf_type)
    grad_gate_w = contract_rows(input_three, grad_gate)
    grad_up_w = contract_rows(input_three, grad_upper)
    grad_normed_three = scatter_grads(
        times_transposed(grad_gate, weight_gate) + times_transposed(grad_upper, weight_up)
    )
    grad_gate_s, grad_up_s, grad_down_s = (
        lax.psum_scatter(grad_gate_w, "dp", scatter_dimension=0, tiled=True),
        lax.psum_scatter(grad_up_w, "dp", scatter_dimension=0, tiled=True),
        lax.psum_scatter(grad_down, "dp", scatter_dimension=1, tiled=True),
    )
    back_three, gain_three = norm_back(grad_normed_three, normed_three, inverse_three, gains[2])
    grad_two = grad_out + back_three
    weight_q, weight_k, weight_v, weight_o, cross_q, cross_k, cross_v, cross_o, spare_gains = (
        fetch_attention()
    )
    branch_two = gather_grads(grad_two.astype(bf_type))
    grad_cross_o = contract_rows(mixed_cross, branch_two)
    grad_mixed_cross = (
        times_transposed(branch_two, cross_o).astype(bf_type).reshape(length, -1, HEAD_DIM)
    )
    grad_qc, grad_kc, grad_vc = attend_back(
        query_cross, key_cross, value_cross, log_cross, grad_mixed_cross
    )
    grad_qc = grad_qc.reshape(length, -1).astype(bf_type)
    grad_kc = grad_kc.reshape(ctx_len, -1).astype(bf_type)
    grad_vc = grad_vc.reshape(ctx_len, -1).astype(bf_type)
    grad_cross_q = contract_rows(input_two, grad_qc)
    grad_cross_k = contract_rows(cond_rows, grad_kc)
    grad_cross_v = contract_rows(cond_rows, grad_vc)
    cond_part = times_transposed(grad_kc, cross_k) + times_transposed(grad_vc, cross_v)
    grad_normed_two = scatter_grads(times_transposed(grad_qc, cross_q))
    back_two, gain_two = norm_back(grad_normed_two, normed_two, inverse_two, gains[1])
    grad_one = grad_two + back_two
    branch_one = gather_grads(grad_one.astype(bf_type))
    grad_self_o = contract_rows(mixed_self, branch_one)
    grad_mixed_self = (
        times_transposed(branch_one, weight_o).astype(bf_type).reshape(length, -1, HEAD_DIM)
    )
    grad_qs, grad_ks, grad_vs = attend_back(
        query_rot, key_rot, value_self, log_self, grad_mixed_self
    )
    grad_qs = rotate_back(grad_qs, rot_cos, rot_sin).reshape(length, -1).astype(bf_type)
    grad_ks = rotate_back(grad_ks, rot_cos, rot_sin).reshape(length, -1).astype(bf_type)
    grad_vs = grad_vs.reshape(length, -1).astype(bf_type)
    grad_self_q = contract_rows(input_one, grad_qs)
    grad_self_k = contract_rows(input_one, grad_ks)
    grad_self_v = contract_rows(input_one, grad_vs)
    grad_normed_one = scatter_grads(
        times_transposed(grad_qs, weight_q)
        + times_transposed(grad_ks, weight_k)
        + times_transposed(grad_vs, weight_v)
    )
    back_one, gain_one = norm_back(grad_normed_one, normed_one, inverse_one, gains[0])
    grad_rows = grad_one + back_one
    gain_part = jnp.stack([gain_one, gain_two, gain_three])
    cond_sum, gain_sum = (
        lax.psum(cond_part.astype(jnp.bfloat16), "tensor").astype(jnp.float32),
        lax.psum(gain_part.astype(jnp.bfloat16), "tensor").astype(jnp.float32),
    )
    (
        grad_q_s,
        grad_k_s,
        grad_v_s,
        grad_o_s,
        grad_cq_s,
        grad_ck_s,
        grad_cv_s,
        grad_co_s,
        grad_gain_s,
    ) = (
        lax.psum_scatter(grad_self_q, "dp", scatter_dimension=0, tiled=True),
        lax.psum_scatter(grad_self_k, "dp", scatter_dimension=0, tiled=True),
        lax.psum_scatter(grad_self_v, "dp", scatter_dimension=0, tiled=True),
        lax.psum_scatter(grad_self_o, "dp", scatter_dimension=1, tiled=True),
        lax.psum_scatter(grad_cross_q, "dp", scatter_dimension=0, tiled=True),
        lax.psum_scatter(grad_cross_k, "dp", scatter_dimension=0, tiled=True),
        lax.psum_scatter(grad_cross_v, "dp", scatter_dimension=0, tiled=True),
        lax.psum_scatter(grad_cross_o, "dp", scatter_dimension=1, tiled=True),
        lax.psum_scatter(gain_sum, "dp", scatter_dimension=1, tiled=True),
    )
    return (
        block_out.astype(bf_type)[None],
        mean_loss,
        grad_rows[None],
        cond_sum[None],
        grad_q_s,
        grad_k_s,
        grad_v_s,
        grad_o_s,
        grad_cq_s,
        grad_ck_s,
        grad_cv_s,
        grad_co_s,
        grad_gate_s,
        grad_up_s,
        grad_down_s,
        grad_gain_s,
    )


def solution(mesh):
    return jax.shard_map(
        body,
        mesh=mesh,
        in_specs=(
            P("dp", "tensor", None),
            P("dp", None, None),
            P("dp", "tensor", None),
            P("dp", "tensor"),
            P(None, "dp"),
            P("dp", "tensor"),
            P("dp", "tensor"),
            P("dp", "tensor"),
            P("tensor", "dp"),
            P("dp", "tensor"),
            P("dp", "tensor"),
            P("dp", "tensor"),
            P("tensor", "dp"),
            P("dp", "tensor"),
            P("dp", "tensor"),
            P("tensor", "dp"),
        ),
        out_specs=(
            P("dp", "tensor", None),
            P(),
            P("dp", "tensor", None),
            P("dp", None, None),
            P("dp", "tensor"),
            P("dp", "tensor"),
            P("dp", "tensor"),
            P("tensor", "dp"),
            P("dp", "tensor"),
            P("dp", "tensor"),
            P("dp", "tensor"),
            P("tensor", "dp"),
            P("dp", "tensor"),
            P("dp", "tensor"),
            P("tensor", "dp"),
            P(None, "dp"),
        ),
        check_vma=False,
    )
```

profile of v0, /device:TPU:0, one launch (start us, length us, event | category | flops | bytes accessed | tf_op | source)
XLA Modules:
  0.0 2734.9 jit_solution(5155967029090758559)
XLA Ops:
  10.6 23.1 all-gather
  39.1 30.3 %all-gather.19.cloned.1.call-done = bf16[768,1536]{1,0:T(8,128)(2,1)} async-done(((bf16[384,1536]{1,0:T(8,128)(2,1)}), bf16[768,1536]{1,0:T(8,128)(2,1)}) %all-gather.19.cloned.1.call-update) | async-done | bytes 2359312 | tf_op jit(solution)/shard_map/all_gather | solution.py:155
  69.5 44.6 %all-gather.25.cloned.1.call-done = bf16[1536,768]{1,0:T(8,128)(2,1)} async-done(((bf16[96,768]{1,0:T(8,128)(2,1)}), bf16[1536,768]{1,0:T(8,128)(2,1)}) %all-gather.25.cloned.1.call-update) | async-done | bytes 2359312 | tf_op jit(solution)/shard_map/all_gather | solution.py:137
  118.6 38.9 %all-gather.23.cloned.1.call-done = bf16[1536,768]{1,0:T(8,128)(2,1)} async-done(((bf16[96,768]{1,0:T(8,128)(2,1)}), bf16[1536,768]{1,0:T(8,128)(2,1)}) %all-gather.23.cloned.1.call-update) | async-done | bytes 2359312 | tf_op jit(solution)/shard_map/all_gather | solution.py:136
  162.9 11.6 multiply_reduce_fusion.1
  174.5 12.4 fusion
  186.9 13.9 all-gather.21.cloned.1.call-done
  205.5 12.0 fusion.36
  217.5 26.6 all-gather.27.cloned.1.call-done
  244.1 5.8 fusion.62
  252.2 56.6 %reduce-scatter.25.cloned.1.call-done = f32[384,1536]{1,0:T(8,128)} async-done(((f32[768,1536]{1,0:T(8,128)}), f32[384,1536]{1,0:T(8,128)}) %reduce-scatter.25.cloned.1.call-update) | async-done | bytes 2359312 | tf_op jit(solution)/shard_map/reduce_scatter | solution.py:158
  314.1 39.7 %all-gather.29.cloned.1.call-done = bf16[1536,768]{1,0:T(8,128)(2,1)} async-done(((bf16[96,768]{1,0:T(8,128)(2,1)}), bf16[1536,768]{1,0:T(8,128)(2,1)}) %all-gather.29.cloned.1.call-update) | async-done | bytes 2359312 | tf_op jit(solution)/shard_map/all_gather | solution.py:142
  356.9 40.6 %all-gather.35.cloned.1.call-done = bf16[1536,768]{1,0:T(8,128)(2,1)} async-done(((bf16[96,768]{1,0:T(8,128)(2,1)}), bf16[1536,768]{1,0:T(8,128)(2,1)}) %all-gather.35.cloned.1.call-update) | async-done | bytes 2359312 | tf_op jit(solution)/shard_map/all_gather | solution.py:141
  399.8 41.3 %all-gather.33.cloned.1.call-done = bf16[1536,768]{1,0:T(8,128)(2,1)} async-done(((bf16[96,768]{1,0:T(8,128)(2,1)}), bf16[1536,768]{1,0:T(8,128)(2,1)}) %all-gather.33.cloned.1.call-update) | async-done | bytes 2359312 | tf_op jit(solution)/shard_map/all_gather | solution.py:140
  441.1 36.9 %all-gather.31.cloned.1.call-done = bf16[768,1536]{1,0:T(8,128)(2,1)} async-done(((bf16[384,1536]{1,0:T(8,128)(2,1)}), bf16[768,1536]{1,0:T(8,128)(2,1)}) %all-gather.31.cloned.1.call-update) | async-done | bytes 2359312 | tf_op jit(solution)/shard_map/all_gather | solution.py:155
  488.3 34.7 %all-gather.37.cloned.1.call-done = bf16[768,1536]{0,1:T(8,128)(2,1)} async-done(((bf16[768,96]{0,1:T(8,128)(2,1)}), bf16[768,1536]{0,1:T(8,128)(2,1)}) %all-gather.37.cloned.1.call-update) | async-done | bytes 2359312 | tf_op jit(solution)/shard_map/all_gather | solution.py:143
  523.0 6.2 fusion.63
  530.0 58.1 %reduce-scatter.27.cloned.1.call-done = f32[384,1536]{1,0:T(8,128)} async-done(((f32[768,1536]{1,0:T(8,128)}), f32[384,1536]{1,0:T(8,128)}) %reduce-scatter.27.cloned.1.call-update) | async-done | bytes 2359312 | tf_op jit(solution)/shard_map/reduce_scatter | solution.py:158
  594.8 77.1 %all-gather.41.cloned.1.call-done = bf16[1536,3072]{1,0:T(8,128)(2,1)} async-done(((bf16[96,3072]{1,0:T(8,128)(2,1)}), bf16[1536,3072]{1,0:T(8,128)(2,1)}) %all-gather.41.cloned.1.call-update) | async-done | bytes 9437200 | tf_op jit(solution)/shard_map/all_gather | solution.py:149
  671.9 36.2 %all-gather.39.cloned.1.call-done = bf16[768,1536]{1,0:T(8,128)(2,1)} async-done(((bf16[384,1536]{1,0:T(8,128)(2,1)}), bf16[768,1536]{1,0:T(8,128)(2,1)}) %all-gather.39.cloned.1.call-update) | async-done | bytes 2359312 | tf_op jit(solution)/shard_map/all_gather | solution.py:155
  708.1 14.1 fusion.64
  722.2 69.5 %all-gather.43.cloned.1.call-done = bf16[1536,3072]{1,0:T(8,128)(2,1)} async-done(((bf16[96,3072]{1,0:T(8,128)(2,1)}), bf16[1536,3072]{1,0:T(8,128)(2,1)}) %all-gather.43.cloned.1.call-update) | async-done | bytes 9437200 | tf_op jit(solution)/shard_map/all_gather | solution.py:150
  791.7 16.3 multiply_convert_fusion.3
  808.0 65.4 %all-gather.45.cloned.1.call-done = bf16[3072,1536]{0,1:T(8,128)(2,1)} async-done(((bf16[3072,96]{0,1:T(8,128)(2,1)}), bf16[3072,1536]{0,1:T(8,128)(2,1)}) %all-gather.45.cloned.1.call-update) | async-done | bytes 9437200 | tf_op jit(solution)/shard_map/all_gather | solution.py:151
  873.4 13.0 fusion.65
  887.7 39.0 %psum.29 = f32[]{:T(128)} all-reduce(f32[]{:T(128)} %get-tuple-element.93), channel_id=1, replica_groups=mesh['dp'=16,'tensor'=2] {'dp','tensor'}, use_global_device_ids=true, to_apply=%region_16.0 | all-reduce | flops 1 | bytes 8 | tf_op jit(solution)/shard_map/psum | solution.py:209
  927.4 18.7 reduce-scatter.29.cloned.1.call-done
  949.9 35.8 %all-gather.47.cloned.1.call-done = bf16[768,1536]{1,0:T(8,128)(2,1)} async-done(((bf16[384,1536]{1,0:T(8,128)(2,1)}), bf16[768,1536]{1,0:T(8,128)(2,1)}) %all-gather.47.cloned.1.call-update) | async-done | bytes 2359312 | tf_op jit(solution)/shard_map/all_gather | solution.py:161
  985.8 19.5 multiply_convert_fusion.1
  1005.3 13.1 fusion.66
  1018.4 10.9 convolution_add_fusion
  1029.3 60.1 %reduce-scatter.31.cloned.1.call-done = f32[384,1536]{1,0:T(8,128)} async-done(((f32[768,1536]{1,0:T(8,128)}), f32[384,1536]{1,0:T(8,128)}) %reduce-scatter.31.cloned.1.call-update) | async-done | bytes 2359312 | tf_op jit(solution)/shard_map/reduce_scatter | solution.py:164
  1097.9 35.9 %all-gather.49.cloned.1.call-done = bf16[768,1536]{1,0:T(8,128)(2,1)} async-done(((bf16[384,1536]{1,0:T(8,128)(2,1)}), bf16[768,1536]{1,0:T(8,128)(2,1)}) %all-gather.49.cloned.1.call-update) | async-done | bytes 2359312 | tf_op jit(solution)/shard_map/all_gather | solution.py:161
  1151.6 60.1 %reduce-scatter.33.cloned.1.call-done = f32[384,1536]{1,0:T(8,128)} async-done(((f32[768,1536]{1,0:T(8,128)}), f32[384,1536]{1,0:T(8,128)}) %reduce-scatter.33.cloned.1.call-update) | async-done | bytes 2359312 | tf_op jit(solution)/shard_map/reduce_scatter | solution.py:164
  1218.0 35.7 %all-gather.51.cloned.1.call-done = bf16[768,1536]{1,0:T(8,128)(2,1)} async-done(((bf16[384,1536]{1,0:T(8,128)(2,1)}), bf16[768,1536]{1,0:T(8,128)(2,1)}) %all-gather.51.cloned.1.call-update) | async-done | bytes 2359312 | tf_op jit(solution)/shard_map/all_gather | solution.py:161
  1258.1 11.9 fusion.33
  1270.0 22.8 multiply_reduce_fusion
  1292.8 23.7 multiply_convert_fusion
  1316.5 9.5 multiply_bitcast_fusion
  1326.0 7.6 multiply_bitcast_fusion.1
  1356.7 48.8 %reduce-scatter.35.cloned.1.call-done = f32[384,1536]{1,0:T(8,128)} async-done(((f32[768,1536]{1,0:T(8,128)}), f32[384,1536]{1,0:T(8,128)}) %reduce-scatter.35.cloned.1.call-update) | async-done | bytes 2359312 | tf_op jit(solution)/shard_map/reduce_scatter | solution.py:164
  1408.2 6.9 psum.31
  1416.3 6.2 fusion.76
  1422.6 6.1 fusion.75
  1431.7 6.0 copy.85
  1440.9 6.1 copy.83
  1447.5 14.2 fusion.79
  1461.8 13.9 fusion.78
  1475.7 13.9 fusion.77
  1490.9 6.1 fusion.74
  1498.2 5.9 fusion.73
  1505.4 6.1 fusion.72
  1512.8 6.0 fusion.71
  1519.5 41.9 %psum.28 = f32[]{:T(128)} all-reduce(f32[]{:T(128)} %get-tuple-element.89), channel_id=1, replica_groups=mesh['dp'=16,'tensor'=2] {'dp','tensor'}, use_global_device_ids=true, to_apply=%region_14.0 | all-reduce | flops 1 | bytes 8 | tf_op jit(solution)/shard_map/psum | solution.py:209
  1574.9 78.9 %reduce-scatter.45.cloned.1.call-done = f32[96,768]{1,0:T(8,128)} async-done(((f32[1536,768]{1,0:T(8,128)}), f32[96,768]{1,0:T(8,128)}) %reduce-scatter.45.cloned.1.call-update) | async-done | bytes 294928 | tf_op jit(solution)/shard_map/reduce_scatter | solution.py:294
  1653.8 79.6 %reduce-scatter.57.cloned.1.call-done = f32[96,768]{1,0:T(8,128)} async-done(((f32[1536,768]{1,0:T(8,128)}), f32[96,768]{1,0:T(8,128)}) %reduce-scatter.57.cloned.1.call-update) | async-done | bytes 294928
  1733.4 79.1 %reduce-scatter.55.cloned.1.call-done = f32[96,768]{1,0:T(8,128)} async-done(((f32[1536,768]{1,0:T(8,128)}), f32[96,768]{1,0:T(8,128)}) %reduce-scatter.55.cloned.1.call-update) | async-done | bytes 294928
  1812.4 198.9 %reduce-scatter.53.cloned.1.call-done = f32[3072,96]{0,1:T(8,128)} async-done(((f32[3072,1536]{0,1:T(8,128)}), f32[3072,96]{0,1:T(8,128)}) %reduce-scatter.53.cloned.1.call-update) | async-done | bytes 1179664 | tf_op jit(solution)/shard_map/reduce_scatter | solution.py:228
  2011.3 199.3 %reduce-scatter.51.cloned.1.call-done = f32[96,3072]{1,0:T(8,128)} async-done(((f32[1536,3072]{1,0:T(8,128)}), f32[96,3072]{1,0:T(8,128)}) %reduce-scatter.51.cloned.1.call-update) | async-done | bytes 1179664 | tf_op jit(solution)/shard_map/reduce_scatter | solution.py:227
  2210.7 199.3 %reduce-scatter.49.cloned.1.call-done = f32[96,3072]{1,0:T(8,128)} async-done(((f32[1536,3072]{1,0:T(8,128)}), f32[96,3072]{1,0:T(8,128)}) %reduce-scatter.49.cloned.1.call-update) | async-done | bytes 1179664 | tf_op jit(solution)/shard_map/reduce_scatter | solution.py:226
  2410.0 79.5 %reduce-scatter.43.cloned.1.call-done = f32[768,96]{0,1:T(8,128)} async-done(((f32[768,1536]{0,1:T(8,128)}), f32[768,96]{0,1:T(8,128)}) %reduce-scatter.43.cloned.1.call-update) | async-done | bytes 294928 | tf_op jit(solution)/shard_map/reduce_scatter | solution.py:293
  2489.5 79.1 %reduce-scatter.41.cloned.1.call-done = f32[96,768]{1,0:T(8,128)} async-done(((f32[1536,768]{1,0:T(8,128)}), f32[96,768]{1,0:T(8,128)}) %reduce-scatter.41.cloned.1.call-update) | async-done | bytes 294928 | tf_op jit(solution)/shard_map/reduce_scatter | solution.py:292
  2568.5 79.6 %reduce-scatter.39.cloned.1.call-done = f32[96,768]{1,0:T(8,128)} async-done(((f32[1536,768]{1,0:T(8,128)}), f32[96,768]{1,0:T(8,128)}) %reduce-scatter.39.cloned.1.call-update) | async-done | bytes 294928 | tf_op jit(solution)/shard_map/reduce_scatter | solution.py:291
  2648.1 78.9 %reduce-scatter.37.cloned.1.call-done = f32[96,768]{1,0:T(8,128)} async-done(((f32[1536,768]{1,0:T(8,128)}), f32[96,768]{1,0:T(8,128)}) %reduce-scatter.37.cloned.1.call-update) | async-done | bytes 294928 | tf_op jit(solution)/shard_map/reduce_scatter | solution.py:290
  (302 shorter events, 146.8 us)
Async XLA Ops:
  7.2 346.6 %copy-start = (bf16[1,130,1536]{2,1,0:T(8,128)(2,1)S(1)}, bf16[1,130,1536]{2,1,0:T(8,128)(2,1)}, u32[]{:S(2)}) copy-start(bf16[1,130,1536]{2,1,0:T(8,128)(2,1)} %param.17) | copy-start | bytes 1198084
  7.2 27.3 copy-start.6
  7.2 62.3 %all-gather.19.cloned.1.call-start = ((), (), s32[]{:S(2)}) async-start(), calls=%async_computation.18 | async-start | bytes 3538944 | tf_op jit(solution)/shard_map/all_gather | solution.py:155
  8.9 27.1 copy-start.53
  10.6 108.0 %copy-start.57 = (f32[384]{0:T(512)}, f32[384]{0:T(512)S(1)}, u32[]{:S(2)}) copy-start(f32[384]{0:T(512)S(1)} %add_rsqrt_fusion.2) | copy-start | bytes 4612
  33.9 277.7 %copy-start.51 = (f32[1536]{0:T(1024)}, f32[1536]{0:T(1024)S(1)}, u32[]{:S(2)}) copy-start(f32[1536]{0:T(1024)S(1)} %get-tuple-element.91) | copy-start | bytes 18436
  35.9 78.2 %all-gather.25.cloned.1.call-start = ((), (), s32[]{:S(2)}) async-start(), calls=%async_computation.21 | async-start | bytes 2506752 | tf_op jit(solution)/shard_map/all_gather | solution.py:137
  36.7 120.8 %all-gather.23.cloned.1.call-start = ((), (), s32[]{:S(2)}) async-start(), calls=%async_computation.20 | async-start | bytes 2506752 | tf_op jit(solution)/shard_map/all_gather | solution.py:136
  37.4 163.4 %all-gather.21.cloned.1.call-start = ((), (), s32[]{:S(2)}) async-start(), calls=%async_computation.19 | async-start | bytes 2506752 | tf_op jit(solution)/shard_map/all_gather | solution.py:138
  38.0 206.1 %all-gather.27.cloned.1.call-start = ((), (), s32[]{:S(2)}) async-start(), calls=%async_computation.22 | async-start | bytes 2506752 | tf_op jit(solution)/shard_map/all_gather | solution.py:139
  38.6 270.3 %reduce-scatter.25.cloned.1.call-start = ((), (), s32[]{:S(2)}) async-start(), calls=%async_computation.23 | async-start | bytes 7077888 | tf_op jit(solution)/shard_map/reduce_scatter | solution.py:158
  39.1 123.0 %copy-start.41 = (f32[768,32]{0,1:T(8,128)}, f32[768,32]{0,1:T(8,128)S(1)}, u32[]{:S(2)}) copy-start(f32[768,32]{0,1:T(8,128)S(1)} %get-tuple-element.118) | copy-start | bytes 294916
  39.1 123.0 %copy-start.43 = (f32[768,32]{0,1:T(8,128)}, f32[768,32]{0,1:T(8,128)S(1)}, u32[]{:S(2)}) copy-start(f32[768,32]{0,1:T(8,128)S(1)} %get-tuple-element.119) | copy-start | bytes 294916
  174.5 30.0 %copy-start.45 = (f32[12,768]{1,0:T(8,128)}, f32[12,768]{1,0:T(8,128)S(1)}, u32[]{:S(2)}) copy-start(f32[12,768]{1,0:T(8,128)S(1)} %get-tuple-element.120) | copy-start | bytes 110596
  174.5 26.3 copy-start.63
  217.5 32.4 %copy-start.68 = (bf16[12,64,768]{2,1,0:T(8,128)(2,1)}, bf16[12,64,768]{2,1,0:T(8,128)(2,1)S(1)}, u32[]{:S(2)}) copy-start(bf16[12,64,768]{2,1,0:T(8,128)(2,1)S(1)} %fusion.36) | copy-start | bytes 3538948
  250.0 103.8 %all-gather.29.cloned.1.call-start = ((), (), s32[]{:S(2)}) async-start(), calls=%async_computation.24 | async-start | bytes 2506752 | tf_op jit(solution)/shard_map/all_gather | solution.py:142
  250.7 146.7 %all-gather.35.cloned.1.call-start = ((), (), s32[]{:S(2)}) async-start(), calls=%async_computation.27 | async-start | bytes 2506752 | tf_op jit(solution)/shard_map/all_gather | solution.py:141
  251.5 189.7 %all-gather.33.cloned.1.call-start = ((), (), s32[]{:S(2)}) async-start(), calls=%async_computation.26 | async-start | bytes 2506752 | tf_op jit(solution)/shard_map/all_gather | solution.py:140
  252.2 225.9 %all-gather.31.cloned.1.call-start = ((), (), s32[]{:S(2)}) async-start(), calls=%async_computation.25 | async-start | bytes 3538944 | tf_op jit(solution)/shard_map/all_gather | solution.py:155
  311.2 276.9 %copy-start.2 = (f32[384,1536]{1,0:T(8,128)}, f32[384,1536]{1,0:T(8,128)S(1)}, u32[]{:S(2)}) copy-start(f32[384,1536]{1,0:T(8,128)S(1)} %get-tuple-element.102) | copy-start | bytes 7077892
  313.0 209.9 %all-gather.37.cloned.1.call-start = ((), (), s32[]{:S(2)}) async-start(), calls=%async_computation.28 | async-start | bytes 2506752 | tf_op jit(solution)/shard_map/all_gather | solution.py:143
  313.8 274.3 %reduce-scatter.27.cloned.1.call-start = ((), (), s32[]{:S(2)}) async-start(), calls=%async_computation.29 | async-start | bytes 7077888 | tf_op jit(solution)/shard_map/reduce_scatter | solution.py:158
  399.8 82.7 %copy-start.30 = (bf16[130,768]{0,1:T(8,128)(2,1)}, bf16[130,768]{0,1:T(8,128)(2,1)S(1)}, u32[]{:S(2)}) copy-start(bf16[130,768]{0,1:T(8,128)(2,1)S(1)} %copy.90) | copy-start | bytes 599044
  529.2 142.7 %all-gather.41.cloned.1.call-start = ((), (), s32[]{:S(2)}) async-start(), calls=%async_computation.31 | async-start | bytes 10027008 | tf_op jit(solution)/shard_map/all_gather | solution.py:149
  529.9 178.2 %all-gather.39.cloned.1.call-start = ((), (), s32[]{:S(2)}) async-start(), calls=%async_computation.30 | async-start | bytes 3538944 | tf_op jit(solution)/shard_map/all_gather | solution.py:155
  593.1 198.6 %all-gather.43.cloned.1.call-start = ((), (), s32[]{:S(2)}) async-start(), calls=%async_computation.32 | async-start | bytes 10027008 | tf_op jit(solution)/shard_map/all_gather | solution.py:150
  593.7 279.7 %all-gather.45.cloned.1.call-start = ((), (), s32[]{:S(2)}) async-start(), calls=%async_computation.33 | async-start | bytes 10027008 | tf_op jit(solution)/shard_map/all_gather | solution.py:151
  594.3 351.8 %reduce-scatter.29.cloned.1.call-start = ((), (), s32[]{:S(2)}) async-start(), calls=%async_computation.34 | async-start | bytes 7077888 | tf_op jit(solution)/shard_map/reduce_scatter | solution.py:158
  708.1 83.6 %copy-start.66 = (bf16[768,1536]{1,0:T(8,128)(2,1)S(1)}, bf16[768,1536]{1,0:T(8,128)(2,1)}, u32[]{:S(2)}) copy-start(bf16[768,1536]{1,0:T(8,128)(2,1)} %all-gather.39.cloned.1.call-done) | copy-start | bytes 7077892
  886.4 59.7 %copy-start.5 = (f32[384,1536]{1,0:T(8,128)S(1)}, f32[384,1536]{1,0:T(8,128)}, u32[]{:S(2)}) copy-start(f32[384,1536]{1,0:T(8,128)} %copy-done.4) | copy-start | bytes 7077892
  886.4 99.3 %all-gather.47.cloned.1.call-start = ((), (), s32[]{:S(2)}) async-start(), calls=%async_computation.35 | async-start | bytes 3538944 | tf_op jit(solution)/shard_map/all_gather | solution.py:161
  949.7 139.7 %reduce-scatter.31.cloned.1.call-start = ((), (), s32[]{:S(2)}) async-start(), calls=%async_computation.36 | async-start | bytes 7077888 | tf_op jit(solution)/shard_map/reduce_scatter | solution.py:164
  985.8 32.6 %slice-start.2 = ((s8[9437184]{0:T(1024)(128)(4,1)}), s8[1048576]{0:T(1024)(128)(4,1)S(1)}, s32[]{:S(2)}) async-start(s8[9437184]{0:T(1024)(128)(4,1)} %bitcast.216), calls=%async_computation.56 | async-start | bytes 2097152
  985.8 32.6 %slice-start.3 = ((s8[9437184]{0:T(1024)(128)(4,1)}), s8[4194304]{0:T(1024)(128)(4,1)S(1)}, s32[]{:S(2)}) async-start(s8[9437184]{0:T(1024)(128)(4,1)} %bitcast.216), calls=%async_computation.57 | async-start | bytes 8388608
  1029.3 104.6 %all-gather.49.cloned.1.call-start = ((), (), s32[]{:S(2)}) async-start(), calls=%async_computation.37 | async-start | bytes 3538944 | tf_op jit(solution)/shard_map/all_gather | solution.py:161
  1097.6 114.1 %reduce-scatter.33.cloned.1.call-start = ((), (), s32[]{:S(2)}) async-start(), calls=%async_computation.38 | async-start | bytes 7077888 | tf_op jit(solution)/shard_map/reduce_scatter | solution.py:164
  1097.9 40.4 %copy-start.34 = (bf16[130,768]{0,1:T(8,128)(2,1)S(1)}, bf16[130,768]{0,1:T(8,128)(2,1)}, u32[]{:S(2)}) copy-start(bf16[130,768]{0,1:T(8,128)(2,1)} %copy.89) | copy-start | bytes 599044
  1151.5 60.2 %copy-start.3 = (f32[384,1536]{1,0:T(8,128)S(1)}, f32[384,1536]{1,0:T(8,128)}, u32[]{:S(2)}) copy-start(f32[384,1536]{1,0:T(8,128)} %copy-done.2) | copy-start | bytes 7077892
  1151.5 60.2 %copy-start.52 = (f32[1536]{0:T(1024)S(1)}, f32[1536]{0:T(1024)}, u32[]{:S(2)}) copy-start(f32[1536]{0:T(1024)} %copy-done.51) | copy-start | bytes 18436
  1151.5 60.2 %copy-start.56 = (f32[384]{0:T(512)S(1)}, f32[384]{0:T(512)}, u32[]{:S(2)}) copy-start(f32[384]{0:T(512)} %copy-done.55) | copy-start | bytes 4612
  1151.5 60.2 %copy-start.60 = (f32[384]{0:T(512)S(1)}, f32[384]{0:T(512)}, u32[]{:S(2)}) copy-start(f32[384]{0:T(512)} %copy-done.59) | copy-start | bytes 4612
  1151.5 102.2 %all-gather.51.cloned.1.call-start = ((), (), s32[]{:S(2)}) async-start(), calls=%async_computation.39 | async-start | bytes 3538944 | tf_op jit(solution)/shard_map/all_gather | solution.py:161
  1217.5 188.0 %reduce-scatter.35.cloned.1.call-start = ((), (), s32[]{:S(2)}) async-start(), calls=%async_computation.40 | async-start | bytes 7077888 | tf_op jit(solution)/shard_map/reduce_scatter | solution.py:164
  1270.0 71.0 %copy-start.25 = (bf16[12,64,768]{2,1,0:T(8,128)(2,1)}, bf16[12,64,768]{2,1,0:T(8,128)(2,1)S(1)}, u32[]{:S(2)}) copy-start(bf16[12,64,768]{2,1,0:T(8,128)(2,1)S(1)} %fusion.33) | copy-start | bytes 3538948
  1292.8 23.7 copy-start.22
  1292.8 23.7 copy-start.24
  1345.3 216.8 %all-reduce.2.cloned.1.call-start = ((), (), s32[]{:S(2)}) async-start(), calls=%async_computation.41 | async-start | bytes 835584 | tf_op jit(solution)/shard_map/psum | solution.py:276
  1354.9 50.6 %copy-start.7 = (bf16[1,384,1536]{2,1,0:T(8,128)(2,1)S(1)}, bf16[1,384,1536]{2,1,0:T(8,128)(2,1)}, u32[]{:S(2)}) copy-start(bf16[1,384,1536]{2,1,0:T(8,128)(2,1)} %param.16) | copy-start | bytes 3538948
  1354.9 50.6 %copy-start.50 = (f32[1536]{0:T(1024)S(1)}, f32[1536]{0:T(1024)}, u32[]{:S(2)}) copy-start(f32[1536]{0:T(1024)} %copy-done.49) | copy-start | bytes 18436
  1354.9 50.6 %copy-start.54 = (f32[384]{0:T(512)S(1)}, f32[384]{0:T(512)}, u32[]{:S(2)}) copy-start(f32[384]{0:T(512)} %copy-done.53) | copy-start | bytes 4612
  1354.9 50.6 %copy-start.58 = (f32[384]{0:T(512)S(1)}, f32[384]{0:T(512)}, u32[]{:S(2)}) copy-start(f32[384]{0:T(512)} %copy-done.57) | copy-start | bytes 4612
  1356.6 212.6 %reduce-scatter.59.cloned.1.call-start = ((), (), s32[]{:S(2)}) async-start(), calls=%async_computation.53 | async-start | bytes 835584
  1416.3 158.6 %reduce-scatter.47.cloned.1.call-start = ((), (), s32[]{:S(2)}) async-start(), calls=%async_computation.47 | async-start | bytes 5013504 | tf_op jit(solution)/shard_map/reduce_scatter | solution.py:297
  1422.6 231.2 %reduce-scatter.45.cloned.1.call-start = ((), (), s32[]{:S(2)}) async-start(), calls=%async_computation.46 | async-start | bytes 5013504 | tf_op jit(solution)/shard_map/reduce_scatter | solution.py:294
  1428.8 304.6 %reduce-scatter.57.cloned.1.call-start = ((), (), s32[]{:S(2)}) async-start(), calls=%async_computation.52 | async-start | bytes 5013504
  1437.8 374.7 %reduce-scatter.55.cloned.1.call-start = ((), (), s32[]{:S(2)}) async-start(), calls=%async_computation.51 | async-start | bytes 5013504
  1447.1 564.3 %reduce-scatter.53.cloned.1.call-start = ((), (), s32[]{:S(2)}) async-start(), calls=%async_computation.50 | async-start | bytes 20054016 | tf_op jit(solution)/shard_map/reduce_scatter | solution.py:228
  1461.8 748.9 %reduce-scatter.51.cloned.1.call-start = ((), (), s32[]{:S(2)}) async-start(), calls=%async_computation.49 | async-start | bytes 20054016 | tf_op jit(solution)/shard_map/reduce_scatter | solution.py:227
  1475.7 934.3 %reduce-scatter.49.cloned.1.call-start = ((), (), s32[]{:S(2)}) async-start(), calls=%async_computation.48 | async-start | bytes 20054016 | tf_op jit(solution)/shard_map/reduce_scatter | solution.py:226
  1489.6 999.8 %reduce-scatter.43.cloned.1.call-start = ((), (), s32[]{:S(2)}) async-start(), calls=%async_computation.45 | async-start | bytes 5013504 | tf_op jit(solution)/shard_map/reduce_scatter | solution.py:293
  1497.0 1071.5 %reduce-scatter.41.cloned.1.call-start = ((), (), s32[]{:S(2)}) async-start(), calls=%async_computation.44 | async-start | bytes 5013504 | tf_op jit(solution)/shard_map/reduce_scatter | solution.py:292
  1504.1 1144.0 %reduce-scatter.39.cloned.1.call-start = ((), (), s32[]{:S(2)}) async-start(), calls=%async_computation.43 | async-start | bytes 5013504 | tf_op jit(solution)/shard_map/reduce_scatter | solution.py:291
  1511.5 1215.6 %reduce-scatter.37.cloned.1.call-start = ((), (), s32[]{:S(2)}) async-start(), calls=%async_computation.42 | async-start | bytes 5013504 | tf_op jit(solution)/shard_map/reduce_scatter | solution.py:290
  (48 other events, 220.2 us)
Sparse Core Ops, SparseCore 0:
  36.1 33.3 all-gather.18
  71.7 42.3 all-gather.24
  116.4 41.0 all-gather.22
  159.7 41.0 all-gather.20
  202.9 41.0 all-gather.26
  250.1 58.7 reduce-scatter.24
  311.4 42.3 all-gather.28
  356.3 41.0 all-gather.34
  400.0 41.0 all-gather.32
  443.2 34.8 all-gather.30
  480.6 42.3 all-gather.36
  529.3 58.7 reduce-scatter.26
  590.4 81.4 all-gather.40
  673.8 34.1 all-gather.38
  710.2 81.4 all-gather.42
  793.8 79.5 all-gather.44
  886.5 59.5 reduce-scatter.28
  949.8 35.8 all-gather.46
  1029.4 59.9 reduce-scatter.30
  1097.7 36.0 all-gather.48
  1151.6 59.9 reduce-scatter.32
  1217.6 36.0 all-gather.50
  1345.4 59.9 reduce-scatter.34
  1408.2 26.2 all-reduce.1
  1438.1 56.6 reduce-scatter.58
  1499.6 75.2 reduce-scatter.46
  1579.2 74.5 reduce-scatter.44
  1658.7 74.5 reduce-scatter.56
  1737.8 74.6 reduce-scatter.54
  1817.5 193.7 reduce-scatter.52
  2016.6 194.0 reduce-scatter.50
  2215.9 194.0 reduce-scatter.48
  2414.7 74.6 reduce-scatter.42
  2493.9 74.5 reduce-scatter.40
  2573.4 74.6 reduce-scatter.38
  2652.4 74.6 reduce-scatter.36
where the time goes:
time: 2740 us; the launch traced here: 2730 us
  waiting for transfers between devices  2170 us (79%)
  matrix products  319 us (12%)
  blocking collectives  111 us (4%)
  other arithmetic  78.1 us (3%)
  local copies, waits for them, and re-layouts  35.4 us (1%)
    reduce_scatter x1, waiting for transfers between devices, body(): lax.psum_scatter(grad_up_w, 'dp', scatter_dimension=0, tiled=True)  199 us
    reduce_scatter x1, waiting for transfers between devices, body(): lax.psum_scatter(grad_gate_w, 'dp', scatter_dimension=0, tiled=True)  199 us
    reduce_scatter x1, waiting for transfers between devices, body(): lax.psum_scatter(grad_down, 'dp', scatter_dimension=1, tiled=True)  199 us
    reduce_scatter x3, waiting for transfers between devices, scatter_grads(): return lax.psum_scatter(values, 'tensor', scatter_dimension=0, tiled=True)  169 us
    unnamed x39, waiting for transfers between devices  166 us
    reduce_scatter x3, waiting for transfers between devices, scatter_rows(): return lax.psum_scatter(values, 'tensor', scatter_dimension=0, tiled=True)  133 us
    all_gather x3, waiting for transfers between devices, gather_grads(): return lax.all_gather(values, 'tensor', axis=0, tiled=True)  107 us
    all_gather x3, waiting for transfers between devices, gather_rows(): return lax.all_gather(values, 'tensor', axis=0, tiled=True)  103 us
  transfers between devices with their start and end apart: 36, of which 34 were waited for; matrix products, arithmetic and copies ran while one was open for 8% of the time, Pallas kernels for 0%

commit v1 on v0

v1 whole, which is shorter than its diff:
```python
import math

import jax
import jax.numpy as jnp
from jax import lax
from jax.sharding import Mesh, PartitionSpec as P

HEAD_DIM = 64
EPSILON = 1e-05
F32 = jnp.float32
BF16 = jnp.bfloat16


def dot(left, right, left_dim, right_dim):
    return lax.dot_general(
        left, right, (((left_dim,), (right_dim,)), ((), ())), preferred_element_type=F32
    )


def norm_stats(values):
    row_mean = jnp.mean(values, axis=-1, keepdims=True)
    centred = values - row_mean
    row_var = jnp.mean(centred * centred, axis=-1, keepdims=True)
    inverse = lax.rsqrt(row_var + EPSILON)
    return (centred * inverse, inverse)


def norm_back(grad_normed, normed, inverse, gain_row):
    scaled = grad_normed * gain_row
    mean_scaled = jnp.mean(scaled, axis=-1, keepdims=True)
    mean_product = jnp.mean(scaled * normed, axis=-1, keepdims=True)
    grad_values = inverse * (scaled - mean_scaled - normed * mean_product)
    return (grad_values, jnp.sum(grad_normed * normed, axis=0))


def rotary_tables(positions):
    half_dim = HEAD_DIM // 2
    freqs = jnp.exp(jnp.arange(half_dim, dtype=F32) * (-math.log(10000.0) / half_dim))
    angles = positions.astype(F32)[:, None] * freqs[None, :]
    return (jnp.cos(angles)[:, None, :], jnp.sin(angles)[:, None, :])


def rotate(values, rot_cos, rot_sin):
    half_dim = HEAD_DIM // 2
    lower = values[..., :half_dim]
    upper = values[..., half_dim:]
    return jnp.concatenate(
        [lower * rot_cos - upper * rot_sin, upper * rot_cos + lower * rot_sin], axis=-1
    )


def attend_forward(queries, keys_in, values_in):
    scale_factor = HEAD_DIM ** (-0.5)
    scores = (
        jnp.einsum("qhd,khd->hqk", queries, keys_in, preferred_element_type=F32) * scale_factor
    )
    row_max = jnp.max(scores, axis=-1, keepdims=True)
    shifted = jnp.exp(scores - row_max)
    row_total = jnp.sum(shifted, axis=-1, keepdims=True)
    soft_probs = (shifted / row_total).astype(BF16)
    mixed = jnp.einsum("hqk,khd->qhd", soft_probs, values_in, preferred_element_type=F32)
    return (mixed, row_max + jnp.log(row_total))


def attend_back(queries, keys_in, values_in, log_total, grad_mixed):
    scale_factor = HEAD_DIM ** (-0.5)
    scores = (
        jnp.einsum("qhd,khd->hqk", queries, keys_in, preferred_element_type=F32) * scale_factor
    )
    soft_probs = jnp.exp(scores - log_total)
    grad_values = jnp.einsum(
        "hqk,qhd->khd", soft_probs.astype(BF16), grad_mixed, preferred_element_type=F32
    )
    grad_probs = jnp.einsum("qhd,khd->hqk", grad_mixed, values_in, preferred_element_type=F32)
    weighted = jnp.sum(soft_probs * grad_probs, axis=-1, keepdims=True)
    grad_scores = (soft_probs * (grad_probs - weighted)).astype(BF16)
    grad_queries = (
        jnp.einsum("hqk,khd->qhd", grad_scores, keys_in, preferred_element_type=F32) * scale_factor
    )
    grad_keys = (
        jnp.einsum("hqk,qhd->khd", grad_scores, queries, preferred_element_type=F32) * scale_factor
    )
    return (grad_queries, grad_keys, grad_values)


def body(
    x_input,
    cond_tokens,
    teacher,
    valid_mask,
    norm_gains,
    w_query,
    w_key,
    w_value,
    w_out,
    c_query,
    c_key,
    c_value,
    c_out,
    w_gate,
    w_up,
    w_down,
):
    chips = lax.axis_size("ring")
    pair = lax.axis_index("core")
    share = lax.axis_index("tensor")
    dp_size = 2 * chips
    dp_axes = ("ring", "core")
    swap = [(0, 1), (1, 0)]

    def to_peer(values):
        return lax.ppermute(values, "tensor", swap)

    def to_core(values):
        return lax.ppermute(values, "core", swap)

    def gather(values):
        return lax.all_gather(values, dp_axes, axis=0, tiled=True)

    def half_of(values, index):
        width = values.shape[1] // 2
        return lax.dynamic_slice(values, (0, index * width), (values.shape[0], width))

    x_bf = x_input[0]
    rows, width = x_bf.shape
    slab = w_query.shape[0]
    heads_width = w_query.shape[1]
    ff_width = w_gate.shape[1]
    cond_rows = cond_tokens[0]
    mask_float = valid_mask[0].astype(F32)
    x_peer_bf = to_peer(x_bf)

    own_count = jnp.sum(valid_mask[0])
    row_ids = lax.broadcasted_iota(jnp.int32, (slab, 1), 0)
    count_col = jnp.where(
        row_ids == 0, own_count // 128, jnp.where(row_ids == 1, own_count % 128, 0)
    ).astype(BF16)
    extra = jnp.pad(
        jnp.concatenate([norm_gains.T, count_col], axis=1), ((0, 0), (0, 124))
    )
    gath_a = gather(jnp.concatenate([w_query, w_key, w_value, extra], axis=1))
    gath_b = gather(jnp.concatenate([w_out.T, c_query, c_key, c_value, c_out.T], axis=1))
    gath_c = gather(jnp.concatenate([w_gate, w_up], axis=1))
    gath_d = gather(w_down.T)

    weight_qkv = gath_a[:, : 3 * heads_width]
    side = gath_a[:, 3 * heads_width :].T[:8].astype(F32)
    gains = side[:3]
    counts = side[3].reshape(dp_size, slab)
    part_count = jnp.sum(counts[:, 0]) * 128.0 + jnp.sum(counts[:, 1])
    part_count = jnp.full((8, 128), part_count, F32)
    valid_count = (part_count + to_peer(part_count))[0, 0]
    weight_o = gath_b[:, :heads_width]
    cross_q, cross_k, cross_v, cross_o = (
        gath_b[:, i * heads_width : (i + 1) * heads_width] for i in range(1, 5)
    )
    weight_gate = gath_c[:, :ff_width]
    weight_up = gath_c[:, ff_width:]

    def both(own):
        return jnp.concatenate([own, to_peer(own)], axis=0)

    length = 2 * rows
    ctx_len = cond_rows.shape[0]
    local_rows = x_bf.astype(F32)
    normed_one, inverse_one = norm_stats(local_rows)
    peer_one, _ = norm_stats(x_peer_bf.astype(F32))
    input_one = jnp.concatenate(
        [(normed_one * gains[0]).astype(BF16), (peer_one * gains[0]).astype(BF16)], axis=0
    )
    places = lax.iota(jnp.int32, length)
    positions = jnp.where(places < rows, places + share * rows, places - share * rows)
    rot_cos, rot_sin = rotary_tables(positions)
    qkv = dot(input_one, weight_qkv, 1, 0)
    query_rot = rotate(
        qkv[:, :heads_width].reshape(length, -1, HEAD_DIM), rot_cos, rot_sin
    ).astype(BF16)
    key_rot = rotate(
        qkv[:, heads_width : 2 * heads_width].reshape(length, -1, HEAD_DIM), rot_cos, rot_sin
    ).astype(BF16)
    value_self = qkv[:, 2 * heads_width :].astype(BF16).reshape(length, -1, HEAD_DIM)
    mixed_self, log_self = attend_forward(query_rot, key_rot, value_self)
    mixed_self = mixed_self.reshape(length, -1).astype(BF16)

    def project(values, weight, weight_dim):
        away = to_peer(dot(values[rows:], weight, 1, weight_dim).astype(BF16))
        return dot(values[:rows], weight, 1, weight_dim) + away.astype(F32)

    hidden_one = local_rows + project(mixed_self, weight_o, 1)

    normed_two, inverse_two = norm_stats(hidden_one)
    input_two = both((normed_two * gains[1]).astype(BF16))
    query_cross = dot(input_two, cross_q, 1, 0).astype(BF16).reshape(length, -1, HEAD_DIM)
    key_cross = dot(cond_rows, cross_k, 1, 0).astype(BF16).reshape(ctx_len, -1, HEAD_DIM)
    value_cross = dot(cond_rows, cross_v, 1, 0).astype(BF16).reshape(ctx_len, -1, HEAD_DIM)
    mixed_cross, log_cross = attend_forward(query_cross, key_cross, value_cross)
    mixed_cross = mixed_cross.reshape(length, -1).astype(BF16)
    hidden_two = hidden_one + project(mixed_cross, cross_o, 1)

    normed_three, inverse_three = norm_stats(hidden_two)
    input_three = both((normed_three * gains[2]).astype(BF16))
    gate_pre = dot(input_three, weight_gate, 1, 0)
    up_pre = dot(input_three, weight_up, 1, 0)
    gate_sigmoid = jax.nn.sigmoid(gate_pre)
    gate_silu = gate_pre * gate_sigmoid
    hidden_ff = (gate_silu * up_pre).astype(BF16)
    block_out = hidden_two + project(hidden_ff, gath_d, 1)

    error_diff = block_out - teacher[0].astype(F32)
    local_error = jnp.sum(mask_float[:, None] * error_diff * error_diff)
    token_total = float(dp_size * lax.axis_size("tensor") * rows)
    grad_out = 2.0 * token_total / valid_count * mask_float[:, None] * error_diff

    def half_grad(row_side, column_side):
        kept = half_of(column_side, pair)
        sent = half_of(column_side, 1 - pair)
        return (
            dot(row_side, kept, 0, 0) + dot(to_core(row_side), to_core(sent), 0, 0)
        ).astype(BF16)

    def scatter(grads):
        return lax.psum_scatter(
            jnp.concatenate(grads, axis=1) if len(grads) > 1 else grads[0],
            "ring",
            scatter_dimension=0,
            tiled=True,
        )

    def finish(scattered, count):
        kept = lax.dynamic_slice(scattered, (pair * slab, 0), (slab, scattered.shape[1]))
        sent = lax.dynamic_slice(scattered, ((1 - pair) * slab, 0), (slab, scattered.shape[1]))
        got = to_core(sent)
        first = jnp.where(pair == 0, kept, got).astype(F32)
        second = jnp.where(pair == 0, got, kept).astype(F32)
        part = scattered.shape[1] // count
        return [
            jnp.concatenate(
                [first[:, i * part : (i + 1) * part], second[:, i * part : (i + 1) * part]], axis=1
            )
            for i in range(count)
        ]

    branch_three = both(grad_out.astype(BF16))
    scat_down = scatter([half_grad(branch_three, hidden_ff)])
    grad_hidden = dot(branch_three, gath_d, 1, 0)
    grad_gate = (
        grad_hidden * up_pre * gate_sigmoid * (1.0 + gate_pre * (1.0 - gate_sigmoid))
    ).astype(BF16)
    grad_upper = (grad_hidden * gate_silu).astype(BF16)

    def pull_ff(part):
        return dot(grad_gate[part], weight_gate, 1, 1) + dot(grad_upper[part], weight_up, 1, 1)

    away = to_peer(pull_ff(slice(rows, length)).astype(BF16))
    grad_normed_three = pull_ff(slice(0, rows)) + away.astype(F32)
    scat_ff = scatter([half_grad(input_three, grad_gate), half_grad(input_three, grad_upper)])
    back_three, gain_three = norm_back(grad_normed_three, normed_three, inverse_three, gains[2])
    grad_two = grad_out + back_three

    branch_two = both(grad_two.astype(BF16))
    grad_mixed_cross = dot(branch_two, cross_o, 1, 0).astype(BF16).reshape(length, -1, HEAD_DIM)
    grad_qc, grad_kc, grad_vc = attend_back(
        query_cross, key_cross, value_cross, log_cross, grad_mixed_cross
    )
    grad_qc = grad_qc.reshape(length, -1).astype(BF16)
    grad_kc = grad_kc.reshape(ctx_len, -1).astype(BF16)
    grad_vc = grad_vc.reshape(ctx_len, -1).astype(BF16)
    cond_part = (dot(grad_kc, cross_k, 1, 1) + dot(grad_vc, cross_v, 1, 1)).astype(BF16)
    cond_sum = cond_part.astype(F32) + to_peer(cond_part).astype(F32)
    grad_normed_two = project(grad_qc, cross_q, 1)
    back_two, gain_two = norm_back(grad_normed_two, normed_two, inverse_two, gains[1])
    grad_one = grad_two + back_two

    branch_one = both(grad_one.astype(BF16))
    grad_mixed_self = dot(branch_one, weight_o, 1, 0).astype(BF16).reshape(length, -1, HEAD_DIM)
    scat_attn = scatter(
        [
            half_grad(branch_one, mixed_self),
            half_grad(input_two, grad_qc),
            half_grad(cond_rows, grad_kc),
            half_grad(cond_rows, grad_vc),
            half_grad(branch_two, mixed_cross),
        ]
    )
    grad_qs, grad_ks, grad_vs = attend_back(
        query_rot, key_rot, value_self, log_self, grad_mixed_self
    )
    grad_qs = rotate(grad_qs, rot_cos, -rot_sin).reshape(length, -1).astype(BF16)
    grad_ks = rotate(grad_ks, rot_cos, -rot_sin).reshape(length, -1).astype(BF16)
    grad_vs = grad_vs.reshape(length, -1).astype(BF16)
    scat_qkv = scatter(
        [
            half_grad(input_one, grad_qs),
            half_grad(input_one, grad_ks),
            half_grad(input_one, grad_vs),
        ]
    )
    grad_qkv = jnp.concatenate([grad_qs, grad_ks, grad_vs], axis=1)
    grad_normed_one = project(grad_qkv, weight_qkv, 1)
    back_one, gain_one = norm_back(grad_normed_one, normed_one, inverse_one, gains[0])
    grad_rows = grad_one + back_one

    small = jnp.concatenate(
        [
            jnp.stack([gain_one, gain_two, gain_three]),
            jnp.full((1, width), local_error, F32),
        ],
        axis=0,
    )
    small = lax.psum(small, ("ring", "core", "tensor"))
    mean_loss = small[3, 0] / (width * valid_count)
    place = (lax.axis_index("ring") * 2 + pair) * slab
    grad_gains = lax.dynamic_slice(small, (0, place), (3, slab))

    (down_t,) = finish(scat_down, 1)
    gate_s, up_s = finish(scat_ff, 2)
    out_t, cq_s, ck_s, cv_s, co_t = finish(scat_attn, 5)
    q_s, k_s, v_s = finish(scat_qkv, 3)
    return (
        block_out.astype(BF16)[None],
        mean_loss,
        grad_rows[None],
        cond_sum[None],
        q_s,
        k_s,
        v_s,
        out_t.T,
        cq_s,
        ck_s,
        cv_s,
        co_t.T,
        gate_s,
        up_s,
        down_t.T,
        grad_gains,
    )


def solution(mesh):
    dp_size, share = mesh.shape["dp"], mesh.shape["tensor"]
    fine = Mesh(mesh.devices.reshape(dp_size // 2, 2, share), ("ring", "core", "tensor"))
    dp = ("ring", "core")
    tokens = P(dp, "tensor", None)
    by_row = P(dp, "tensor")
    by_column = P("tensor", dp)
    return jax.shard_map(
        body,
        mesh=fine,
        in_specs=(
            tokens,
            P(dp, None, None),
            tokens,
            by_row,
            P(None, dp),
            by_row,
            by_row,
            by_row,
            by_column,
            by_row,
            by_row,
            by_row,
            by_column,
            by_row,
            by_row,
            by_column,
        ),
        out_specs=(
            tokens,
            P(),
            tokens,
            P(dp, None, None),
            by_row,
            by_row,
            by_row,
            by_column,
            by_row,
            by_row,
            by_row,
            by_column,
            by_row,
            by_row,
            by_column,
            P(None, dp),
        ),
        check_vma=False,
    )
```

time: 2740 us -> 1100 us (0.40)
  waiting for transfers between devices: 2170 us -> 506 us
  blocking collectives: 111 us -> 41 us
  local copies, waits for them, and re-layouts: 35.4 us -> 92.7 us
    reduce_scatter x15 -> x1, waiting for transfers between devices: 1300 us -> 0.01 us  [scatter(): lax.psum_scatter(jnp.concatenate(grads, axis=1) if len(grads) > 1 else gr...]
    all_gather x17 -> x4, waiting for transfers between devices: 703 us -> 96.9 us  [gather(): return lax.all_gather(values, dp_axes, axis=0, tiled=True)]
    ppermute x0 -> x36, waiting for transfers between devices: none -> 266 us  [the longest x14 258 us: to_peer(): return lax.ppermute(values, 'tensor', swap)]
    psum x3 -> x1, blocking collectives: 87.9 us -> 41 us  [body(): small = lax.psum(small, ('ring', 'core', 'tensor'))]
    unnamed x39 -> x11, waiting for transfers between devices: 166 us -> 143 us
    unnamed x157 -> x260, local copies, waits for them, and re-layouts: 34.2 us -> 56.6 us
    dot_general x41 -> x55, matrix products: 277 us -> 275 us  [the longest x47 231 us: dot(): lax.dot_general(left, right, (((left_dim,), (right_dim,)), ((), ())), pre...]
  transfers between devices with their start and end apart: 36 -> 44, of which waited for: 34 -> 19; matrix products, arithmetic and copies ran while one was open for 8% -> 36% of each run, Pallas kernels for 0% -> 0%
where the time goes in v1:
time: 1100 us; the launch traced here: 1090 us
  waiting for transfers between devices  506 us (46%)
  matrix products  313 us (28%)
  local copies, waits for them, and re-layouts  92.7 us (8%)
  other arithmetic  89.9 us (8%)
  blocking collectives  41 us (4%)
  starting transfers between devices  27 us (2%)
  between operations  23.4 us (2%)
    ppermute x14, waiting for transfers between devices, to_peer(): return lax.ppermute(values, 'tensor', swap)  258 us
    dot_general x47, matrix products, dot(): lax.dot_general(left, right, (((left_dim,), (right_dim,)), ((), ())), pre...  231 us
    unnamed x11, waiting for transfers between devices  143 us
    all_gather x4, waiting for transfers between devices, gather(): return lax.all_gather(values, dp_axes, axis=0, tiled=True)  96.9 us
    unnamed x260, local copies, waits for them, and re-layouts  56.6 us
    psum x1, blocking collectives, body(): small = lax.psum(small, ('ring', 'core', 'tensor'))  41 us
    convert_element_type x2, other arithmetic, attend_back(): grad_scores = (soft_probs * (grad_probs - weighted)).astype(BF16)  25.5 us
    dot_general x2, matrix products, attend_back(): jnp.einsum('qhd,khd->hqk', grad_mixed, values_in, preferred_element_type=...  23.7 us
  transfers between devices with their start and end apart: 44, of which 19 were waited for; matrix products, arithmetic and copies ran while one was open for 36% of the time, Pallas kernels for 0%

profile of v1, /device:TPU:0, one launch (start us, length us, event | category | flops | bytes accessed | tf_op | source)
XLA Modules:
  0.0 1093.1 jit_solution(17473600523991093292)
XLA Ops:
  19.1 3.0 collective-permute-start
  24.6 23.4 %collective-permute-done = bf16[384,1536]{1,0:T(8,128)(2,1)S(1)} collective-permute-done((bf16[384,1536]{1,0:T(8,128)(2,1)S(1)}, bf16[384,1536]{1,0:T(8,128)(2,1)S(1)}, u32[]{:S(2)}, u32[]{:S(2)}) %collective-permute-start) | collective-permute-done | bytes 1179680 | tf_op jit(solution)/shard_map/ppermute | solution.py:112
  49.4 36.8 %all-gather.5.cloned.1.call-done = bf16[1536,2432]{1,0:T(8,128)(2,1)} async-done(((bf16[96,2432]{1,0:T(8,128)(2,1)}), bf16[1536,2432]{1,0:T(8,128)(2,1)}) %all-gather.5.cloned.1.call-update) | async-done | bytes 7471120 | tf_op jit(solution)/shard_map/all_gather | solution.py:118
  90.4 5.6 fusion.22
  102.4 3.1 copy.84
  107.9 11.5 %multiply_reduce_fusion.1 = (f32[12,768]{1,0:T(8,128)S(1)}, f32[12,768,768]{1,2,0:T(8,128)}) fusion(bf16[768,12,32]{0,2,1:T(8,128)(2,1)S(1)} %get-tuple-element.140, bf16[768,12,32]{0,2,1:T(8,128)(2,1)S(1)} %get-tuple-element.141, bf16[768,12,32]{0,2,1:T(8,128)(2,1)S(1)} %get-tuple-element.94, bf16[768,12,32]{0,2,1:T(8,128)(2,1)S(1)} %get-tuple-element.93), kind=kOutput, calls=%fused_computation.6 | convolution fusion | flops 924834816 | bytes 30707712 | tf_op jit(solution)/shard_map/qhd,khd->hqk/dot_general | solution.py:55
  119.5 13.0 %fusion = f32[12,768]{1,0:T(8,128)S(1)} fusion(f32[12,768,768]{1,2,0:T(8,128)} %get-tuple-element.148, f32[12,768]{1,0:T(8,128)S(1)} %get-tuple-element.147), kind=kLoop, calls=%fused_computation.5 | loop fusion | flops 21224448 | bytes 28385280 | tf_op jit(solution)/shard_map/reduce_sum | solution.py:59
  132.5 12.7 %fusion.136 = bf16[12,64,768]{2,1,0:T(8,128)(2,1)S(1)} fusion(bf16[768,12,64]{0,2,1:T(8,128)(2,1)S(1)} %bitcast.177, f32[12,768,768]{1,2,0:T(8,128)} %get-tuple-element.148, f32[12,768]{1,0:T(8,128)S(1)} %fusion, f32[12,768]{1,0:T(8,128)S(1)} %get-tuple-element.147), kind=kOutput, calls=%fused_computation.183 | convolution fusion | flops 934871040 | bytes 30744576 | tf_op jit(solution)/shard_map/hqk,khd->qhd/dot_general | solution.py:61
  147.2 36.0 %all-gather.7.cloned.1.call-done = bf16[1536,3840]{1,0:T(8,128)(2,1)} async-done(((bf16[96,3840]{1,0:T(8,128)(2,1)}), bf16[1536,3840]{1,0:T(8,128)(2,1)}) %all-gather.7.cloned.1.call-update) | async-done | bytes 11796496 | tf_op jit(solution)/shard_map/all_gather | solution.py:118
  187.6 26.7 %collective-permute-done.1 = bf16[384,1536]{1,0:T(8,128)(2,1)S(1)} collective-permute-done((bf16[384,1536]{1,0:T(8,128)(2,1)S(1)}, bf16[384,1536]{1,0:T(8,128)(2,1)S(1)}, u32[]{:S(2)}, u32[]{:S(2)}) %collective-permute-start.1) | collective-permute-done | bytes 1179680 | tf_op jit(solution)/shard_map/ppermute | solution.py:112
  214.3 3.2 fusion.206
  224.5 3.0 fusion.147
  229.4 16.4 %collective-permute-done.2 = bf16[384,1536]{1,0:T(8,128)(2,1)} collective-permute-done((bf16[384,1536]{1,0:T(8,128)(2,1)S(1)}, bf16[384,1536]{1,0:T(8,128)(2,1)}, u32[]{:S(2)}, u32[]{:S(2)}) %collective-permute-start.2) | collective-permute-done | bytes 1179680 | tf_op jit(solution)/shard_map/ppermute | solution.py:112
  245.8 4.2 fusion.127
  254.8 3.1 convolution_convert_fusion.2
  259.5 24.9 %collective-permute-done.3 = bf16[384,1536]{1,0:T(8,128)(2,1)S(1)} collective-permute-done((bf16[384,1536]{1,0:T(8,128)(2,1)S(1)}, bf16[384,1536]{1,0:T(8,128)(2,1)S(1)}, u32[]{:S(2)}, u32[]{:S(2)}) %collective-permute-start.3) | collective-permute-done | bytes 1179680 | tf_op jit(solution)/shard_map/ppermute | solution.py:112
  284.4 3.0 fusion.207
  290.2 24.1 %collective-permute-done.4 = bf16[384,1536]{1,0:T(8,128)(2,1)} collective-permute-done((bf16[384,1536]{1,0:T(8,128)(2,1)S(1)}, bf16[384,1536]{1,0:T(8,128)(2,1)}, u32[]{:S(2)}, u32[]{:S(2)}) %collective-permute-start.4) | collective-permute-done | bytes 1179680 | tf_op jit(solution)/shard_map/ppermute | solution.py:112
  314.3 10.4 fusion.16
  324.7 3.6 copy-done.107
  328.3 13.6 %multiply_convert_fusion.3 = (bf16[768,3072]{1,0:T(8,128)(2,1)}, f32[768,3072]{1,0:T(8,128)}) fusion(f32[768,3072]{1,0:T(8,128)S(1)} %fusion.16, bf16[1536,6144]{1,0:T(8,128)(2,1)} %all-gather.9.cloned.1.call-done, bf16[384,1536]{1,0:T(8,128)(2,1)} %collective-permute-done.4, bf16[384,1536]{1,0:T(8,128)(2,1)S(1)} %multiply_convert_fusion.6), kind=kOutput, calls=%fused_computation.16 | convolution fusion | flops 7266631680 | bytes 35389440 | tf_op jit(solution)/shard_map/dot_general | solution.py:15
  341.9 24.2 %all-gather.11.cloned.1.call-done = bf16[1536,3072]{1,0:T(8,128)(2,1)} async-done(((bf16[96,3072]{1,0:T(8,128)(2,1)}), bf16[1536,3072]{1,0:T(8,128)(2,1)}) %all-gather.11.cloned.1.call-update) | async-done | bytes 9437200 | tf_op jit(solution)/shard_map/all_gather | solution.py:118
  366.1 9.3 convolution_convert_fusion.1
  381.0 22.9 %collective-permute-done.6 = f32[8,128]{1,0:T(8,128)S(1)} collective-permute-done((f32[8,128]{1,0:T(8,128)S(1)}, f32[8,128]{1,0:T(8,128)S(1)}, u32[]{:S(2)}, u32[]{:S(2)}) %collective-permute-start.6) | collective-permute-done | bytes 4128 | tf_op jit(solution)/shard_map/ppermute | solution.py:112
  405.2 10.4 fusion.78
  418.5 25.9 %collective-permute-done.7 = bf16[384,1536]{1,0:T(8,128)(2,1)S(1)} collective-permute-done((bf16[384,1536]{1,0:T(8,128)(2,1)S(1)}, bf16[384,1536]{1,0:T(8,128)(2,1)S(1)}, u32[]{:S(2)}, u32[]{:S(2)}) %collective-permute-start.7) | collective-permute-done | bytes 1179680 | tf_op jit(solution)/shard_map/ppermute | solution.py:112
  445.4 18.0 %multiply_convert_fusion.2 = (bf16[768,3072]{1,0:T(8,128)(2,1)}, bf16[768,3072]{1,0:T(8,128)(2,1)}) fusion(f32[768,3072]{1,0:T(8,128)} %copy-done.107, f32[768,3072]{1,0:T(8,128)} %get-tuple-element.156, bf16[1536,3072]{1,0:T(8,128)(2,1)} %all-gather.11.cloned.1.call-done, bf16[384,1536]{1,0:T(8,128)(2,1)} %copy-done.61, bf16[384,1536]{1,0:T(8,128)(2,1)} %copy-done.42), kind=kOutput, calls=%fused_computation.15 | convolution fusion | flops 7283146752 | bytes 40108032 | tf_op jit(solution)/shard_map/dot_general | solution.py:15
  463.4 7.7 fusion.6
  471.1 7.7 fusion.40
  480.4 9.6 fusion.8
  490.0 15.3 %collective-permute-done.8 = bf16[384,1536]{1,0:T(8,128)(2,1)S(1)} collective-permute-done((bf16[384,1536]{1,0:T(8,128)(2,1)S(1)}, bf16[384,1536]{1,0:T(8,128)(2,1)S(1)}, u32[]{:S(2)}, u32[]{:S(2)}) %collective-permute-start.8) | collective-permute-done | bytes 1179680 | tf_op jit(solution)/shard_map/ppermute | solution.py:112
  505.4 10.1 multiply_reduce_fusion.7
  520.0 24.0 %collective-permute-done.9 = bf16[384,1536]{1,0:T(8,128)(2,1)S(1)} collective-permute-done((bf16[384,1536]{1,0:T(8,128)(2,1)S(1)}, bf16[384,1536]{1,0:T(8,128)(2,1)S(1)}, u32[]{:S(2)}, u32[]{:S(2)}) %collective-permute-start.9) | collective-permute-done | bytes 1179680 | tf_op jit(solution)/shard_map/ppermute | solution.py:112
  544.0 4.1 fusion.130
  552.6 3.8 convolution_convert_fusion
  558.0 3.4 constant_dynamic-slice_fusion.2
  567.0 14.4 %collective-permute-done.10 = bf16[384,1536]{1,0:T(8,128)(2,1)} collective-permute-done((bf16[384,1536]{1,0:T(8,128)(2,1)}, bf16[384,1536]{1,0:T(8,128)(2,1)}, u32[]{:S(2)}, u32[]{:S(2)}) %collective-permute-start.10) | collective-permute-done | bytes 1179680 | tf_op jit(solution)/shard_map/ppermute | solution.py:112
  581.4 4.5 multiply_reduce_fusion.6
  589.8 7.3 fusion.210
  597.1 6.0 add_convert_fusion
  603.2 8.9 collective-permute-done.11
  612.1 4.1 fusion.124
  616.2 22.4 %multiply_reduce_fusion = (f32[12,768]{1,0:T(8,128)S(1)}, f32[12,768,768]{1,2,0:T(8,128)}) fusion(f32[12,768,768]{1,2,0:T(8,128)} %get-tuple-element.148, f32[12,768]{1,0:T(8,128)} %log_add_fusion.1, bf16[768,12,64]{0,2,1:T(8,128)(2,1)S(1)} %bitcast.175, bf16[768,12,64]{0,2,1:T(8,128)(2,1)S(1)} %bitcast.178), kind=kOutput, calls=%fused_computation.1 | convolution fusion | flops 934272000 | bytes 59056128 | tf_op jit(solution)/shard_map/qhd,khd->hqk/dot_general | solution.py:74
  638.6 12.2 %fusion.133 = bf16[12,64,768]{2,1,0:T(8,128)(2,1)S(1)} fusion(bf16[768,12,64]{0,2,1:T(8,128)(2,1)S(1)} %bitcast.176, f32[12,768,768]{1,2,0:T(8,128)} %get-tuple-element.148, f32[12,768]{1,0:T(8,128)S(1)} %copy-done.68), kind=kOutput, calls=%fused_computation.182 | convolution fusion | flops 927793152 | bytes 30707712 | tf_op jit(solution)/shard_map/hqk,qhd->khd/dot_general | solution.py:71
  650.8 24.4 %multiply_convert_fusion = bf16[12,768,768]{1,2,0:T(8,128)(2,1)} fusion(f32[12,768,768]{1,2,0:T(8,128)} %get-tuple-element.162, f32[12,768,768]{1,2,0:T(8,128)} %get-tuple-element.148, f32[12,768]{1,0:T(8,128)S(1)} %get-tuple-element.161, f32[12,768]{1,0:T(8,128)S(1)} %copy-done.68), kind=kLoop, calls=%fused_computation | loop fusion | flops 35389440 | bytes 70852608 | tf_op jit(solution)/shard_map/convert_element_type | solution.py:76
  675.3 7.7 multiply_bitcast_fusion.1
  683.8 9.8 multiply_bitcast_fusion
  709.2 3.9 copy.111
  724.5 4.8 collective-permute-done.22
  733.3 3.4 fusion.49
  736.7 3.4 fusion.51
  745.4 8.6 copy.113
  761.3 3.3 collective-permute-done.31
  764.6 6.6 fusion.209
  771.1 6.5 fusion.208
  777.6 7.0 add_convert_fusion.1
  784.7 7.0 add_convert_fusion.2
  791.6 12.3 %pad_maximum_fusion = bf16[1536,3072]{0,1:T(8,128)(2,1)} fusion(bf16[1536,1536]{0,1:T(8,128)(2,1)S(1)} %add_convert_fusion.1, bf16[1536,1536]{0,1:T(8,128)(2,1)S(1)} %add_convert_fusion.2), kind=kLoop, calls=%fused_computation.10 | loop fusion | flops 18874368 | bytes 18874368 | tf_op jit(solution)/shard_map/concatenate | solution.py:223
  803.9 12.7 %copy.115 = bf16[1536,3072]{1,0:T(8,128)(2,1)} copy(bf16[1536,3072]{0,1:T(8,128)(2,1)} %pad_maximum_fusion) | data formatting | bytes 18874368
  820.2 8.5 fusion.54
  834.9 31.0 %collective-permute-done.13 = bf16[130,1536]{1,0:T(8,128)(2,1)S(1)} collective-permute-done((bf16[130,1536]{1,0:T(8,128)(2,1)S(1)}, bf16[130,1536]{1,0:T(8,128)(2,1)S(1)}, u32[]{:S(2)}, u32[]{:S(2)}) %collective-permute-start.13) | collective-permute-done | bytes 399392 | tf_op jit(solution)/shard_map/ppermute | solution.py:112
  867.8 7.7 fusion.69
  878.9 41.0 %psum.7 = f32[4,1536]{1,0:T(4,128)S(1)} all-reduce(f32[4,1536]{1,0:T(4,128)S(1)} %maximum_maximum_fusion), channel_id=1, replica_groups=mesh['ring'=8,'core'=2,'tensor'=2] {'ring','core','tensor'}, use_global_device_ids=true, to_apply=%region_25.26 | all-reduce | flops 6144 | bytes 49152 | tf_op jit(solution)/shard_map/psum | solution.py:310
  931.0 142.6 %reduce-scatter.17.cloned.1.call-done = bf16[192,3072]{1,0:T(8,128)(2,1)} async-done(((bf16[1536,3072]{1,0:T(8,128)(2,1)}), bf16[192,3072]{1,0:T(8,128)(2,1)}) %reduce-scatter.17.cloned.1.call-update) | async-done | bytes 1179664
  (475 shorter events, 160.4 us)
Async XLA Ops:
  7.2 78.9 %all-gather.5.cloned.1.call-start = ((), (), s32[]{:S(2)}) async-start(), calls=%async_computation.4 | async-start | bytes 7938048 | tf_op jit(solution)/shard_map/all_gather | solution.py:118
  14.0 169.2 %all-gather.7.cloned.1.call-start = ((), (), s32[]{:S(2)}) async-start(), calls=%async_computation.5 | async-start | bytes 12533760 | tf_op jit(solution)/shard_map/all_gather | solution.py:118
  17.8 296.5 %all-gather.9.cloned.1.call-start = ((), (), s32[]{:S(2)}) async-start(), calls=%async_computation.6 | async-start | bytes 20054016 | tf_op jit(solution)/shard_map/all_gather | solution.py:118
  19.0 347.1 %all-gather.11.cloned.1.call-start = ((), (), s32[]{:S(2)}) async-start(), calls=%async_computation.7 | async-start | bytes 10027008 | tf_op jit(solution)/shard_map/all_gather | solution.py:118
  19.1 29.0 %collective-permute-start = (bf16[384,1536]{1,0:T(8,128)(2,1)S(1)}, bf16[384,1536]{1,0:T(8,128)(2,1)S(1)}, u32[]{:S(2)}, u32[]{:S(2)}) collective-permute-start(bf16[384,1536]{1,0:T(8,128)(2,1)S(1)} %bitcast.156), channel_id=1, source_target_pairs={{0,1},{1,0},{2,3},{3,2},{4,5},{5,4},{6,7},{7,6},{8,9},{9,8},{10,11... | collective-permute-start | bytes 3538952 | tf_op jit(solution)/shard_map/ppermute | solution.py:112
  22.1 855.6 %reduce-scatter.11.cloned.1.call-start = ((), (), s32[]{:S(2)}) async-start(), calls=%async_computation.8 | async-start | bytes 5308416 | tf_op jit(solution)/shard_map/reduce_scatter | solution.py:222
  22.4 26.9 %copy-start.90 = (f32[384]{0:T(512)}, f32[384]{0:T(512)S(1)}, u32[]{:S(2)}) copy-start(f32[384]{0:T(512)S(1)} %broadcast_multiply_fusion.10) | copy-start | bytes 4612
  88.8 129.0 %copy-start.86 = (f32[1536]{0:T(1024)}, f32[1536]{0:T(1024)S(1)}, u32[]{:S(2)}) copy-start(f32[1536]{0:T(1024)S(1)} %get-tuple-element.75) | copy-start | bytes 18436
  183.2 31.1 %copy-start.72 = (bf16[384,12,64]{0,2,1:T(8,128)(2,1)S(1)}, bf16[384,12,64]{0,2,1:T(8,128)(2,1)}, u32[]{:S(2)}) copy-start(bf16[384,12,64]{0,2,1:T(8,128)(2,1)} %get-tuple-element.110) | copy-start | bytes 1769476
  186.1 28.2 %collective-permute-start.1 = (bf16[384,1536]{1,0:T(8,128)(2,1)S(1)}, bf16[384,1536]{1,0:T(8,128)(2,1)S(1)}, u32[]{:S(2)}, u32[]{:S(2)}) collective-permute-start(bf16[384,1536]{1,0:T(8,128)(2,1)S(1)} %convolution_convert_fusion.3), channel_id=1, source_target_pairs={{0,1},{1,0},{2,3},{3,2},{4,5},{5,4},{6,7},{7,6},{8,9},{9,8},{10,11... | collective-permute-start | bytes 3538952 | tf_op jit(solution)/shard_map/ppermute | solution.py:112
  218.2 27.6 %copy-start.33 = (bf16[384,1536]{1,0:T(8,128)(2,1)}, bf16[384,1536]{1,0:T(8,128)(2,1)S(1)}, u32[]{:S(2)}) copy-start(bf16[384,1536]{1,0:T(8,128)(2,1)S(1)} %multiply_convert_fusion.7) | copy-start | bytes 3538948
  218.2 27.6 %collective-permute-start.2 = (bf16[384,1536]{1,0:T(8,128)(2,1)S(1)}, bf16[384,1536]{1,0:T(8,128)(2,1)}, u32[]{:S(2)}, u32[]{:S(2)}) collective-permute-start(bf16[384,1536]{1,0:T(8,128)(2,1)S(1)} %multiply_convert_fusion.7), channel_id=1, source_target_pairs={{0,1},{1,0},{2,3},{3,2},{4,5},{5,4},{6,7},{7,6},{8,9},{9,8},{10,11... | collective-permute-start | bytes 3538952 | tf_op jit(solution)/shard_map/ppermute | solution.py:112
  258.0 26.4 %collective-permute-start.3 = (bf16[384,1536]{1,0:T(8,128)(2,1)S(1)}, bf16[384,1536]{1,0:T(8,128)(2,1)S(1)}, u32[]{:S(2)}, u32[]{:S(2)}) collective-permute-start(bf16[384,1536]{1,0:T(8,128)(2,1)S(1)} %convolution_convert_fusion.2), channel_id=1, source_target_pairs={{0,1},{1,0},{2,3},{3,2},{4,5},{5,4},{6,7},{7,6},{8,9},{9,8},{10,11... | collective-permute-start | bytes 3538952 | tf_op jit(solution)/shard_map/ppermute | solution.py:112
  288.8 35.9 %copy-start.31 = (bf16[384,1536]{1,0:T(8,128)(2,1)}, bf16[384,1536]{1,0:T(8,128)(2,1)S(1)}, u32[]{:S(2)}) copy-start(bf16[384,1536]{1,0:T(8,128)(2,1)S(1)} %multiply_convert_fusion.6) | copy-start | bytes 3538948
  288.8 25.6 %collective-permute-start.4 = (bf16[384,1536]{1,0:T(8,128)(2,1)S(1)}, bf16[384,1536]{1,0:T(8,128)(2,1)}, u32[]{:S(2)}, u32[]{:S(2)}) collective-permute-start(bf16[384,1536]{1,0:T(8,128)(2,1)S(1)} %multiply_convert_fusion.6), channel_id=1, source_target_pairs={{0,1},{1,0},{2,3},{3,2},{4,5},{5,4},{6,7},{7,6},{8,9},{9,8},{10,11... | collective-permute-start | bytes 3538952 | tf_op jit(solution)/shard_map/ppermute | solution.py:112
  366.1 39.1 %copy-start.24 = (bf16[1,384,1536]{2,1,0:T(8,128)(2,1)S(1)}, bf16[1,384,1536]{2,1,0:T(8,128)(2,1)}, u32[]{:S(2)}) copy-start(bf16[1,384,1536]{2,1,0:T(8,128)(2,1)} %param.18) | copy-start | bytes 3538948
  375.5 29.7 %collective-permute-start.5 = (bf16[384,1536]{1,0:T(8,128)(2,1)}, bf16[384,1536]{1,0:T(8,128)(2,1)}, u32[]{:S(2)}, u32[]{:S(2)}) collective-permute-start(bf16[384,1536]{1,0:T(8,128)(2,1)} %convolution_convert_fusion.1), channel_id=1, source_target_pairs={{0,1},{1,0},{2,3},{3,2},{4,5},{5,4},{6,7},{7,6},{8,9},{9,8},{10,11... | collective-permute-start | bytes 3538952 | tf_op jit(solution)/shard_map/ppermute | solution.py:112
  379.7 24.3 %collective-permute-start.6 = (f32[8,128]{1,0:T(8,128)S(1)}, f32[8,128]{1,0:T(8,128)S(1)}, u32[]{:S(2)}, u32[]{:S(2)}) collective-permute-start(f32[8,128]{1,0:T(8,128)S(1)} %broadcast_in_dim.23), channel_id=1, source_target_pairs={{0,1},{1,0},{2,3},{3,2},{4,5},{5,4},{6,7},{7,6},{8,9},{9,8},{10,11... | collective-permute-start | bytes 12296 | tf_op jit(solution)/shard_map/ppermute | solution.py:112
  417.0 27.4 %collective-permute-start.7 = (bf16[384,1536]{1,0:T(8,128)(2,1)S(1)}, bf16[384,1536]{1,0:T(8,128)(2,1)S(1)}, u32[]{:S(2)}, u32[]{:S(2)}) collective-permute-start(bf16[384,1536]{1,0:T(8,128)(2,1)S(1)} %multiply_convert_fusion.8), channel_id=1, source_target_pairs={{0,1},{1,0},{2,3},{3,2},{4,5},{5,4},{6,7},{7,6},{8,9},{9,8},{10,11... | collective-permute-start | bytes 3538952 | tf_op jit(solution)/shard_map/ppermute | solution.py:112
  478.8 26.5 %copy-start.2 = (f32[384,1536]{1,0:T(8,128)S(1)}, f32[384,1536]{1,0:T(8,128)}, u32[]{:S(2)}) copy-start(f32[384,1536]{1,0:T(8,128)} %copy-done.1) | copy-start | bytes 7077892
  478.8 26.5 %copy-start.89 = (f32[384]{0:T(512)S(1)}, f32[384]{0:T(512)}, u32[]{:S(2)}) copy-start(f32[384]{0:T(512)} %copy-done.88) | copy-start | bytes 4612
  478.8 26.5 %copy-start.97 = (f32[384]{0:T(512)S(1)}, f32[384]{0:T(512)}, u32[]{:S(2)}) copy-start(f32[384]{0:T(512)} %copy-done.96) | copy-start | bytes 4612
  478.8 26.5 %collective-permute-start.8 = (bf16[384,1536]{1,0:T(8,128)(2,1)S(1)}, bf16[384,1536]{1,0:T(8,128)(2,1)S(1)}, u32[]{:S(2)}, u32[]{:S(2)}) collective-permute-start(bf16[384,1536]{1,0:T(8,128)(2,1)S(1)} %fusion.40), channel_id=1, source_target_pairs={{0,1},{1,0},{2,3},{3,2},{4,5},{5,4},{6,7},{7,6},{8,9},{9,8},{10,11... | collective-permute-start | bytes 3538952 | tf_op jit(solution)/shard_map/ppermute | solution.py:112
  515.5 32.7 %slice-start = ((s8[5013504]{0:T(1024)(128)(4,1)}), s8[4194304]{0:T(1024)(128)(4,1)S(1)}, s32[]{:S(2)}) async-start(s8[5013504]{0:T(1024)(128)(4,1)} %bitcast.152), calls=%async_computation.12 | async-start | bytes 8388608
  518.4 29.7 %copy-start.25 = (bf16[384,1536]{1,0:T(8,128)(2,1)}, bf16[384,1536]{1,0:T(8,128)(2,1)S(1)}, u32[]{:S(2)}) copy-start(bf16[384,1536]{1,0:T(8,128)(2,1)S(1)} %get-tuple-element.83) | copy-start | bytes 3538948
  518.4 25.6 %collective-permute-start.9 = (bf16[384,1536]{1,0:T(8,128)(2,1)S(1)}, bf16[384,1536]{1,0:T(8,128)(2,1)S(1)}, u32[]{:S(2)}, u32[]{:S(2)}) collective-permute-start(bf16[384,1536]{1,0:T(8,128)(2,1)S(1)} %get-tuple-element.83), channel_id=1, source_target_pairs={{0,1},{1,0},{2,3},{3,2},{4,5},{5,4},{6,7},{7,6},{8,9},{9,8},{10,11... | collective-permute-start | bytes 3538952 | tf_op jit(solution)/shard_map/ppermute | solution.py:112
  519.9 29.6 %copy-start.66 = (f32[12,768]{1,0:T(8,128)}, f32[12,768]{1,0:T(8,128)S(1)}, u32[]{:S(2)}) copy-start(f32[12,768]{1,0:T(8,128)S(1)} %log_add_fusion) | copy-start | bytes 110596
  519.9 28.2 %slice-start.1 = ((s8[5013504]{0:T(1024)(128)(4,1)}), s8[819200]{0:T(1024)(128)(4,1)S(1)}, s32[]{:S(2)}) async-start(s8[5013504]{0:T(1024)(128)(4,1)} %bitcast.152), calls=%async_computation.13 | async-start | bytes 1638400
  520.0 28.2 %copy-start.57 = (bf16[130,768]{0,1:T(8,128)(2,1)S(1)}, bf16[130,768]{0,1:T(8,128)(2,1)}, u32[]{:S(2)}) copy-start(bf16[130,768]{0,1:T(8,128)(2,1)} %copy.117) | copy-start | bytes 599044
  556.5 24.9 %collective-permute-start.10 = (bf16[384,1536]{1,0:T(8,128)(2,1)}, bf16[384,1536]{1,0:T(8,128)(2,1)}, u32[]{:S(2)}, u32[]{:S(2)}) collective-permute-start(bf16[384,1536]{1,0:T(8,128)(2,1)} %convolution_convert_fusion), channel_id=1, source_target_pairs={{0,1},{1,0},{2,3},{3,2},{4,5},{5,4},{6,7},{7,6},{8,9},{9,8},{10,11... | collective-permute-start | bytes 3538952 | tf_op jit(solution)/shard_map/ppermute | solution.py:112
  561.3 28.4 %collective-permute-start.34 = (bf16[768,1536]{1,0:T(8,128)(2,1)}, bf16[768,1536]{1,0:T(8,128)(2,1)}, u32[]{:S(2)}, u32[]{:S(2)}) collective-permute-start(bf16[768,1536]{1,0:T(8,128)(2,1)} %constant_dynamic-slice_fusion.2), channel_id=1, source_target_pairs={{0,2},{2,0},{1,3},{3,1},{4,6},{6,4},{5,7},{7,5},{8,10},{10,8},{9,1... | collective-permute-start | bytes 7077896 | tf_op jit(solution)/shard_map/ppermute | solution.py:115
  562.9 26.8 %collective-permute-start.33 = (bf16[768,1536]{1,0:T(8,128)(2,1)}, bf16[768,1536]{1,0:T(8,128)(2,1)}, u32[]{:S(2)}, u32[]{:S(2)}) collective-permute-start(bf16[768,1536]{1,0:T(8,128)(2,1)} %pad_maximum_fusion.6), channel_id=1, source_target_pairs={{0,2},{2,0},{1,3},{3,1},{4,6},{6,4},{5,7},{7,5},{8,10},{10,8},{9,1... | collective-permute-start | bytes 7077896 | tf_op jit(solution)/shard_map/ppermute | solution.py:115
  566.4 134.0 %collective-permute-start.14 = (bf16[768,1536]{1,0:T(8,128)(2,1)}, bf16[768,1536]{1,0:T(8,128)(2,1)}, u32[]{:S(2)}, u32[]{:S(2)}) collective-permute-start(bf16[768,1536]{1,0:T(8,128)(2,1)} %pad_maximum_fusion.3), channel_id=1, source_target_pairs={{0,2},{2,0},{1,3},{3,1},{4,6},{6,4},{5,7},{7,5},{8,10},{10,8},{9,1... | collective-permute-start | bytes 7077896 | tf_op jit(solution)/shard_map/ppermute | solution.py:115
  588.2 23.8 %collective-permute-start.11 = (bf16[384,1536]{1,0:T(8,128)(2,1)S(1)}, bf16[384,1536]{1,0:T(8,128)(2,1)}, u32[]{:S(2)}, u32[]{:S(2)}) collective-permute-start(bf16[384,1536]{1,0:T(8,128)(2,1)S(1)} %get-tuple-element.81), channel_id=1, source_target_pairs={{0,1},{1,0},{2,3},{3,2},{4,5},{5,4},{6,7},{7,6},{8,9},{9,8},{10,11... | collective-permute-start | bytes 3538952 | tf_op jit(solution)/shard_map/ppermute | solution.py:112
  603.1 319.6 %reduce-scatter.13.cloned.1.call-start = ((), (), s32[]{:S(2)}) async-start(), calls=%async_computation.9 | async-start | bytes 3981312
  650.8 44.3 %copy-start.9 = (bf16[12,64,768]{2,1,0:T(8,128)(2,1)}, bf16[12,64,768]{2,1,0:T(8,128)(2,1)S(1)}, u32[]{:S(2)}) copy-start(bf16[12,64,768]{2,1,0:T(8,128)(2,1)S(1)} %fusion.133) | copy-start | bytes 3538948
  683.8 16.6 %collective-permute-start.17 = (bf16[768,384]{0,1:T(8,128)(2,1)}, bf16[768,384]{0,1:T(8,128)(2,1)}, u32[]{:S(2)}, u32[]{:S(2)}) collective-permute-start(bf16[768,384]{0,1:T(8,128)(2,1)} %constant_dynamic-slice_fusion.16), channel_id=1, source_target_pairs={{0,2},{2,0},{1,3},{3,1},{4,6},{6,4},{5,7},{7,5},{8,10},{10,8},{9,1... | collective-permute-start | bytes 1769480 | tf_op jit(solution)/shard_map/ppermute | solution.py:115
  694.6 8.8 collective-permute-start.16
  698.8 7.3 collective-permute-start.15
  713.1 212.7 %reduce-scatter.15.cloned.1.call-start = ((), (), s32[]{:S(2)}) async-start(), calls=%async_computation.10 | async-start | bytes 6635520
  716.3 8.0 collective-permute-start.21
  716.5 14.1 %collective-permute-start.27 = (bf16[768,384]{0,1:T(8,128)(2,1)S(1)}, bf16[768,384]{0,1:T(8,128)(2,1)S(1)}, u32[]{:S(2)}, u32[]{:S(2)}) collective-permute-start(bf16[768,384]{0,1:T(8,128)(2,1)S(1)} %constant_dynamic-slice_fusion.9), channel_id=1, source_target_pairs={{0,2},{2,0},{1,3},{3,1},{4,6},{6,4},{5,7},{7,5},{8,10},{10,8},{9,1... | collective-permute-start | bytes 1769480 | tf_op jit(solution)/shard_map/ppermute | solution.py:115
  717.3 13.8 %collective-permute-start.26 = (bf16[768,1536]{1,0:T(8,128)(2,1)S(1)}, bf16[768,1536]{1,0:T(8,128)(2,1)S(1)}, u32[]{:S(2)}, u32[]{:S(2)}) collective-permute-start(bf16[768,1536]{1,0:T(8,128)(2,1)S(1)} %pad_maximum_fusion.7), channel_id=1, source_target_pairs={{0,2},{2,0},{1,3},{3,1},{4,6},{6,4},{5,7},{7,5},{8,10},{10,8},{9,1... | collective-permute-start | bytes 7077896 | tf_op jit(solution)/shard_map/ppermute | solution.py:115
  720.0 12.3 %collective-permute-start.19 = (bf16[768,1536]{1,0:T(8,128)(2,1)S(1)}, bf16[768,1536]{1,0:T(8,128)(2,1)S(1)}, u32[]{:S(2)}, u32[]{:S(2)}) collective-permute-start(bf16[768,1536]{1,0:T(8,128)(2,1)S(1)} %pad_maximum_fusion.8), channel_id=1, source_target_pairs={{0,2},{2,0},{1,3},{3,1},{4,6},{6,4},{5,7},{7,5},{8,10},{10,8},{9,1... | collective-permute-start | bytes 7077896 | tf_op jit(solution)/shard_map/ppermute | solution.py:115
  720.7 8.6 collective-permute-start.22
  724.3 15.9 %collective-permute-start.24 = (bf16[130,1536]{1,0:T(8,128)(2,1)S(1)}, bf16[130,1536]{1,0:T(8,128)(2,1)S(1)}, u32[]{:S(2)}, u32[]{:S(2)}) collective-permute-start(bf16[130,1536]{1,0:T(8,128)(2,1)S(1)} %bitcast.194), channel_id=1, source_target_pairs={{0,2},{2,0},{1,3},{3,1},{4,6},{6,4},{5,7},{7,5},{8,10},{10,8},{9,1... | collective-permute-start | bytes 1198088 | tf_op jit(solution)/shard_map/ppermute | solution.py:115
  729.3 2.9 collective-permute-start.20
  730.6 9.6 collective-permute-start.23
  731.0 10.7 collective-permute-start.25
  753.9 319.7 %reduce-scatter.17.cloned.1.call-start = ((), (), s32[]{:S(2)}) async-start(), calls=%async_computation.11 | async-start | bytes 10616832
  756.6 4.7 collective-permute-start.29
  758.8 5.8 collective-permute-start.31
  761.0 10.2 collective-permute-start.30
  828.7 39.1 %collective-permute-start.12 = (bf16[384,1536]{1,0:T(8,128)(2,1)}, bf16[384,1536]{1,0:T(8,128)(2,1)}, u32[]{:S(2)}, u32[]{:S(2)}) collective-permute-start(bf16[384,1536]{1,0:T(8,128)(2,1)} %fusion.54), channel_id=1, source_target_pairs={{0,1},{1,0},{2,3},{3,2},{4,5},{5,4},{6,7},{7,6},{8,9},{9,8},{10,11... | collective-permute-start | bytes 3538952 | tf_op jit(solution)/shard_map/ppermute | solution.py:112
  832.8 35.0 %copy-start.106 = (f32[1536]{0:T(1024)S(1)}, f32[1536]{0:T(1024)}, u32[]{:S(2)}) copy-start(f32[1536]{0:T(1024)} %get-tuple-element.67) | copy-start | bytes 18436
  832.8 35.0 %copy-start.6 = (bf16[1,384,1536]{2,1,0:T(8,128)(2,1)S(1)}, bf16[1,384,1536]{2,1,0:T(8,128)(2,1)}, u32[]{:S(2)}) copy-start(bf16[1,384,1536]{2,1,0:T(8,128)(2,1)} %param.16) | copy-start | bytes 3538948
  832.8 35.0 %copy-start.85 = (f32[1536]{0:T(1024)S(1)}, f32[1536]{0:T(1024)}, u32[]{:S(2)}) copy-start(f32[1536]{0:T(1024)} %copy-done.84) | copy-start | bytes 18436
  832.8 35.0 %copy-start.92 = (f32[384]{0:T(512)S(1)}, f32[384]{0:T(512)}, u32[]{:S(2)}) copy-start(f32[384]{0:T(512)} %copy-done.90) | copy-start | bytes 4612
  832.8 35.0 %copy-start.101 = (f32[384]{0:T(512)S(1)}, f32[384]{0:T(512)}, u32[]{:S(2)}) copy-start(f32[384]{0:T(512)} %add_rsqrt_fusion.3) | copy-start | bytes 4612
  832.8 33.1 %collective-permute-start.13 = (bf16[130,1536]{1,0:T(8,128)(2,1)S(1)}, bf16[130,1536]{1,0:T(8,128)(2,1)S(1)}, u32[]{:S(2)}, u32[]{:S(2)}) collective-permute-start(bf16[130,1536]{1,0:T(8,128)(2,1)S(1)} %fusion.66), channel_id=1, source_target_pairs={{0,1},{1,0},{2,3},{3,2},{4,5},{5,4},{6,7},{7,6},{8,9},{9,8},{10,11... | collective-permute-start | bytes 1198088 | tf_op jit(solution)/shard_map/ppermute | solution.py:112
  878.7 43.0 %collective-permute-start.35 = (bf16[96,1536]{1,0:T(8,128)(2,1)S(1)}, bf16[96,1536]{1,0:T(8,128)(2,1)S(1)}, u32[]{:S(2)}, u32[]{:S(2)}) collective-permute-start(bf16[96,1536]{1,0:T(8,128)(2,1)S(1)} %constant_dynamic-slice_fusion.1), channel_id=1, source_target_pairs={{0,2},{2,0},{1,3},{3,1},{4,6},{6,4},{5,7},{7,5},{8,10},{10,8},{9,1... | collective-permute-start | bytes 884744 | tf_op jit(solution)/shard_map/ppermute | solution.py:115
  924.1 1.6 collective-permute-start.18
  927.3 3.4 collective-permute-start.28
  1074.9 5.0 collective-permute-start.32
  (98 other events, 613.5 us)
Sparse Core Ops, SparseCore 0:
  14.1 71.9 all-gather.4
  89.0 94.1 all-gather.6
  185.4 97.1 all-gather.8
  284.7 81.4 all-gather.10
  603.2 92.7 reduce-scatter.10
  713.2 77.5 reduce-scatter.12
  794.5 112.0 reduce-scatter.14
  910.2 163.3 reduce-scatter.16

commit v2 on v1

v2 whole, which is shorter than its diff:
```python
import functools
import math

import jax
import jax.numpy as jnp
from jax import lax
from jax.experimental import pallas as pl
from jax.experimental.pallas import tpu as pltpu
from jax.sharding import Mesh, PartitionSpec as P

HEAD_DIM = 64
PAIR = 2 * HEAD_DIM
SCALE = HEAD_DIM**-0.5
EPSILON = 1e-05
F32 = jnp.float32
BF16 = jnp.bfloat16
KERNEL_VMEM = 24 << 20
PACK_VMEM = 56 << 20
GRAD_VMEM = 32 << 20
BACK_VMEM = 44 << 20
DOWN_PIECES = (768, 512, 256)
GATE_PIECES = (1024, 512)
UP_PIECES = (256, 1280)
PULL_ROWS = 256
NORM_ROWS = 128
FEED_COLUMNS = 512
SMALL_COST = pl.CostEstimate(flops=1 << 20, bytes_accessed=1 << 14, transcendentals=0)


def dot(left, right, left_dim, right_dim):
    return lax.dot_general(
        left, right, (((left_dim,), (right_dim,)), ((), ())), preferred_element_type=F32
    )


def norm_stats(values):
    row_mean = jnp.mean(values, axis=-1, keepdims=True)
    centred = values - row_mean
    row_var = jnp.mean(centred * centred, axis=-1, keepdims=True)
    inverse = lax.rsqrt(row_var + EPSILON)
    return (centred * inverse, inverse)


def rotary_tables(positions):
    half_dim = HEAD_DIM // 2
    freqs = jnp.exp(jnp.arange(half_dim, dtype=F32) * (-math.log(10000.0) / half_dim))
    angles = positions.astype(F32)[:, None] * freqs[None, :]
    cosine, sine = jnp.cos(angles), jnp.sin(angles)
    return (
        jnp.concatenate([cosine] * 4, axis=1),
        jnp.concatenate([-sine, sine] * 2, axis=1),
    )


def spin(values, cosines, sines):
    lane = lax.broadcasted_iota(jnp.int32, values.shape, 1)
    ahead = pltpu.roll(values, PAIR - HEAD_DIM // 2, 1)
    behind = pltpu.roll(values, HEAD_DIM // 2, 1)
    other = jnp.where(lane % HEAD_DIM < HEAD_DIM // 2, ahead, behind)
    return values * cosines + other * sines


def one_head(values, head):
    lane = lax.broadcasted_iota(jnp.int32, values.shape, 1)
    return jnp.where(lane // HEAD_DIM == head, values, jnp.zeros_like(values))


def turn(values):
    return values.astype(F32).T.astype(BF16)


def attend(keys, key_count, queries, values_t, out_ref, log_ref):
    mixed = []
    for head in range(2):
        scores = dot(keys, one_head(queries, head), 1, 1)
        if key_count < keys.shape[0]:
            row = lax.broadcasted_iota(jnp.int32, scores.shape, 0)
            scores = jnp.where(row < key_count, scores, -1e30)
        top = jnp.max(scores, axis=0, keepdims=True)
        shifted = jnp.exp(scores - top)
        total = jnp.sum(shifted, axis=0, keepdims=True)
        part = values_t[head * HEAD_DIM : (head + 1) * HEAD_DIM]
        mixed.append(dot(part, shifted.astype(BF16), 1, 0) / total)
        log_ref[0, head : head + 1, :] = top + jnp.log(total)
    out_ref[...] = jnp.concatenate(mixed, axis=0).T.astype(BF16)


def attend_back(queries, keys, key_count, values, grads, logs):
    keys_t = keys.astype(F32).T.astype(BF16)
    grad_k = jnp.zeros((keys.shape[0], PAIR), F32)
    grad_v = jnp.zeros((keys.shape[0], PAIR), F32)
    grad_q = []
    for head in range(2):
        query, grad = one_head(queries, head), one_head(grads, head)
        probs = jnp.exp(dot(keys, query, 1, 1) - logs[head : head + 1])
        if key_count < keys.shape[0]:
            row = lax.broadcasted_iota(jnp.int32, probs.shape, 0)
            probs = jnp.where(row < key_count, probs, 0.0)
        product = probs * dot(values, grad, 1, 1)
        weighted = jnp.sum(product, axis=0, keepdims=True)
        grad_s = (product - probs * weighted).astype(BF16)
        grad_v = grad_v + dot(probs.astype(BF16), grad, 1, 0)
        grad_k = grad_k + dot(grad_s, query, 1, 0)
        grad_q.append(dot(keys_t[head * HEAD_DIM : (head + 1) * HEAD_DIM], grad_s, 1, 0))
    return (jnp.concatenate(grad_q, axis=0).T * SCALE, grad_k, grad_v)


def self_forward_kernel(qkv, cos_in, sin_in, mixed, q_out, k_out, v_out, logs):
    cosines, sines = cos_in[...], sin_in[...]
    queries = spin(qkv[:, :PAIR], cosines, sines).astype(BF16).astype(F32)
    queries = (queries * SCALE).astype(BF16)
    keys = spin(qkv[:, PAIR : 2 * PAIR], cosines, sines).astype(BF16)
    values = qkv[:, 2 * PAIR :]
    q_out[...] = queries
    k_out[...] = keys
    v_out[...] = values.astype(BF16)
    attend(keys, keys.shape[0], queries, values.T.astype(BF16), mixed, logs)


def self_back_kernel(
    places, q_in, k_in, v_in, own_in, peer_in, out_w, qkv_w, logs, cos_in, sin_in,
    out, sent, own_out, peer_out, peer_sum,
):
    pair, pairs = pl.program_id(0), pl.num_programs(0)
    cosines, sines = cos_in[...], -sin_in[...]
    keys, weights = k_in[...], out_w[...]
    grads = jnp.concatenate([dot(own_in[...], weights, 1, 0), dot(peer_in[...], weights, 1, 0)], axis=0)
    grad_q, grad_k, grad_v = attend_back(
        q_in[...], keys, keys.shape[0], v_in[...], grads.astype(BF16), logs[0]
    )
    out[:, :PAIR] = spin(grad_q, cosines, sines).astype(BF16)
    out[:, PAIR : 2 * PAIR] = spin(grad_k, cosines, sines).astype(BF16)
    out[:, 2 * PAIR :] = grad_v.astype(BF16)

    @pl.when((2 * pair >= pairs) == (places[1] == 0))
    def _():
        sent[...] = out[...]

    rows = own_in.shape[0]
    own = dot(out[:rows, :], qkv_w[...], 1, 1)
    peer = dot(out[rows:, :], qkv_w[...], 1, 1)

    @pl.when(pair == 0)
    def _():
        own_out[...] = own
        peer_sum[...] = peer

    @pl.when(pair > 0)
    def _():
        own_out[...] += own
        peer_sum[...] += peer

    @pl.when(pair == pairs - 1)
    def _():
        peer_out[...] = peer_sum[...].astype(BF16)


def pick(own, peer):
    return jnp.where(2 * pl.program_id(0) < pl.num_programs(0), own[...], peer[...])


def cross_forward_kernel(key_count, q_own, q_peer, kv_own, kv_peer, mixed, logs):
    queries, keyvals = pick(q_own, q_peer), pick(kv_own, kv_peer)
    queries = (queries.astype(F32) * SCALE).astype(BF16)
    attend(keyvals[:, :PAIR], key_count, queries, turn(keyvals[:, PAIR:]), mixed, logs)


def cross_back_kernel(
    key_count, q_own, q_peer, g_own, g_peer, kv_own, kv_peer, logs, q_out, kv_out
):
    queries, keyvals = pick(q_own, q_peer), pick(kv_own, kv_peer)
    queries = (queries.astype(F32) * SCALE).astype(BF16)
    grad_q, grad_k, grad_v = attend_back(
        queries, keyvals[:, :PAIR], key_count, keyvals[:, PAIR:], pick(g_own, g_peer), logs[0]
    )
    q_out[...] = grad_q.astype(BF16)
    kv_out[:, :PAIR] = grad_k.astype(BF16)
    kv_out[:, PAIR:] = grad_v.astype(BF16)


def column_block(count):
    return pl.BlockSpec((count, PAIR), lambda i: (0, i))


def call_pairs(kernel, width, in_specs, out_specs, out_shape, args):
    return pl.pallas_call(
        kernel,
        grid=(width // PAIR,),
        in_specs=in_specs,
        out_specs=out_specs,
        out_shape=out_shape,
        compiler_params=pltpu.CompilerParams(vmem_limit_bytes=KERNEL_VMEM),
        cost_estimate=SMALL_COST,
    )(*args)


def self_forward(qkv, cosines, sines):
    rows, width = qkv.shape[0], qkv.shape[1] // 3
    pairs = width // PAIR
    table = pl.BlockSpec((rows, PAIR), lambda i: (0, 0))
    act = jax.ShapeDtypeStruct((rows, width), BF16)
    return call_pairs(
        self_forward_kernel,
        width,
        [pl.BlockSpec((rows, 3 * PAIR), lambda i: (0, i)), table, table],
        [column_block(rows)] * 4 + [pl.BlockSpec((1, 2, rows), lambda i: (i, 0, 0))],
        [act] * 4 + [jax.ShapeDtypeStruct((pairs, 2, rows), F32)],
        (qkv, cosines, sines),
    )


def self_back(places, queries, keys, values, own, peer, weights, logs, cosines, sines):
    rows, width = queries.shape
    count, depth = own.shape
    pairs = width // PAIR
    block = pl.BlockSpec((rows, PAIR), lambda i, places: (0, i))
    table = pl.BlockSpec((rows, PAIR), lambda i, places: (0, 0))
    token = pl.BlockSpec((count, depth), lambda i, places: (0, 0))
    half = pairs // 2
    return pl.pallas_call(
        self_back_kernel,
        grid_spec=pltpu.PrefetchScalarGridSpec(
            num_scalar_prefetch=1,
            grid=(pairs,),
            in_specs=[
                block,
                block,
                block,
                token,
                token,
                pl.BlockSpec((depth, PAIR), lambda i, places: (0, 3 * pairs + i)),
                pl.BlockSpec((depth, 3 * PAIR), lambda i, places: (0, i)),
                pl.BlockSpec((1, 2, rows), lambda i, places: (i, 0, 0)),
                table,
                table,
            ],
            out_specs=[
                pl.BlockSpec((rows, 3 * PAIR), lambda i, places: (0, i)),
                pl.BlockSpec(
                    (rows, 3 * PAIR),
                    lambda i, places: (0, jnp.clip(i - half * (1 - places[1]), 0, half - 1)),
                ),
                token,
                token,
            ],
            scratch_shapes=[pltpu.VMEM((count, depth), F32)],
        ),
        out_shape=[
            jax.ShapeDtypeStruct((rows, 3 * width), BF16),
            jax.ShapeDtypeStruct((rows, 3 * width // 2), BF16),
            jax.ShapeDtypeStruct((count, depth), F32),
            jax.ShapeDtypeStruct((count, depth), BF16),
        ],
        compiler_params=pltpu.CompilerParams(vmem_limit_bytes=BACK_VMEM),
        cost_estimate=SMALL_COST,
    )(places, queries, keys, values, own, peer, weights, weights, logs, cosines, sines)


def cross_call(kernel, key_count, arrays, logs, out_specs, out_shape):
    pairs = arrays[0][0].shape[1] // PAIR
    specs, args = [], []
    for own, peer in arrays:
        block = (own.shape[0], own.shape[1] // pairs)
        specs.append(pl.BlockSpec(block, lambda i: (0, jnp.minimum(i, pairs - 1))))
        specs.append(pl.BlockSpec(block, lambda i: (0, jnp.maximum(i - pairs, 0))))
        args += [own, peer]
    if logs is not None:
        specs.append(pl.BlockSpec((1,) + logs.shape[1:], lambda i: (i, 0, 0)))
        args.append(logs)
    return pl.pallas_call(
        functools.partial(kernel, key_count),
        grid=(2 * pairs,),
        in_specs=specs,
        out_specs=out_specs,
        out_shape=out_shape,
        compiler_params=pltpu.CompilerParams(vmem_limit_bytes=KERNEL_VMEM),
        cost_estimate=SMALL_COST,
    )(*args)


def cross_forward(queries, keyvals, key_count):
    rows, width = queries[0].shape
    return cross_call(
        cross_forward_kernel,
        key_count,
        (queries, keyvals),
        None,
        [column_block(rows), pl.BlockSpec((1, 2, rows), lambda i: (i, 0, 0))],
        [
            jax.ShapeDtypeStruct((rows, 2 * width), BF16),
            jax.ShapeDtypeStruct((2 * width // PAIR, 2, rows), F32),
        ],
    )


def cross_back(queries, grads, keyvals, logs, key_count):
    rows, width = queries[0].shape
    keys = keyvals[0].shape[0]
    return cross_call(
        cross_back_kernel,
        key_count,
        (queries, grads, keyvals),
        logs,
        [column_block(rows), pl.BlockSpec((keys, 2 * PAIR), lambda i: (0, i))],
        [
            jax.ShapeDtypeStruct((rows, 2 * width), BF16),
            jax.ShapeDtypeStruct((keys, 4 * width), BF16),
        ],
    )


def norm_back_kernel(away, *refs):
    pulled, peer = refs[0], refs[1] if away else None
    hidden, gain_row, skip, total_out, low_out, gain_out = refs[1 + away :]
    grad = pulled[...] + peer[...].astype(F32) if away else pulled[...]
    normed, inverse = norm_stats(hidden[...].astype(F32))
    scaled = grad * gain_row[...]
    mean_scaled = jnp.mean(scaled, axis=-1, keepdims=True)
    mean_product = jnp.mean(scaled * normed, axis=-1, keepdims=True)
    total = skip[...] + inverse * (scaled - mean_scaled - normed * mean_product)
    total_out[...] = total
    low_out[...] = total.astype(BF16)
    received = jnp.sum(grad * normed, axis=0, keepdims=True)

    @pl.when(pl.program_id(0) == 0)
    def _():
        gain_out[...] = received

    @pl.when(pl.program_id(0) > 0)
    def _():
        gain_out[...] += received


def norm_back(pulled, away, hidden, gain_row, skip):
    rows, depth = pulled.shape
    block = pl.BlockSpec((NORM_ROWS, depth), lambda i: (i, 0))
    row = pl.BlockSpec((1, depth), lambda i: (0, 0))
    arrays = (pulled,) if away is None else (pulled, away)
    return pl.pallas_call(
        functools.partial(norm_back_kernel, len(arrays) - 1),
        grid=(rows // NORM_ROWS,),
        in_specs=[block] * len(arrays) + [block, row, block],
        out_specs=[block, block, row],
        out_shape=[
            jax.ShapeDtypeStruct((rows, depth), F32),
            jax.ShapeDtypeStruct((rows, depth), BF16),
            jax.ShapeDtypeStruct((1, depth), F32),
        ],
        compiler_params=pltpu.CompilerParams(vmem_limit_bytes=KERNEL_VMEM),
        cost_estimate=SMALL_COST,
    )(*arrays, hidden, gain_row, skip)


def feed_back_kernel(places, g_in, weights, gate_in, up_in, gate_out, up_out, sent):
    grad_hidden = dot(g_in[...], weights[...], 1, 0)
    gate_pre, up_pre = gate_in[...].astype(F32), up_in[...].astype(F32)
    sigmoid = 1.0 / (1.0 + jnp.exp(-gate_pre))
    grad_gate = grad_hidden * up_pre * sigmoid * (1.0 + gate_pre * (1.0 - sigmoid))
    gate_out[...] = grad_gate.astype(BF16)
    up_out[...] = (grad_hidden * (gate_pre * sigmoid)).astype(BF16)

    @pl.when((2 * pl.program_id(0) >= pl.num_programs(0)) == (places[1] == 0))
    def _():
        sent[0] = gate_out[...]
        sent[1] = up_out[...]


def feed_back(places, grads, weights, gate_pre, up_pre, part):
    rows, depth = grads.shape
    width = gate_pre.shape[1]
    steps = width // FEED_COLUMNS
    half = steps // 2
    column = pl.BlockSpec((rows, FEED_COLUMNS), lambda i, places: (0, i))
    row_part = pl.BlockSpec((rows, FEED_COLUMNS), lambda i, places: (part, i))
    act = jax.ShapeDtypeStruct((rows, width), BF16)
    return pl.pallas_call(
        feed_back_kernel,
        grid_spec=pltpu.PrefetchScalarGridSpec(
            num_scalar_prefetch=1,
            grid=(steps,),
            in_specs=[
                pl.BlockSpec((rows, depth), lambda i, places: (0, 0)),
                pl.BlockSpec((depth, FEED_COLUMNS), lambda i, places: (0, 2 * steps + i)),
                row_part,
                row_part,
            ],
            out_specs=[
                column,
                column,
                pl.BlockSpec(
                    (2, rows, FEED_COLUMNS),
                    lambda i, places: (0, 0, jnp.clip(i - half * (1 - places[1]), 0, half - 1)),
                ),
            ],
        ),
        out_shape=[act, act, jax.ShapeDtypeStruct((2, rows, width // 2), BF16)],
        compiler_params=pltpu.CompilerParams(vmem_limit_bytes=BACK_VMEM),
        cost_estimate=SMALL_COST,
    )(places, grads, weights, gate_pre, up_pre)


def weight_grad_kernel(count, pieces, group, places, *refs):
    outs = refs[2 * count :]
    total = dot(refs[0][...], refs[1][...], 0, 0)
    for index in range(1, count):
        total = total + dot(refs[2 * index][...], refs[2 * index + 1][...], 0, 0)

    def side(index):
        starts = range(index * group, total.shape[0], 2 * group)
        parts = [total[at : at + group] for at in starts]
        return (jnp.concatenate(parts, axis=0) if len(parts) > 1 else parts[0]).astype(BF16)

    first, second = side(0), side(1)

    def write(values, targets):
        at = 0
        for piece, target in zip(pieces, targets, strict=True):
            target[...] = values[:, at : at + piece]
            at += piece

    @pl.when(places[0] == 0)
    def _():
        write(first, outs[: len(pieces)])
        write(second, outs[len(pieces) :])

    @pl.when(places[0] != 0)
    def _():
        write(second, outs[: len(pieces)])
        write(first, outs[len(pieces) :])


def weight_grad(places, far, pieces, parts):
    columns = sum(pieces)
    sides = [[side if isinstance(side, tuple) else (side, None) for side in part[:2]] for part in parts]
    depth = sides[0][0][0].shape[1]
    block = math.lcm(depth // far, 128)
    specs, args = [], []
    for ((left, left_half), (right, right_half)), (_, _, at) in zip(sides, parts, strict=True):
        tokens = left.shape[0] if left_half is None else left.shape[0] // 2
        first, second = left_half or 0, right_half or 0
        specs.append(pl.BlockSpec((tokens, block), lambda i, places, first=first: (first, i)))
        if at is None:
            spec = pl.BlockSpec(
                (tokens, columns), lambda i, places, second=second: (second, places[1])
            )
        elif right.ndim == 3:
            spec = pl.BlockSpec(
                (pl.Squeezed(), tokens, columns), lambda i, places, at=at: (at, 0, 0)
            )
        else:
            spec = pl.BlockSpec(
                (tokens, columns), lambda i, places, second=second, at=at: (second, at)
            )
        specs.append(spec)
        args += [left, right]
    outs = pl.pallas_call(
        functools.partial(weight_grad_kernel, len(parts), pieces, depth // far // 2),
        grid_spec=pltpu.PrefetchScalarGridSpec(
            num_scalar_prefetch=1,
            grid=(depth // block,),
            in_specs=specs,
            out_specs=[
                pl.BlockSpec((block // 2, piece), lambda i, places: (i, 0)) for piece in 2 * pieces
            ],
        ),
        out_shape=[jax.ShapeDtypeStruct((depth // 2, piece), BF16) for piece in 2 * pieces],
        compiler_params=pltpu.CompilerParams(vmem_limit_bytes=GRAD_VMEM),
        cost_estimate=SMALL_COST,
    )(places, *args)
    return outs[: len(pieces)], outs[len(pieces) :]


def pull_kernel(gate_in, up_in, weights, out):
    width = gate_in.shape[1]
    total = dot(gate_in[...], weights[:, :width], 1, 1) + dot(up_in[...], weights[:, width:], 1, 1)
    out[...] = total.astype(out.dtype)


def pull(grad_gate, grad_upper, weights, kind):
    rows, width = grad_gate.shape
    depth = weights.shape[0]
    whole = pl.BlockSpec((rows, width), lambda i: (0, 0))
    return pl.pallas_call(
        pull_kernel,
        grid=(depth // PULL_ROWS,),
        in_specs=[whole, whole, pl.BlockSpec((PULL_ROWS, 2 * width), lambda i: (i, 0))],
        out_specs=pl.BlockSpec((rows, PULL_ROWS), lambda i: (0, i)),
        out_shape=jax.ShapeDtypeStruct((rows, depth), kind),
        compiler_params=pltpu.CompilerParams(vmem_limit_bytes=GRAD_VMEM),
        cost_estimate=SMALL_COST,
    )(grad_gate, grad_upper, weights)


def pack_attention_kernel(q_in, k_in, v_in, o_in, cq_in, ck_in, cv_in, co_in, gains, mask, out):
    width = q_in.shape[1]
    for pair in range(width // PAIR):
        for index, ref in enumerate((q_in, k_in, v_in)):
            at = (3 * pair + index) * PAIR
            out[:, at : at + PAIR] = ref[:, pair * PAIR : (pair + 1) * PAIR]
    out[:, 3 * width : 4 * width] = turn(o_in[...])
    for pair in range(width // PAIR):
        for index, ref in enumerate((ck_in, cv_in)):
            at = 4 * width + (2 * pair + index) * PAIR
            out[:, at : at + PAIR] = ref[:, pair * PAIR : (pair + 1) * PAIR]
    out[:, 6 * width : 7 * width] = cq_in[...]
    out[:, 7 * width : 8 * width] = turn(co_in[...])
    count = jnp.sum(mask[...].astype(F32), axis=1, keepdims=True)
    upper = jnp.floor(count * (1.0 / 128.0))
    side = gains[...].astype(F32).T
    row = lax.broadcasted_iota(jnp.int32, side.shape, 0)
    lane = lax.broadcasted_iota(jnp.int32, side.shape, 1)
    side = jnp.where((lane == 3) & (row == 0), upper, side)
    side = jnp.where((lane == 3) & (row == 1), count - 128.0 * upper, side)
    out[:, 8 * width :] = side.astype(BF16)


def pack_feed_kernel(gate_in, up_in, down_in, out):
    width = gate_in.shape[1]
    out[:, :width] = gate_in[...]
    out[:, width : 2 * width] = up_in[...]
    out[:, 2 * width :] = turn(down_in[...])


def pack(kernel, columns, *parts):
    return pl.pallas_call(
        kernel,
        out_shape=jax.ShapeDtypeStruct((parts[0].shape[0], columns), BF16),
        compiler_params=pltpu.CompilerParams(vmem_limit_bytes=PACK_VMEM),
    )(*parts)


def after(value, *earlier):
    return lax.optimization_barrier((value, *earlier))[0]


def body(
    x_input,
    cond_tokens,
    teacher,
    valid_mask,
    norm_gains,
    w_query,
    w_key,
    w_value,
    w_out,
    c_query,
    c_key,
    c_value,
    c_out,
    w_gate,
    w_up,
    w_down,
):
    far = lax.axis_size("far")
    near_at, pair, share = (lax.axis_index(name) for name in ("near", "core", "tensor"))
    dp_axes = ("far", "near", "core")
    dp_size = 4 * far
    swap = [(0, 1), (1, 0)]

    def to_peer(values):
        return lax.ppermute(values, "tensor", swap)

    def to_core(values):
        return lax.ppermute(values, "core", swap)

    def to_near(values):
        return lax.ppermute(values, "near", swap)

    def gather(values):
        return lax.all_gather(values, dp_axes, axis=0, tiled=True)

    x_bf = x_input[0]
    rows, width = x_bf.shape
    slab = w_query.shape[0]
    heads_width = w_query.shape[1]
    ff_width = w_gate.shape[1]
    length = 2 * rows
    ctx_len = cond_tokens.shape[1]
    cond_rows = jnp.pad(cond_tokens[0], ((0, -ctx_len % 16), (0, 0)))
    mask_float = valid_mask[0].astype(F32)
    x_peer_bf = to_peer(x_bf)

    gath_a = gather(
        pack(
            pack_attention_kernel,
            8 * heads_width + PAIR,
            w_query,
            w_key,
            w_value,
            w_out,
            c_query,
            c_key,
            c_value,
            c_out,
            jnp.pad(norm_gains, ((0, PAIR - 3), (0, 0))),
            valid_mask,
        )
    )
    gath_b = gather(pack(pack_feed_kernel, 3 * ff_width, w_gate, w_up, w_down))

    weight_qkv = gath_a[:, : 3 * heads_width]
    weight_o = gath_a[:, 3 * heads_width : 4 * heads_width]
    cross_kv = gath_a[:, 4 * heads_width : 6 * heads_width]
    side = gath_a[:, 8 * heads_width :].T[:8].astype(F32)
    gains = side[:3]
    counts = side[3].reshape(dp_size, slab)
    part_count = jnp.sum(counts[:, 0]) * 128.0 + jnp.sum(counts[:, 1])
    part_count = jnp.full((8, 128), part_count, F32)
    valid_count = (part_count + to_peer(part_count))[0, 0]
    half_ff, half_heads = ff_width // 2, heads_width // 2
    places = jnp.stack([near_at, pair]).astype(jnp.int32)

    def fetch_peer(first):
        return to_peer(
            lax.dynamic_slice(
                gath_a, (pair * (width // 2), first * heads_width), (width // 2, heads_width)
            )
        )

    def join_cores(got):
        other = to_core(got)
        return jnp.concatenate(
            [jnp.where(pair == 0, got, other), jnp.where(pair == 0, other, got)], axis=0
        )

    cross_q_own = gath_a[:, 6 * heads_width : 7 * heads_width]
    cross_o_own = gath_a[:, 7 * heads_width : 8 * heads_width]
    cross_q_peer = fetch_peer(6)

    local_rows = x_bf.astype(F32)
    normed_one, _ = norm_stats(local_rows)
    peer_one, _ = norm_stats(x_peer_bf.astype(F32))
    input_one = jnp.concatenate(
        [(normed_one * gains[0]).astype(BF16), (peer_one * gains[0]).astype(BF16)], axis=0
    )
    order = lax.iota(jnp.int32, length)
    positions = jnp.where(order < rows, order + share * rows, order - share * rows)
    cosines, sines = rotary_tables(positions)
    def half_of(values, index):
        half = values.shape[1] // 2
        return lax.dynamic_slice(values, (0, index * half), (values.shape[0], half))

    def other_half(values):
        return to_core(half_of(values, 1 - pair))

    def project(values, weight, weight_dim, *meanwhile):
        away = to_peer(dot(values[rows:], weight, 1, weight_dim).astype(BF16))
        mine = dot(values[:rows], weight, 1, weight_dim)
        return mine + after(away, mine, *meanwhile).astype(F32)

    qkv = dot(input_one, weight_qkv, 1, 0)
    mixed_self, query_self, key_self, value_self, logs_self = self_forward(qkv, cosines, sines)
    cross_q_peer = join_cores(after(cross_q_peer, mixed_self))
    cross_o_peer = fetch_peer(7)
    keyvals_own = dot(cond_rows, cross_kv, 1, 0).astype(BF16)
    keyvals_peer = to_peer(keyvals_own)
    core_one = to_core(input_one)
    hidden_one = local_rows + project(mixed_self, weight_o, 1, core_one, cross_q_peer)

    normed_two, _ = norm_stats(hidden_one)
    own_two = (normed_two * gains[1]).astype(BF16)
    query_cross = tuple(
        dot(own_two, weight, 1, 0).astype(BF16) for weight in (cross_q_own, cross_q_peer)
    )
    keyvals = (keyvals_own, after(keyvals_peer, own_two))
    mixed_cross, logs_cross = cross_forward(query_cross, keyvals, ctx_len)
    cross_o_peer = join_cores(after(cross_o_peer, mixed_cross))
    hidden_two = (
        hidden_one
        + dot(mixed_cross[:, :heads_width], cross_o_own, 1, 1)
        + dot(mixed_cross[:, heads_width:], cross_o_peer, 1, 1)
    )

    normed_three, _ = norm_stats(hidden_two)
    own_three = (normed_three * gains[2]).astype(BF16)
    peer_three = to_peer(own_three)
    core_mixed_self, core_cond = other_half(mixed_self), to_core(cond_rows)
    peer_three = after(peer_three, core_mixed_self, core_cond)
    input_three = jnp.concatenate([own_three, peer_three], axis=0)
    weight_gate = gath_b[:, :ff_width]
    weight_up = gath_b[:, ff_width : 2 * ff_width]
    weight_down = gath_b[:, 2 * ff_width :]
    gate_pre = dot(input_three, weight_gate, 1, 0).astype(BF16)
    up_sum = dot(input_three, weight_up, 1, 0)
    gate_sum = gate_pre.astype(F32)
    hidden_ff = (gate_sum * jax.nn.sigmoid(gate_sum) * up_sum).astype(BF16)
    up_pre = up_sum.astype(BF16)
    core_three, core_hidden = to_core(input_three), other_half(hidden_ff)
    block_out = hidden_two + project(hidden_ff, weight_down, 1, core_three, core_hidden)

    error_diff = block_out - teacher[0].astype(F32)
    local_error = jnp.sum(mask_float[:, None] * error_diff * error_diff)
    token_total = float(dp_size * lax.axis_size("tensor") * rows)
    grad_out = 2.0 * token_total / valid_count * mask_float[:, None] * error_diff

    def grad_of(pieces, *parts):
        return weight_grad(places, far, pieces, parts)

    landed, scattered = [], []

    def launch(sent, *events):
        return to_near(after(sent, *events))

    def land(got, kept, *events):
        got = after(got, *events, *scattered[:-1])
        landed.append((kept.astype(F32) + got.astype(F32)).astype(BF16))
        scattered.append(scatter(landed[-1]))
        return scattered[-1]

    def scatter(summed):
        return lax.psum_scatter(summed, "far", scatter_dimension=0, tiled=True)

    def finish(scattered):
        columns = scattered.shape[1]
        kept = lax.dynamic_slice(scattered, (pair * slab, 0), (slab, columns))
        got = to_core(lax.dynamic_slice(scattered, ((1 - pair) * slab, 0), (slab, columns)))
        first = jnp.where(pair == 0, kept, got).astype(F32)
        second = jnp.where(pair == 0, got, kept).astype(F32)
        return (first, second)

    def columns_at(sides, places, size):
        return jnp.concatenate(
            [side[:, at : at + size] for side in sides for at in places], axis=1
        )

    own_e3 = grad_out.astype(BF16)
    peer_e3 = to_peer(own_e3)
    core_own_e3 = to_core(own_e3)

    def row(index):
        return gains[index : index + 1]

    dgate_own, dup_own, halves_own = feed_back(places, own_e3, gath_b, gate_pre, up_pre, 0)
    core_own_halves = to_core(halves_own)
    pulled_own = pull(dgate_own, dup_own, gath_b, F32)
    peer_e3 = after(peer_e3, pulled_own)
    core_peer_e3 = to_core(peer_e3)
    peer_two = to_peer(after(own_two, peer_e3))
    peer_mixed = to_peer(after(mixed_cross, peer_e3)[:, heads_width:])
    dgate_peer, dup_peer, halves_peer = feed_back(places, peer_e3, gath_b, gate_pre, up_pre, 1)
    kept_down, sent_down = grad_of(
        DOWN_PIECES,
        (own_e3, (hidden_ff, 0), None),
        (after(peer_e3, dgate_peer), (hidden_ff, 1), None),
        (core_own_e3, (core_hidden, 0), 0),
        (core_peer_e3, (core_hidden, 1), 0),
    )
    near_down = launch(sent_down[0])
    dgate_peer, dup_peer, _ = lax.optimization_barrier((dgate_peer, dup_peer, sent_down[0]))
    core_peer_halves = to_core(halves_peer)
    pulled_peer, peer_two, peer_mixed = lax.optimization_barrier(
        (pull(dgate_peer, dup_peer, gath_b, BF16), peer_two, peer_mixed)
    )
    away = to_peer(pulled_peer)

    def feed_grad(pieces, own, peer, at, *earlier):
        return grad_of(
            pieces,
            (own_three, after(own, *earlier), None),
            (peer_three, peer, None),
            ((core_three, 0), core_own_halves, at),
            ((core_three, 1), core_peer_halves, at),
        )

    kept_gate, sent_gate = feed_grad(GATE_PIECES, dgate_own, dgate_peer, 0, pulled_peer)
    scat_down = [land(near_down, kept_down[0], sent_gate[0])]
    near_down = launch(sent_down[1], landed[-1])
    kept_up, sent_up = feed_grad(UP_PIECES, dup_own, dup_peer, 1, sent_gate[0])
    scat_down.append(land(near_down, kept_down[1], sent_up[0]))
    near_gate = launch(sent_gate[0], landed[-1])
    grad_two, own_e2, gain_three = norm_back(
        pulled_own, after(away, landed[-1]), hidden_two, row(2), grad_out
    )

    grad_mixed = tuple(
        dot(own_e2, weight, 1, 0).astype(BF16) for weight in (cross_o_own, cross_o_peer)
    )
    grad_qc, grad_kv = cross_back(query_cross, grad_mixed, keyvals, logs_cross, ctx_len)
    pulled_two = dot(grad_qc[:, :heads_width], cross_q_own, 1, 1) + dot(
        grad_qc[:, heads_width:], cross_q_peer, 1, 1
    )
    grad_one, own_e1, gain_two = norm_back(pulled_two, None, hidden_one, row(1), grad_two)

    peer_e1 = to_peer(own_e1)
    scat_gate = [land(near_gate, kept_gate[0], own_e1)]
    near_mid = launch(jnp.concatenate([sent_gate[1], sent_up[0]], axis=1), landed[-1])
    mid = land(near_mid, jnp.concatenate([kept_gate[1], kept_up[0]], axis=1), peer_e1)
    peer_e1 = after(peer_e1, landed[-1])
    near_up = launch(jnp.concatenate([sent_up[1], sent_down[2]], axis=1), landed[-1])
    peer_e2, peer_qc = to_peer(after(own_e2, peer_e1)), to_peer(after(grad_qc, peer_e1)[:, heads_width:])
    peer_kv = to_peer(after(grad_kv, peer_e1)[:, 2 * heads_width :])
    grad_qkv, halves_qkv, pulled_own, pulled_peer = self_back(
        places,
        query_self,
        key_self,
        value_self,
        own_e1,
        peer_e1,
        gath_a,
        logs_self,
        cosines,
        sines,
    )
    peer_e2, peer_qc, peer_kv, pulled_peer, grad_qkv = lax.optimization_barrier(
        (peer_e2, peer_qc, peer_kv, pulled_peer, grad_qkv)
    )
    away = to_peer(pulled_peer)
    core_qkv = to_core(halves_qkv)
    last_ff = land(near_up, jnp.concatenate([kept_up[1], kept_down[2]], axis=1), pulled_peer)
    kept_qkv, sent_qkv = grad_of(
        (3 * half_heads,),
        (input_one, after(grad_qkv, landed[-1]), None),
        (core_one, core_qkv, 0),
    )
    near_qkv = launch(sent_qkv[0])
    branch_one = jnp.concatenate([own_e1, peer_e1], axis=0)
    branch_two = jnp.concatenate([own_e2, peer_e2], axis=0)
    input_two = jnp.concatenate([own_two, peer_two], axis=0)
    mixed_two = jnp.concatenate([mixed_cross[:, :heads_width], peer_mixed], axis=0)
    both_qc = jnp.concatenate([grad_qc[:, :heads_width], peer_qc], axis=0)
    sum_kv = (grad_kv[:, : 2 * heads_width].astype(F32) + peer_kv.astype(F32)).astype(BF16)
    kept_wo, sent_wo = grad_of(
        (half_heads,),
        (branch_one, after(mixed_self, sent_qkv[0]), None),
        (to_core(after(branch_one, grad_qkv)), core_mixed_self, 0),
    )
    kept_co, sent_co = grad_of(
        (half_heads,),
        (branch_two, after(mixed_two, sent_wo[0]), None),
        (to_core(after(branch_two, sent_qkv[0])), other_half(mixed_two), 0),
    )
    kept_cq, sent_cq = grad_of(
        (half_heads,),
        (input_two, after(both_qc, sent_co[0]), None),
        (to_core(after(input_two, sent_wo[0])), other_half(both_qc), 0),
    )
    kept_ckv, sent_ckv = grad_of(
        (heads_width,),
        (cond_rows, after(sum_kv, sent_cq[0]), None),
        (core_cond, other_half(sum_kv), 0),
    )
    near_w = launch(jnp.concatenate(sent_wo + sent_co, axis=1))
    near_c = launch(jnp.concatenate(sent_cq + sent_ckv, axis=1))
    scat_qkv = land(near_qkv, kept_qkv[0], sent_ckv[0])
    grad_rows, _, gain_one = norm_back(
        pulled_own, after(away, landed[-1]), x_bf, row(0), grad_one
    )
    scat_w = land(near_w, jnp.concatenate(kept_wo + kept_co, axis=1), grad_rows)
    cond_part = dot(after(sum_kv, landed[-1]), cross_kv, 1, 1)[:ctx_len].astype(BF16)
    cond_sum = cond_part.astype(F32) + to_peer(cond_part).astype(F32)
    scat_c = land(near_c, jnp.concatenate(kept_cq + kept_ckv, axis=1), cond_part)

    small = jnp.concatenate(
        [gain_one, gain_two, gain_three, jnp.full((1, width), local_error, F32)],
        axis=0,
    )
    small = after(small, landed[-1])
    for axis in ("tensor", "core", "near", "far"):
        size = lax.axis_size(axis)
        if size & (size - 1):
            small = lax.psum(small, axis)
            continue
        hop = 1
        while hop < size:
            small = small + lax.ppermute(small, axis, [(i, i ^ hop) for i in range(size)])
            hop *= 2
    mean_loss = small[3, 0] / (width * valid_count)
    place = (lax.axis_index("far") * 4 + near_at * 2 + pair) * slab
    grad_gains = lax.dynamic_slice(small, (0, place), (3, slab))

    split = GATE_PIECES[1]
    gate_parts = scat_gate + [mid[:, :split]]
    up_parts = [mid[:, split:], last_ff[:, : UP_PIECES[1]]]
    down_parts = scat_down + [last_ff[:, UP_PIECES[1] :]]
    down_t, gate_s, up_s = (
        jnp.concatenate(finish(jnp.concatenate(parts, axis=1)), axis=1)
        for parts in (down_parts, gate_parts, up_parts)
    )
    sides = finish(scat_qkv)
    q_s, k_s, v_s = (
        columns_at(sides, range(i * PAIR, 3 * half_heads, 3 * PAIR), PAIR) for i in range(3)
    )
    sides = finish(scat_w)
    out_t, co_t = (columns_at(sides, [i * half_heads], half_heads) for i in range(2))
    sides = finish(scat_c)
    cq_s = columns_at(sides, [0], half_heads)
    ck_s, cv_s = (
        columns_at(sides, range(half_heads + i * PAIR, 3 * half_heads, 2 * PAIR), PAIR)
        for i in range(2)
    )
    return (
        block_out.astype(BF16)[None],
        mean_loss,
        grad_rows[None],
        cond_sum[None],
        q_s,
        k_s,
        v_s,
        out_t.T,
        cq_s,
        ck_s,
        cv_s,
        co_t.T,
        gate_s,
        up_s,
        down_t.T,
        grad_gains,
    )


def solution(mesh):
    dp_size, share = mesh.shape["dp"], mesh.shape["tensor"]
    fine = Mesh(
        mesh.devices.reshape(dp_size // 4, 2, 2, share), ("far", "near", "core", "tensor")
    )
    dp = ("far", "near", "core")
    tokens = P(dp, "tensor", None)
    per_latent = P(dp, None, None)
    by_row = P(dp, "tensor")
    by_column = P("tensor", dp)
    weights = (by_row,) * 3 + (by_column,) + (by_row,) * 3 + (by_column, by_row, by_row, by_column)
    return jax.shard_map(
        body,
        mesh=fine,
        in_specs=(tokens, per_latent, tokens, by_row, P(None, dp)) + weights,
        out_specs=(tokens, P(), tokens, per_latent) + weights + (P(None, dp),),
        check_vma=False,
    )
```

time: 1100 us -> 809 us (0.74)
  matrix products: 313 us -> 80.6 us
  Pallas kernels: 0 us -> 213 us
  waiting for transfers between devices: 506 us -> 295 us
  blocking collectives: 41 us -> 0 us
  other arithmetic: 89.9 us -> 68.1 us
  starting transfers between devices: 27 us -> 44.6 us
  local copies, waits for them, and re-layouts: 92.7 us -> 78.9 us
    pallas_call x0 -> x21, Pallas kernels: none -> 213 us  [the longest x8 72.1 us: weight_grad(): pl.pallas_call(functools.partial(weight_grad_kernel, len(parts), pieces,...]
    dot_general x47 -> x17, matrix products: 231 us -> 80.6 us  [dot(): lax.dot_general(left, right, (((left_dim,), (right_dim,)), ((), ())), pre...]
    unnamed x11 -> x10, waiting for transfers between devices: 143 us -> 0.16 us
    ppermute x14 -> x18, waiting for transfers between devices: 258 us -> 147 us  [to_peer(): return lax.ppermute(values, 'tensor', swap)]
    dot_general x12 -> x0, matrix products: 82.3 us -> none  [the longest x2 23.7 us: attend_back(): jnp.einsum('qhd,khd->hqk', grad_mixed, values_in, preferred_element_type=...]
    ppermute x0 -> x13, waiting for transfers between devices: none -> 51.6 us  [the longest x8 45.2 us: to_near(): return lax.ppermute(values, 'near', swap)]
    psum x1 -> x0, blocking collectives: 41 us -> none  [body(): small = lax.psum(small, ('ring', 'core', 'tensor'))]
    all_gather x4 -> x2, waiting for transfers between devices: 96.9 us -> 73.7 us  [gather(): return lax.all_gather(values, dp_axes, axis=0, tiled=True)]
  transfers between devices with their start and end apart: 44 -> 65, of which waited for: 19 -> 25; matrix products, arithmetic and copies ran while one was open for 36% -> 21% of each run, Pallas kernels for 0% -> 26%
where the time goes in v2:
time: 809 us; the launch traced here: 801 us
  waiting for transfers between devices  295 us (36%)
  Pallas kernels  213 us (26%)
  matrix products  80.6 us (10%)
  local copies, waits for them, and re-layouts  78.9 us (10%)
  other arithmetic  68.1 us (8%)
  starting transfers between devices  44.6 us (6%)
  between operations  21.1 us (3%)
    ppermute x18, waiting for transfers between devices, to_peer(): return lax.ppermute(values, 'tensor', swap)  147 us
    dot_general x17, matrix products, dot(): lax.dot_general(left, right, (((left_dim,), (right_dim,)), ((), ())), pre...  80.6 us
    all_gather x2, waiting for transfers between devices, gather(): return lax.all_gather(values, dp_axes, axis=0, tiled=True)  73.7 us
    pallas_call x8, Pallas kernels, weight_grad(): pl.pallas_call(functools.partial(weight_grad_kernel, len(parts), pieces,...  72.1 us
    unnamed x301, local copies, waits for them, and re-layouts  52.4 us
    ppermute x8, waiting for transfers between devices, to_near(): return lax.ppermute(values, 'near', swap)  45.2 us
    pallas_call x1, Pallas kernels, self_back(): pl.pallas_call(self_back_kernel, grid_spec=pltpu.PrefetchScalarGridSpec(n...  42.6 us
    pallas_call x2, Pallas kernels, pull(): pl.pallas_call(pull_kernel, grid=(depth // PULL_ROWS,), in_specs=[whole,...  24.5 us
  transfers between devices with their start and end apart: 65, of which 25 were waited for; matrix products, arithmetic and copies ran while one was open for 21% of the time, Pallas kernels for 26%

profile of v2, /device:TPU:0, one launch (start us, length us, event | category | flops | bytes accessed | tf_op | source)
XLA Modules:
  0.0 801.5 jit_solution(16091899580152392806)
XLA Ops:
  12.0 2.7 shard_map.279
  16.0 3.1 shard_map.282
  19.1 3.0 collective-permute-start
  25.9 22.2 %collective-permute-done = bf16[384,1536]{1,0:T(8,128)(2,1)S(1)} collective-permute-done((bf16[384,1536]{1,0:T(8,128)(2,1)S(1)}, bf16[384,1536]{1,0:T(8,128)(2,1)S(1)}, u32[]{:S(2)}, u32[]{:S(2)}) %collective-permute-start) | collective-permute-done | bytes 1179680 | tf_op jit(solution)/shard_map/ppermute | solution.py:561
  48.8 69.6 %all-gather.3.cloned.1.call-done.out_w.qkv_w = bf16[1536,6272]{1,0:T(8,128)(2,1)} async-done(((bf16[96,6272]{1,0:T(8,128)(2,1)}), bf16[1536,6272]{1,0:T(8,128)(2,1)}) %all-gather.3.cloned.1.call-update) | async-done | bytes 19267600 | tf_op jit(solution)/shard_map/all_gather | solution.py:570
  122.1 3.3 constant_dynamic-slice_fusion.8
  127.0 8.1 %fusion.13.qkv = f32[768,2304]{1,0:T(8,128)S(1)} fusion(bf16[1536,6272]{1,0:T(8,128)(2,1)} %all-gather.3.cloned.1.call-done.out_w.qkv_w, bf16[384,1536]{1,0:T(8,128)(2,1)S(1)} %get-tuple-element.337, bf16[384,1536]{1,0:T(8,128)(2,1)S(1)} %get-tuple-element.336), kind=kOutput, calls=%fused_computation.15 | convolution fusion | flops 5440536576 | bytes 16515072 | tf_op jit(solution)/shard_map/dot_general | solution.py:31
  135.1 14.7 %shard_map.280 = (bf16[768,768]{1,0:T(8,128)(2,1)S(1)}, bf16[768,768]{1,0:T(8,128)(2,1)S(1)}, bf16[768,768]{1,0:T(8,128)(2,1)S(1)}, bf16[768,768]{1,0:T(8,128)(2,1)S(1)}, f32[6,2,768]{2,1,0:T(2,128)S(1)}) custom-call(f32[768,2304]{1,0:T(8,128)S(1)} %fusion.13.qkv, f32[768,128]{1,0:T(8,128)S(1)} %copy-done.26, f32[768,128]{1,0:T(8,128)S(1)} %copy-done.28), custom_call_target="tpu_custom_call" | custom-call | flops 1048576 | bytes 16384 | tf_op jit(solution)/shard_map/pallas_call | solution.py:186
  149.8 3.9 collective-permute-done.3
  153.7 3.8 convolution_convert_fusion
  159.2 3.5 fusion.29.kv_own
  164.8 2.8 fusion.49
  169.4 17.3 %collective-permute-done.1 = bf16[384,1536]{1,0:T(8,128)(2,1)} collective-permute-done((bf16[384,1536]{1,0:T(8,128)(2,1)}, bf16[384,1536]{1,0:T(8,128)(2,1)}, u32[]{:S(2)}, u32[]{:S(2)}) %collective-permute-start.1) | collective-permute-done | bytes 1179680 | tf_op jit(solution)/shard_map/ppermute | solution.py:561
  189.7 6.5 collective-permute-done.5.kv_peer
  197.2 3.0 fusion.53.q_own
  200.3 9.7 %shard_map.281 = (bf16[384,1536]{1,0:T(8,128)(2,1)S(1)}, f32[12,2,384]{2,1,0:T(2,128)S(1)}) custom-call(bf16[384,768]{1,0:T(8,128)(2,1)S(1)} %fusion.53.q_own, bf16[384,768]{1,0:T(8,128)(2,1)S(1)} %convolution_convert_fusion.1.q_peer, bf16[144,1536]{1,0:T(8,128)(2,1)S(1)} %fusion.29.kv_own, bf16[144,1536]{1,0:T(8,128)(2,1)S(1)} %collective-permute-done.5.kv_peer), custom_call_target="tpu_custom_call" | custom-call | flops 1048576 | bytes 16384 | tf_op jit(solution)/shard_map/pallas_call | solution.py:270
  210.0 11.1 %collective-permute-done.6 = bf16[768,768]{1,0:T(8,128)(2,1)S(1)} collective-permute-done((bf16[768,768]{1,0:T(8,128)(2,1)S(1)}, bf16[768,768]{1,0:T(8,128)(2,1)S(1)}, u32[]{:S(2)}, u32[]{:S(2)}) %collective-permute-start.6) | collective-permute-done | bytes 1179680 | tf_op jit(solution)/shard_map/ppermute | solution.py:561
  221.0 2.8 convolution_add_fusion.2
  237.6 18.7 %collective-permute-done.14 = f32[8,128]{1,0:T(8,128)} collective-permute-done((f32[8,128]{1,0:T(8,128)}, f32[8,128]{1,0:T(8,128)}, u32[]{:S(2)}, u32[]{:S(2)}) %collective-permute-start.14) | collective-permute-done | bytes 4128 | tf_op jit(solution)/shard_map/ppermute | solution.py:561
  258.3 3.2 pad_maximum_fusion.3
  261.5 4.1 all-gather.5.cloned.1.call-done.weights
  265.6 10.7 %fusion.15.gate_in = bf16[768,3072]{1,0:T(8,128)(2,1)S(1)} fusion(bf16[1536,9216]{1,0:T(8,128)(2,1)} %all-gather.5.cloned.1.call-done.weights, bf16[384,1536]{1,0:T(8,128)(2,1)} %collective-permute-done.8.refs_2_, bf16[384,1536]{1,0:T(8,128)(2,1)} %multiply_convert_fusion.refs_0_), kind=kOutput, calls=%fused_computation.17 | convolution fusion | flops 7254835200 | bytes 16515072 | tf_op jit(solution)/shard_map/dot_general | solution.py:31
  276.4 14.6 %fusion.79 = (bf16[768,3072]{1,0:T(8,128)(2,1)}, bf16[768,3072]{1,0:T(8,128)(2,1)S(1)}) fusion(bf16[768,3072]{1,0:T(8,128)(2,1)S(1)} %fusion.15.gate_in, bf16[1536,9216]{1,0:T(8,128)(2,1)} %all-gather.5.cloned.1.call-done.weights, bf16[384,1536]{1,0:T(8,128)(2,1)} %collective-permute-done.8.refs_2_, bf16[384,1536]{1,0:T(8,128)(2,1)} %multiply_convert_fusion.refs_0_), kind=kOutput, calls=%fused_computation.216 | convolution fusion | flops 7271350272 | bytes 25952256 | tf_op jit(solution)/shard_map/dot_general | solution.py:31
  291.5 9.7 %fusion.26 = bf16[384,1536]{1,0:T(8,128)(2,1)} fusion(bf16[1536,9216]{1,0:T(8,128)(2,1)} %all-gather.5.cloned.1.call-done.weights, bf16[768,3072]{1,0:T(8,128)(2,1)S(1)} %get-tuple-element.281.refs_1_.refs_3_), kind=kOutput, calls=%fused_computation.39 | convolution fusion | flops 3624468480 | bytes 12976128 | tf_op jit(solution)/shard_map/dot_general | solution.py:31
  302.7 6.8 fusion.11
  309.5 20.0 %collective-permute-done.11 = bf16[384,1536]{1,0:T(8,128)(2,1)S(1)} collective-permute-done((bf16[384,1536]{1,0:T(8,128)(2,1)}, bf16[384,1536]{1,0:T(8,128)(2,1)S(1)}, u32[]{:S(2)}, u32[]{:S(2)}) %collective-permute-start.11) | collective-permute-done | bytes 1179680 | tf_op jit(solution)/shard_map/ppermute | solution.py:561
  331.2 2.5 fusion.76
  335.3 11.9 %shard_map.283 = (bf16[384,3072]{1,0:T(8,128)(2,1)S(1)}, bf16[384,3072]{1,0:T(8,128)(2,1)S(1)}, bf16[2,384,1536]{2,1,0:T(8,128)(2,1)}) custom-call(s32[2]{0:T(128)S(1)} %pad_add_fusion.places, bf16[384,1536]{1,0:T(8,128)(2,1)} %get-tuple-element.274.g_in.refs_0_, bf16[1536,9216]{1,0:T(8,128)(2,1)} %all-gather.5.cloned.1.call-done.weights, ...), custom_call_target="tpu_custom_call" | custom-call | flops 1048576 | bytes 16384 | tf_op jit(solution)/shard_map/pallas_call | solution.py:376
  347.8 12.8 %shard_map.284.refs_0_ = f32[384,1536]{1,0:T(8,128)S(1)} custom-call(bf16[384,3072]{1,0:T(8,128)(2,1)S(1)} %get-tuple-element.143.gate_in.refs_1_, bf16[384,3072]{1,0:T(8,128)(2,1)S(1)} %get-tuple-element.149.up_in.refs_1_, bf16[1536,9216]{1,0:T(8,128)(2,1)} %all-gather.5.cloned.1.call-done.weights), custom_call_target="tpu_custom_call" | custom-call | flops 1048576 | bytes 16384 | tf_op jit(solution)/shard_map/pallas_call | solution.py:483
  362.6 11.9 %shard_map.285 = (bf16[384,3072]{1,0:T(8,128)(2,1)S(1)}, bf16[384,3072]{1,0:T(8,128)(2,1)S(1)}, bf16[2,384,1536]{2,1,0:T(8,128)(2,1)}) custom-call(s32[2]{0:T(128)S(1)} %pad_add_fusion.places, bf16[384,1536]{1,0:T(8,128)(2,1)} %collective-permute-done.15.g_in.refs_2_, bf16[1536,9216]{1,0:T(8,128)(2,1)} %all-gather.5.cloned.1.call-done.weights, ...), custom_call_target="tpu_custom_call" | custom-call | flops 1048576 | bytes 16384 | tf_op jit(solution)/shard_map/pallas_call | solution.py:376
  382.1 13.1 %shard_map.286 = (bf16[768,768]{1,0:T(8,128)(2,1)S(1)}, bf16[768,512]{1,0:T(8,128)(2,1)S(1)}, bf16[768,256]{1,0:T(8,128)(2,1)S(1)}, bf16[768,768]{1,0:T(8,128)(2...) custom-call(s32[2]{0:T(128)S(1)} %pad_add_fusion.places, ...), custom_call_target="tpu_custom_call" | custom-call | flops 1048576 | bytes 16384 | tf_op jit(solution)/shard_map/pallas_call | solution.py:456
  400.3 11.7 %shard_map.287 = bf16[384,1536]{1,0:T(8,128)(2,1)S(1)} custom-call(bf16[384,3072]{1,0:T(8,128)(2,1)S(1)} %copy-done.15, bf16[384,3072]{1,0:T(8,128)(2,1)S(1)} %copy-done.10, bf16[1536,9216]{1,0:T(8,128)(2,1)} %all-gather.5.cloned.1.call-done.weights), custom_call_target="tpu_custom_call" | custom-call | flops 1048576 | bytes 16384 | tf_op jit(solution)/shard_map/pallas_call | solution.py:483
  413.1 5.4 collective-permute-done.19
  419.8 13.6 %shard_map.288 = (bf16[768,1024]{1,0:T(8,128)(2,1)S(1)}, bf16[768,512]{1,0:T(8,128)(2,1)S(1)}, bf16[768,1024]{1,0:T(8,128)(2,1)S(1)}, bf16[768,512]{1,0:T(8,128)(2,1)S(1)}) custom-call(s32[2]{0:T(128)S(1)} %pad_add_fusion.places, bf16[384,1536]{1,0:T(8,128)(2,1)} %multiply_convert_fusion.refs_0_, bf16[384,3072]{1,0:T(8,128)(2,1)S(1)} %copy-done.13, ...), custom_call_target="tpu_custom_call" | custom-call | flops 1048576 | bytes 16384 | tf_op jit(solution)/shard_map/pallas_call | solution.py:456
  446.6 13.4 %shard_map.289 = (bf16[768,256]{1,0:T(8,128)(2,1)S(1)}, bf16[768,1280]{1,0:T(8,128)(2,1)S(1)}, bf16[768,256]{1,0:T(8,128)(2,1)S(1)}, bf16[768,1280]{1,0:T(8,128)(2,1)S(1)}) custom-call(s32[2]{0:T(128)S(1)} %pad_add_fusion.places, bf16[384,1536]{1,0:T(8,128)(2,1)} %multiply_convert_fusion.refs_0_, bf16[384,3072]{1,0:T(8,128)(2,1)S(1)} %copy-done.6, ...), custom_call_target="tpu_custom_call" | custom-call | flops 1048576 | bytes 16384 | tf_op jit(solution)/shard_map/pallas_call | solution.py:456
  465.2 3.3 collective-permute-done.20.refs_1_
  474.2 3.5 shard_map.290
  478.9 2.9 fusion.56.g_own
  481.8 11.5 %shard_map.291 = (bf16[384,1536]{1,0:T(8,128)(2,1)S(1)}, bf16[144,3072]{1,0:T(8,128)(2,1)S(1)}) custom-call(bf16[384,768]{1,0:T(8,128)(2,1)S(1)} %copy-done.46, bf16[384,768]{1,0:T(8,128)(2,1)S(1)} %copy-done.44, bf16[384,768]{1,0:T(8,128)(2,1)S(1)} %fusion.56.g_own, bf16[384,768]{1,0:T(8,128)(2,1)S(1)} %fusion.59.g_peer, bf16[144,1536]{1,0:T(8,128)(2,1)S(1)} %copy-done.52, ...), custom_call_target="tpu_custom_call" | custom-call | flops 1048576 | bytes 16384 | tf_op jit(solution)/shard_map/pallas_call | solution.py:270
  494.3 3.2 fusion.44
  503.7 3.8 add_convert_fusion.3
  509.9 2.6 pad_maximum_fusion.4
  512.5 23.0 %collective-permute-done.25.peer_in = bf16[384,1536]{1,0:T(8,128)(2,1)S(1)} collective-permute-done((bf16[384,1536]{1,0:T(8,128)(2,1)S(1)}, bf16[384,1536]{1,0:T(8,128)(2,1)S(1)}, u32[]{:S(2)}, u32[]{:S(2)}) %collective-permute-start.25) | collective-permute-done | bytes 1179680 | tf_op jit(solution)/shard_map/ppermute | solution.py:561
  535.9 2.9 add_convert_fusion.5
  547.0 42.6 %shard_map.293 = (bf16[768,2304]{1,0:T(8,128)(2,1)}, bf16[768,1152]{1,0:T(8,128)(2,1)}, f32[384,1536]{1,0:T(8,128)}, bf16[384,1536]{1,0:T(8,128)(2,1)S(1)}) custom-call(s32[2]{0:T(128)S(1)} %pad_add_fusion.places, bf16[768,768]{1,0:T(8,128)(2,1)S(1)} %copy-done.57, bf16[768,768]{1,0:T(8,128)(2,1)S(1)} %copy-done.59, bf16[768,768]{1,0:T(8,128)(2,1)S(1)} %copy-done.61, ...), custom_call_target="tpu_custom_call" | custom-call | flops 1048576 | bytes 16384 | tf_op jit(solution)/shard_map/pallas_call | solution.py:220
  592.3 4.3 add_convert_fusion
  600.0 2.5 constant_dynamic-update-slice_fusion.refs_0_
  602.5 10.5 %shard_map.294 = (bf16[768,1152]{1,0:T(8,128)(2,1)S(1)}, bf16[768,1152]{1,0:T(8,128)(2,1)}) custom-call(s32[2]{0:T(128)S(1)} %pad_add_fusion.places, bf16[768,1536]{1,0:T(8,128)(2,1)S(1)} %copy-done.20, bf16[768,2304]{1,0:T(8,128)(2,1)S(1)} %copy-done.30, bf16[768,1536]{1,0:T(8,128)(2,1)} %collective-permute-done.2.refs_2_, ...), custom_call_target="tpu_custom_call" | custom-call | flops 1048576 | bytes 16384 | tf_op jit(solution)/shard_map/pallas_call | solution.py:456
  613.1 6.0 shard_map.295
  628.3 5.8 shard_map.296
  634.1 5.5 shard_map.297
  641.3 4.3 shard_map.298
  646.6 15.4 %collective-permute-done.34 = bf16[768,1152]{1,0:T(8,128)(2,1)} collective-permute-done((bf16[768,1152]{1,0:T(8,128)(2,1)}, bf16[768,1152]{1,0:T(8,128)(2,1)}, u32[]{:S(2)}, u32[]{:S(2)}) %collective-permute-start.34) | collective-permute-done | bytes 1769504 | tf_op jit(solution)/shard_map/ppermute | solution.py:567
  662.0 3.7 add_convert_fusion.2
  677.6 15.5 %collective-permute-done.31.refs_1_ = bf16[384,1536]{1,0:T(8,128)(2,1)S(1)} collective-permute-done((bf16[384,1536]{1,0:T(8,128)(2,1)}, bf16[384,1536]{1,0:T(8,128)(2,1)S(1)}, u32[]{:S(2)}, u32[]{:S(2)}) %collective-permute-start.31) | collective-permute-done | bytes 1179680 | tf_op jit(solution)/shard_map/ppermute | solution.py:561
  695.8 3.4 shard_map.299
  699.2 3.6 collective-permute-done.42
  702.9 2.6 add_convert_fusion.4
  705.5 4.1 fusion.18
  714.7 25.8 %collective-permute-done.41 = bf16[768,1152]{1,0:T(8,128)(2,1)} collective-permute-done((bf16[768,1152]{1,0:T(8,128)(2,1)}, bf16[768,1152]{1,0:T(8,128)(2,1)}, u32[]{:S(2)}, u32[]{:S(2)}) %collective-permute-start.41) | collective-permute-done | bytes 1769504 | tf_op jit(solution)/shard_map/ppermute | solution.py:567
  740.4 3.2 add_convert_fusion.1
  756.9 2.6 collective-permute-start.47
  759.6 4.1 collective-permute-done.47
  768.2 19.6 %reduce-scatter.23.cloned.1.call-done = bf16[192,1152]{1,0:T(8,128)(2,1)} async-done(((bf16[768,1152]{1,0:T(8,128)(2,1)}), bf16[192,1152]{1,0:T(8,128)(2,1)}) %reduce-scatter.23.cloned.1.call-update) | async-done | bytes 442384 | tf_op jit(solution)/shard_map/reduce_scatter | solution.py:711
  (527 shorter events, 163.5 us)
Async XLA Ops:
  7.2 111.2 %all-gather.3.cloned.1.call-start = ((), (), s32[]{:S(2)}) async-start(), calls=%async_computation.8 | async-start | bytes 20471808 | tf_op jit(solution)/shard_map/all_gather | solution.py:570
  14.7 250.9 %all-gather.5.cloned.1.call-start = ((), (), s32[]{:S(2)}) async-start(), calls=%async_computation.9 | async-start | bytes 30081024 | tf_op jit(solution)/shard_map/all_gather | solution.py:570
  19.0 484.7 %reduce-scatter.9.cloned.1.call-start = ((), (), s32[]{:S(2)}) async-start(), calls=%async_computation.10 | async-start | bytes 1474560 | tf_op jit(solution)/shard_map/reduce_scatter | solution.py:711
  19.1 29.0 %collective-permute-start = (bf16[384,1536]{1,0:T(8,128)(2,1)S(1)}, bf16[384,1536]{1,0:T(8,128)(2,1)S(1)}, u32[]{:S(2)}, u32[]{:S(2)}) collective-permute-start(bf16[384,1536]{1,0:T(8,128)(2,1)S(1)} %bitcast.34), channel_id=1, source_target_pairs={{0,1},{1,0},{2,3},{3,2},{4,5},{5,4},{6,7},{7,6},{8,9},{9,8},{10,11... | collective-permute-start | bytes 3538952 | tf_op jit(solution)/shard_map/ppermute | solution.py:561
  121.8 65.0 %collective-permute-start.2 = (bf16[768,1536]{1,0:T(8,128)(2,1)S(1)}, bf16[768,1536]{1,0:T(8,128)(2,1)}, u32[]{:S(2)}, u32[]{:S(2)}) collective-permute-start(bf16[768,1536]{1,0:T(8,128)(2,1)S(1)} %pad_maximum_fusion.refs_0_), channel_id=1, source_target_pairs={{0,2},{2,0},{1,3},{3,1},{4,6},{6,4},{5,7},{7,5},{8,10},{10,8},{9,1... | collective-permute-start | bytes 7077896 | tf_op jit(solution)/shard_map/ppermute | solution.py:564
  125.4 28.3 %collective-permute-start.3 = (bf16[768,768]{1,0:T(8,128)(2,1)S(1)}, bf16[768,768]{1,0:T(8,128)(2,1)}, u32[]{:S(2)}, u32[]{:S(2)}) collective-permute-start(bf16[768,768]{1,0:T(8,128)(2,1)S(1)} %get-tuple-element.279), channel_id=1, source_target_pairs={{0,1},{1,0},{2,3},{3,2},{4,5},{5,4},{6,7},{7,6},{8,9},{9,8},{10,11... | collective-permute-start | bytes 3538952 | tf_op jit(solution)/shard_map/ppermute | solution.py:561
  153.7 13.8 %collective-permute-start.4 = (bf16[768,768]{1,0:T(8,128)(2,1)}, bf16[768,768]{1,0:T(8,128)(2,1)}, u32[]{:S(2)}, u32[]{:S(2)}) collective-permute-start(bf16[768,768]{1,0:T(8,128)(2,1)} %collective-permute-done.3), channel_id=1, source_target_pairs={{0,2},{2,0},{1,3},{3,1},{4,6},{6,4},{5,7},{7,5},{8,10},{10,8},{9,1... | collective-permute-start | bytes 3538952 | tf_op jit(solution)/shard_map/ppermute | solution.py:564
  157.6 29.1 %collective-permute-start.1 = (bf16[384,1536]{1,0:T(8,128)(2,1)}, bf16[384,1536]{1,0:T(8,128)(2,1)}, u32[]{:S(2)}, u32[]{:S(2)}) collective-permute-start(bf16[384,1536]{1,0:T(8,128)(2,1)} %convolution_convert_fusion), channel_id=1, source_target_pairs={{0,1},{1,0},{2,3},{3,2},{4,5},{5,4},{6,7},{7,6},{8,9},{9,8},{10,11... | collective-permute-start | bytes 3538952 | tf_op jit(solution)/shard_map/ppermute | solution.py:561
  162.7 33.4 %collective-permute-start.5 = (bf16[144,1536]{1,0:T(8,128)(2,1)S(1)}, bf16[144,1536]{1,0:T(8,128)(2,1)S(1)}, u32[]{:S(2)}, u32[]{:S(2)}) collective-permute-start(bf16[144,1536]{1,0:T(8,128)(2,1)S(1)} %fusion.29.kv_own), channel_id=1, source_target_pairs={{0,1},{1,0},{2,3},{3,2},{4,5},{5,4},{6,7},{7,6},{8,9},{9,8},{10,11... | collective-permute-start | bytes 1327112 | tf_op jit(solution)/shard_map/ppermute | solution.py:561
  163.3 57.7 %collective-permute-start.6 = (bf16[768,768]{1,0:T(8,128)(2,1)S(1)}, bf16[768,768]{1,0:T(8,128)(2,1)S(1)}, u32[]{:S(2)}, u32[]{:S(2)}) collective-permute-start(bf16[768,768]{1,0:T(8,128)(2,1)S(1)} %copy-done.121), channel_id=1, source_target_pairs={{0,1},{1,0},{2,3},{3,2},{4,5},{5,4},{6,7},{7,6},{8,9},{9,8},{10,11... | collective-permute-start | bytes 3538952 | tf_op jit(solution)/shard_map/ppermute | solution.py:561
  221.0 2.9 collective-permute-start.7
  227.6 30.7 %collective-permute-start.8 = (bf16[384,1536]{1,0:T(8,128)(2,1)}, bf16[384,1536]{1,0:T(8,128)(2,1)}, u32[]{:S(2)}, u32[]{:S(2)}) collective-permute-start(bf16[384,1536]{1,0:T(8,128)(2,1)} %multiply_convert_fusion.refs_0_), channel_id=1, source_target_pairs={{0,1},{1,0},{2,3},{3,2},{4,5},{5,4},{6,7},{7,6},{8,9},{9,8},{10,11... | collective-permute-start | bytes 3538952 | tf_op jit(solution)/shard_map/ppermute | solution.py:561
  229.9 28.4 %collective-permute-start.10 = (bf16[144,1536]{1,0:T(8,128)(2,1)}, bf16[144,1536]{1,0:T(8,128)(2,1)}, u32[]{:S(2)}, u32[]{:S(2)}) collective-permute-start(bf16[144,1536]{1,0:T(8,128)(2,1)} %pad.9.refs_0_), channel_id=1, source_target_pairs={{0,2},{2,0},{1,3},{3,1},{4,6},{6,4},{5,7},{7,5},{8,10},{10,8},{9,1... | collective-permute-start | bytes 1327112 | tf_op jit(solution)/shard_map/ppermute | solution.py:564
  232.0 26.2 %collective-permute-start.9 = (bf16[768,384]{1,0:T(8,128)(2,1)}, bf16[768,384]{1,0:T(8,128)(2,1)}, u32[]{:S(2)}, u32[]{:S(2)}) collective-permute-start(bf16[768,384]{1,0:T(8,128)(2,1)} %constant_dynamic-slice_fusion.7), channel_id=1, source_target_pairs={{0,2},{2,0},{1,3},{3,1},{4,6},{6,4},{5,7},{7,5},{8,10},{10,8},{9,1... | collective-permute-start | bytes 1769480 | tf_op jit(solution)/shard_map/ppermute | solution.py:564
  237.1 19.3 %collective-permute-start.14 = (f32[8,128]{1,0:T(8,128)}, f32[8,128]{1,0:T(8,128)}, u32[]{:S(2)}, u32[]{:S(2)}) collective-permute-start(f32[8,128]{1,0:T(8,128)} %broadcast_in_dim.11), channel_id=1, source_target_pairs={{0,1},{1,0},{2,3},{3,2},{4,5},{5,4},{6,7},{7,6},{8,9},{9,8},{10,11... | collective-permute-start | bytes 12296 | tf_op jit(solution)/shard_map/ppermute | solution.py:561
  261.5 48.0 %collective-permute-start.12 = (bf16[768,1536]{1,0:T(8,128)(2,1)}, bf16[768,1536]{1,0:T(8,128)(2,1)}, u32[]{:S(2)}, u32[]{:S(2)}) collective-permute-start(bf16[768,1536]{1,0:T(8,128)(2,1)} %pad_maximum_fusion.3), channel_id=1, source_target_pairs={{0,2},{2,0},{1,3},{3,1},{4,6},{6,4},{5,7},{7,5},{8,10},{10,8},{9,1... | collective-permute-start | bytes 7077896 | tf_op jit(solution)/shard_map/ppermute | solution.py:564
  291.1 38.4 %collective-permute-start.13 = (bf16[768,1536]{1,0:T(8,128)(2,1)S(1)}, bf16[768,1536]{1,0:T(8,128)(2,1)S(1)}, u32[]{:S(2)}, u32[]{:S(2)}) collective-permute-start(bf16[768,1536]{1,0:T(8,128)(2,1)S(1)} %constant_dynamic-slice_fusion.6), channel_id=1, source_target_pairs={{0,2},{2,0},{1,3},{3,1},{4,6},{6,4},{5,7},{7,5},{8,10},{10,8},{9,1... | collective-permute-start | bytes 7077896 | tf_op jit(solution)/shard_map/ppermute | solution.py:564
  301.2 28.3 %collective-permute-start.11 = (bf16[384,1536]{1,0:T(8,128)(2,1)}, bf16[384,1536]{1,0:T(8,128)(2,1)S(1)}, u32[]{:S(2)}, u32[]{:S(2)}) collective-permute-start(bf16[384,1536]{1,0:T(8,128)(2,1)} %fusion.26), channel_id=1, source_target_pairs={{0,1},{1,0},{2,3},{3,2},{4,5},{5,4},{6,7},{7,6},{8,9},{9,8},{10,11... | collective-permute-start | bytes 3538952 | tf_op jit(solution)/shard_map/ppermute | solution.py:561
  333.8 28.3 %collective-permute-start.15 = (bf16[384,1536]{1,0:T(8,128)(2,1)}, bf16[384,1536]{1,0:T(8,128)(2,1)}, u32[]{:S(2)}, u32[]{:S(2)}) collective-permute-start(bf16[384,1536]{1,0:T(8,128)(2,1)} %get-tuple-element.274.g_in.refs_0_), channel_id=1, source_target_pairs={{0,1},{1,0},{2,3},{3,2},{4,5},{5,4},{6,7},{7,6},{8,9},{9,8},{10,11... | collective-permute-start | bytes 3538952 | tf_op jit(solution)/shard_map/ppermute | solution.py:561
  335.3 42.8 %collective-permute-start.16 = (bf16[384,1536]{1,0:T(8,128)(2,1)}, bf16[384,1536]{1,0:T(8,128)(2,1)S(1)}, u32[]{:S(2)}, u32[]{:S(2)}) collective-permute-start(bf16[384,1536]{1,0:T(8,128)(2,1)} %get-tuple-element.274.g_in.refs_0_), channel_id=1, source_target_pairs={{0,2},{2,0},{1,3},{3,1},{4,6},{6,4},{5,7},{7,5},{8,10},{10,8},{9,1... | collective-permute-start | bytes 3538952 | tf_op jit(solution)/shard_map/ppermute | solution.py:564
  347.2 71.3 %collective-permute-start.22 = (bf16[2,384,1536]{2,1,0:T(8,128)(2,1)}, bf16[2,384,1536]{2,1,0:T(8,128)(2,1)S(1)}, u32[]{:S(2)}, u32[]{:S(2)}) collective-permute-start(bf16[2,384,1536]{2,1,0:T(8,128)(2,1)} %get-tuple-element.144), channel_id=1, source_target_pairs={{0,2},{2,0},{1,3},{3,1},{4,6},{6,4},{5,7},{7,5},{8,10},{10,8},{9,1... | collective-permute-start | bytes 7077896 | tf_op jit(solution)/shard_map/ppermute | solution.py:564
  362.0 17.1 %collective-permute-start.17 = (bf16[384,1536]{1,0:T(8,128)(2,1)}, bf16[384,1536]{1,0:T(8,128)(2,1)}, u32[]{:S(2)}, u32[]{:S(2)}) collective-permute-start(bf16[384,1536]{1,0:T(8,128)(2,1)} %collective-permute-done.15.g_in.refs_2_), channel_id=1, source_target_pairs={{0,2},{2,0},{1,3},{3,1},{4,6},{6,4},{5,7},{7,5},{8,10},{10,8},{9,1... | collective-permute-start | bytes 3538952 | tf_op jit(solution)/shard_map/ppermute | solution.py:564
  377.3 42.4 %collective-permute-start.23 = (bf16[2,384,1536]{2,1,0:T(8,128)(2,1)}, bf16[2,384,1536]{2,1,0:T(8,128)(2,1)}, u32[]{:S(2)}, u32[]{:S(2)}) collective-permute-start(bf16[2,384,1536]{2,1,0:T(8,128)(2,1)} %get-tuple-element.145), channel_id=1, source_target_pairs={{0,2},{2,0},{1,3},{3,1},{4,6},{6,4},{5,7},{7,5},{8,10},{10,8},{9,1... | collective-permute-start | bytes 7077896 | tf_op jit(solution)/shard_map/ppermute | solution.py:564
  377.4 41.2 %collective-permute-start.18 = (bf16[384,1536]{1,0:T(8,128)(2,1)}, bf16[384,1536]{1,0:T(8,128)(2,1)S(1)}, u32[]{:S(2)}, u32[]{:S(2)}) collective-permute-start(bf16[384,1536]{1,0:T(8,128)(2,1)} %copy-done.107), channel_id=1, source_target_pairs={{0,1},{1,0},{2,3},{3,2},{4,5},{5,4},{6,7},{7,6},{8,9},{9,8},{10,11... | collective-permute-start | bytes 3538952 | tf_op jit(solution)/shard_map/ppermute | solution.py:561
  395.2 42.2 %collective-permute-start.21 = (bf16[768,768]{1,0:T(8,128)(2,1)S(1)}, bf16[768,768]{1,0:T(8,128)(2,1)S(1)}, u32[]{:S(2)}, u32[]{:S(2)}) collective-permute-start(bf16[768,768]{1,0:T(8,128)(2,1)S(1)} %get-tuple-element.134), channel_id=1, source_target_pairs={{0,4},{4,0},{1,5},{5,1},{2,6},{6,2},{3,7},{7,3},{8,12},{12,8},{9,1... | collective-permute-start | bytes 3538952 | tf_op jit(solution)/shard_map/ppermute | solution.py:567
  397.3 21.3 %collective-permute-start.19 = (bf16[384,768]{1,0:T(8,128)(2,1)S(1)}, bf16[384,768]{1,0:T(8,128)(2,1)S(1)}, u32[]{:S(2)}, u32[]{:S(2)}) collective-permute-start(bf16[384,768]{1,0:T(8,128)(2,1)S(1)} %slice.247), channel_id=1, source_target_pairs={{0,1},{1,0},{2,3},{3,2},{4,5},{5,4},{6,7},{7,6},{8,9},{9,8},{10,11... | collective-permute-start | bytes 1769480 | tf_op jit(solution)/shard_map/ppermute | solution.py:561
  438.8 96.7 %reduce-scatter.11.cloned.1.call-start = ((), (), s32[]{:S(2)}) async-start(), calls=%async_computation.11 | async-start | bytes 983040 | tf_op jit(solution)/shard_map/reduce_scatter | solution.py:711
  438.9 25.2 %collective-permute-start.24 = (bf16[768,512]{1,0:T(8,128)(2,1)}, bf16[768,512]{1,0:T(8,128)(2,1)S(1)}, u32[]{:S(2)}, u32[]{:S(2)}) collective-permute-start(bf16[768,512]{1,0:T(8,128)(2,1)} %copy-done.104), channel_id=1, source_target_pairs={{0,4},{4,0},{1,5},{5,1},{2,6},{6,2},{3,7},{7,3},{8,12},{12,8},{9,1... | collective-permute-start | bytes 2359304 | tf_op jit(solution)/shard_map/ppermute | solution.py:567
  440.9 27.6 %collective-permute-start.20 = (bf16[384,1536]{1,0:T(8,128)(2,1)}, bf16[384,1536]{1,0:T(8,128)(2,1)}, u32[]{:S(2)}, u32[]{:S(2)}) collective-permute-start(bf16[384,1536]{1,0:T(8,128)(2,1)} %copy-done.62), channel_id=1, source_target_pairs={{0,1},{1,0},{2,3},{3,2},{4,5},{5,4},{6,7},{7,6},{8,9},{9,8},{10,11... | collective-permute-start | bytes 3538952 | tf_op jit(solution)/shard_map/ppermute | solution.py:561
  465.2 38.5 %collective-permute-start.26 = (bf16[768,1024]{1,0:T(8,128)(2,1)}, bf16[768,1024]{1,0:T(8,128)(2,1)}, u32[]{:S(2)}, u32[]{:S(2)}) collective-permute-start(bf16[768,1024]{1,0:T(8,128)(2,1)} %copy-done.102), channel_id=1, source_target_pairs={{0,4},{4,0},{1,5},{5,1},{2,6},{6,2},{3,7},{7,3},{8,12},{12,8},{9,1... | collective-permute-start | bytes 4718600 | tf_op jit(solution)/shard_map/ppermute | solution.py:567
  468.5 123.8 %reduce-scatter.13.cloned.1.call-start = ((), (), s32[]{:S(2)}) async-start(), calls=%async_computation.12 | async-start | bytes 1966080 | tf_op jit(solution)/shard_map/reduce_scatter | solution.py:711
  507.6 139.0 %reduce-scatter.15.cloned.1.call-start = ((), (), s32[]{:S(2)}) async-start(), calls=%async_computation.13 | async-start | bytes 1474560 | tf_op jit(solution)/shard_map/reduce_scatter | solution.py:711
  509.2 26.4 %collective-permute-start.25 = (bf16[384,1536]{1,0:T(8,128)(2,1)S(1)}, bf16[384,1536]{1,0:T(8,128)(2,1)S(1)}, u32[]{:S(2)}, u32[]{:S(2)}) collective-permute-start(bf16[384,1536]{1,0:T(8,128)(2,1)S(1)} %copy-done.25), channel_id=1, source_target_pairs={{0,1},{1,0},{2,3},{3,2},{4,5},{5,4},{6,7},{7,6},{8,9},{9,8},{10,11... | collective-permute-start | bytes 3538952 | tf_op jit(solution)/shard_map/ppermute | solution.py:561
  509.6 26.3 %collective-permute-start.27 = (bf16[768,768]{1,0:T(8,128)(2,1)}, bf16[768,768]{1,0:T(8,128)(2,1)}, u32[]{:S(2)}, u32[]{:S(2)}) collective-permute-start(bf16[768,768]{1,0:T(8,128)(2,1)} %pad_maximum_fusion.13), channel_id=1, source_target_pairs={{0,4},{4,0},{1,5},{5,1},{2,6},{6,2},{3,7},{7,3},{8,12},{12,8},{9,1... | collective-permute-start | bytes 3538952 | tf_op jit(solution)/shard_map/ppermute | solution.py:567
  538.8 53.5 %collective-permute-start.32 = (bf16[768,1536]{1,0:T(8,128)(2,1)}, bf16[768,1536]{1,0:T(8,128)(2,1)}, u32[]{:S(2)}, u32[]{:S(2)}) collective-permute-start(bf16[768,1536]{1,0:T(8,128)(2,1)} %pad_maximum_fusion.4), channel_id=1, source_target_pairs={{0,4},{4,0},{1,5},{5,1},{2,6},{6,2},{3,7},{7,3},{8,12},{12,8},{9,1... | collective-permute-start | bytes 7077896 | tf_op jit(solution)/shard_map/ppermute | solution.py:567
  539.4 163.4 %reduce-scatter.17.cloned.1.call-start = ((), (), s32[]{:S(2)}) async-start(), calls=%async_computation.14 | async-start | bytes 2949120 | tf_op jit(solution)/shard_map/reduce_scatter | solution.py:711
  539.8 52.0 %collective-permute-start.28 = (bf16[384,1536]{1,0:T(8,128)(2,1)}, bf16[384,1536]{1,0:T(8,128)(2,1)}, u32[]{:S(2)}, u32[]{:S(2)}) collective-permute-start(bf16[384,1536]{1,0:T(8,128)(2,1)} %copy-done.63), channel_id=1, source_target_pairs={{0,1},{1,0},{2,3},{3,2},{4,5},{5,4},{6,7},{7,6},{8,9},{9,8},{10,11... | collective-permute-start | bytes 3538952 | tf_op jit(solution)/shard_map/ppermute | solution.py:561
  542.7 48.3 %collective-permute-start.29 = (bf16[384,768]{1,0:T(8,128)(2,1)S(1)}, bf16[384,768]{1,0:T(8,128)(2,1)}, u32[]{:S(2)}, u32[]{:S(2)}) collective-permute-start(bf16[384,768]{1,0:T(8,128)(2,1)S(1)} %slice.250), channel_id=1, source_target_pairs={{0,1},{1,0},{2,3},{3,2},{4,5},{5,4},{6,7},{7,6},{8,9},{9,8},{10,11... | collective-permute-start | bytes 1769480 | tf_op jit(solution)/shard_map/ppermute | solution.py:561
  544.3 46.7 %collective-permute-start.30 = (bf16[144,1536]{1,0:T(8,128)(2,1)S(1)}, bf16[144,1536]{1,0:T(8,128)(2,1)S(1)}, u32[]{:S(2)}, u32[]{:S(2)}) collective-permute-start(bf16[144,1536]{1,0:T(8,128)(2,1)S(1)} %slice.251), channel_id=1, source_target_pairs={{0,1},{1,0},{2,3},{3,2},{4,5},{5,4},{6,7},{7,6},{8,9},{9,8},{10,11... | collective-permute-start | bytes 1327112 | tf_op jit(solution)/shard_map/ppermute | solution.py:561
  591.8 21.3 %collective-permute-start.35 = (bf16[768,1536]{1,0:T(8,128)(2,1)}, bf16[768,1536]{1,0:T(8,128)(2,1)}, u32[]{:S(2)}, u32[]{:S(2)}) collective-permute-start(bf16[768,1536]{1,0:T(8,128)(2,1)} %constant_dynamic-update-slice_fusion.2.refs_0_), channel_id=1, source_target_pairs={{0,2},{2,0},{1,3},{3,1},{4,6},{6,4},{5,7},{7,5},{8,10},{10,8},{9,1... | collective-permute-start | bytes 7077896 | tf_op jit(solution)/shard_map/ppermute | solution.py:564
  591.8 10.7 %collective-permute-start.33 = (bf16[768,1152]{1,0:T(8,128)(2,1)}, bf16[768,1152]{1,0:T(8,128)(2,1)}, u32[]{:S(2)}, u32[]{:S(2)}) collective-permute-start(bf16[768,1152]{1,0:T(8,128)(2,1)} %get-tuple-element.184), channel_id=1, source_target_pairs={{0,2},{2,0},{1,3},{3,1},{4,6},{6,4},{5,7},{7,5},{8,10},{10,8},{9,1... | collective-permute-start | bytes 5308424 | tf_op jit(solution)/shard_map/ppermute | solution.py:564
  596.6 143.9 %reduce-scatter.19.cloned.1.call-start = ((), (), s32[]{:S(2)}) async-start(), calls=%async_computation.15 | async-start | bytes 2211840 | tf_op jit(solution)/shard_map/reduce_scatter | solution.py:711
  613.0 15.2 %collective-permute-start.36 = (bf16[768,1536]{1,0:T(8,128)(2,1)}, bf16[768,1536]{1,0:T(8,128)(2,1)}, u32[]{:S(2)}, u32[]{:S(2)}) collective-permute-start(bf16[768,1536]{1,0:T(8,128)(2,1)} %constant_dynamic-update-slice_fusion.refs_0_), channel_id=1, source_target_pairs={{0,2},{2,0},{1,3},{3,1},{4,6},{6,4},{5,7},{7,5},{8,10},{10,8},{9,1... | collective-permute-start | bytes 7077896 | tf_op jit(solution)/shard_map/ppermute | solution.py:564
  620.7 13.4 %collective-permute-start.38 = (bf16[768,1536]{1,0:T(8,128)(2,1)S(1)}, bf16[768,1536]{1,0:T(8,128)(2,1)}, u32[]{:S(2)}, u32[]{:S(2)}) collective-permute-start(bf16[768,1536]{1,0:T(8,128)(2,1)S(1)} %pad_maximum_fusion.5.refs_0_), channel_id=1, source_target_pairs={{0,2},{2,0},{1,3},{3,1},{4,6},{6,4},{5,7},{7,5},{8,10},{10,8},{9,1... | collective-permute-start | bytes 7077896 | tf_op jit(solution)/shard_map/ppermute | solution.py:564
  621.2 40.8 %collective-permute-start.34 = (bf16[768,1152]{1,0:T(8,128)(2,1)}, bf16[768,1152]{1,0:T(8,128)(2,1)}, u32[]{:S(2)}, u32[]{:S(2)}) collective-permute-start(bf16[768,1152]{1,0:T(8,128)(2,1)} %get-tuple-element.186), channel_id=1, source_target_pairs={{0,4},{4,0},{1,5},{5,1},{2,6},{6,2},{3,7},{7,3},{8,12},{12,8},{9,1... | collective-permute-start | bytes 5308424 | tf_op jit(solution)/shard_map/ppermute | solution.py:567
  624.8 2.1 collective-permute-start.37
  626.0 8.0 %collective-permute-start.39 = (bf16[768,384]{1,0:T(8,128)(2,1)S(1)}, bf16[768,384]{1,0:T(8,128)(2,1)S(1)}, u32[]{:S(2)}, u32[]{:S(2)}) collective-permute-start(bf16[768,384]{1,0:T(8,128)(2,1)S(1)} %fusion.61), channel_id=1, source_target_pairs={{0,2},{2,0},{1,3},{3,1},{4,6},{6,4},{5,7},{7,5},{8,10},{10,8},{9,1... | collective-permute-start | bytes 1769480 | tf_op jit(solution)/shard_map/ppermute | solution.py:564
  626.9 14.4 %collective-permute-start.40 = (bf16[144,768]{1,0:T(8,128)(2,1)S(1)}, bf16[144,768]{1,0:T(8,128)(2,1)S(1)}, u32[]{:S(2)}, u32[]{:S(2)}) collective-permute-start(bf16[144,768]{1,0:T(8,128)(2,1)S(1)} %constant_dynamic-slice_fusion.5), channel_id=1, source_target_pairs={{0,2},{2,0},{1,3},{3,1},{4,6},{6,4},{5,7},{7,5},{8,10},{10,8},{9,1... | collective-permute-start | bytes 663560 | tf_op jit(solution)/shard_map/ppermute | solution.py:564
  665.8 88.9 %reduce-scatter.21.cloned.1.call-start = ((), (), s32[]{:S(2)}) async-start(), calls=%async_computation.16 | async-start | bytes 1474560 | tf_op jit(solution)/shard_map/reduce_scatter | solution.py:711
  665.8 27.3 %collective-permute-start.31 = (bf16[384,1536]{1,0:T(8,128)(2,1)}, bf16[384,1536]{1,0:T(8,128)(2,1)S(1)}, u32[]{:S(2)}, u32[]{:S(2)}) collective-permute-start(bf16[384,1536]{1,0:T(8,128)(2,1)} %copy-done.103), channel_id=1, source_target_pairs={{0,1},{1,0},{2,3},{3,2},{4,5},{5,4},{6,7},{7,6},{8,9},{9,8},{10,11... | collective-permute-start | bytes 3538952 | tf_op jit(solution)/shard_map/ppermute | solution.py:561
  669.6 5.8 collective-permute-start.52
  674.0 28.9 %collective-permute-start.42 = (bf16[768,768]{1,0:T(8,128)(2,1)S(1)}, bf16[768,768]{1,0:T(8,128)(2,1)}, u32[]{:S(2)}, u32[]{:S(2)}) collective-permute-start(bf16[768,768]{1,0:T(8,128)(2,1)S(1)} %pad_maximum_fusion.14), channel_id=1, source_target_pairs={{0,4},{4,0},{1,5},{5,1},{2,6},{6,2},{3,7},{7,3},{8,12},{12,8},{9,1... | collective-permute-start | bytes 3538952 | tf_op jit(solution)/shard_map/ppermute | solution.py:567
  694.5 45.9 %collective-permute-start.41 = (bf16[768,1152]{1,0:T(8,128)(2,1)}, bf16[768,1152]{1,0:T(8,128)(2,1)}, u32[]{:S(2)}, u32[]{:S(2)}) collective-permute-start(bf16[768,1152]{1,0:T(8,128)(2,1)} %pad_maximum_fusion.6), channel_id=1, source_target_pairs={{0,4},{4,0},{1,5},{5,1},{2,6},{6,2},{3,7},{7,3},{8,12},{12,8},{9,1... | collective-permute-start | bytes 5308424 | tf_op jit(solution)/shard_map/ppermute | solution.py:567
  710.4 39.8 %collective-permute-start.48 = (bf16[130,1536]{1,0:T(8,128)(2,1)}, bf16[130,1536]{1,0:T(8,128)(2,1)}, u32[]{:S(2)}, u32[]{:S(2)}) collective-permute-start(bf16[130,1536]{1,0:T(8,128)(2,1)} %slice.446), channel_id=1, source_target_pairs={{0,1},{1,0},{2,3},{3,2},{4,5},{5,4},{6,7},{7,6},{8,9},{9,8},{10,11... | collective-permute-start | bytes 1198088 | tf_op jit(solution)/shard_map/ppermute | solution.py:561
  712.0 75.8 %reduce-scatter.23.cloned.1.call-start = ((), (), s32[]{:S(2)}) async-start(), calls=%async_computation.17 | async-start | bytes 2211840 | tf_op jit(solution)/shard_map/reduce_scatter | solution.py:711
  712.5 1.6 collective-permute-start.53
  712.7 1.9 collective-permute-start.54
  743.6 3.8 collective-permute-start.43
  748.7 4.3 collective-permute-start.45
  753.0 3.9 collective-permute-start.46
  755.6 10.0 %collective-permute-start.50 = (bf16[96,768]{1,0:T(8,128)(2,1)S(1)}, bf16[96,768]{1,0:T(8,128)(2,1)S(1)}, u32[]{:S(2)}, u32[]{:S(2)}) collective-permute-start(bf16[96,768]{1,0:T(8,128)(2,1)S(1)} %constant_dynamic-slice_fusion.3), channel_id=1, source_target_pairs={{0,2},{2,0},{1,3},{3,1},{4,6},{6,4},{5,7},{7,5},{8,10},{10,8},{9,1... | collective-permute-start | bytes 442376 | tf_op jit(solution)/shard_map/ppermute | solution.py:564
  756.9 6.8 collective-permute-start.47
  759.5 8.5 %collective-permute-start.49 = (bf16[96,1152]{1,0:T(8,128)(2,1)S(1)}, bf16[96,1152]{1,0:T(8,128)(2,1)S(1)}, u32[]{:S(2)}, u32[]{:S(2)}) collective-permute-start(bf16[96,1152]{1,0:T(8,128)(2,1)S(1)} %constant_dynamic-slice_fusion.4), channel_id=1, source_target_pairs={{0,2},{2,0},{1,3},{3,1},{4,6},{6,4},{5,7},{7,5},{8,10},{10,8},{9,1... | collective-permute-start | bytes 663560 | tf_op jit(solution)/shard_map/ppermute | solution.py:564
  788.8 1.5 collective-permute-start.51
  (144 other events, 986.2 us)
Sparse Core Ops, SparseCore 0:
  14.9 103.5 all-gather.2
  120.0 145.5 all-gather.4
  439.0 28.7 reduce-scatter.8
  469.9 21.7 reduce-scatter.10
  507.7 33.9 reduce-scatter.12
  543.8 28.1 reduce-scatter.14
  596.7 46.9 reduce-scatter.16
  665.9 37.2 reduce-scatter.18
  712.1 28.0 reduce-scatter.20
  748.8 38.9 reduce-scatter.22

commit v3 on v2

--- a/solution.py
+++ b/solution.py
@@ -14,13 +14,13 @@
 EPSILON = 1e-05
 F32 = jnp.float32
 BF16 = jnp.bfloat16
-KERNEL_VMEM = 24 << 20
-PACK_VMEM = 56 << 20
-GRAD_VMEM = 32 << 20
-BACK_VMEM = 44 << 20
+KERNEL_VMEM = 60 << 20
+PACK_VMEM = 60 << 20
+GRAD_VMEM = 60 << 20
+BACK_VMEM = 60 << 20
 DOWN_PIECES = (768, 512, 256)
-GATE_PIECES = (1024, 512)
-UP_PIECES = (256, 1280)
+GATE_PIECES = (1408, 128)
+UP_PIECES = (768, 768)
 PULL_ROWS = 256
 NORM_ROWS = 128
 FEED_COLUMNS = 512
@@ -470,6 +470,129 @@
     return outs[: len(pieces)], outs[len(pieces) :]
 
 
+def whole_call(kernel, out_shape, *args):
+    return pl.pallas_call(
+        kernel,
+        out_shape=out_shape,
+        compiler_params=pltpu.CompilerParams(vmem_limit_bytes=BACK_VMEM),
+        cost_estimate=SMALL_COST,
+    )(*args)
+
+
+def join_kernel(axis, *refs):
+    refs[-1][...] = jnp.concatenate([ref[...] for ref in refs[:-1]], axis=axis)
+
+
+def join(axis, *parts):
+    shape = list(parts[0].shape)
+    shape[axis] = sum(part.shape[axis] for part in parts)
+    return whole_call(
+        functools.partial(join_kernel, axis), jax.ShapeDtypeStruct(shape, parts[0].dtype), *parts
+    )
+
+
+def near_sum_kernel(*refs):
+    got, out = refs[-2:]
+    at = 0
+    for ref in refs[:-2]:
+        end = at + ref.shape[1]
+        out[:, at:end] = (ref[...].astype(F32) + got[:, at:end].astype(F32)).astype(BF16)
+        at = end
+
+
+def near_sum(kept, got):
+    rows, columns = got.shape
+    block = rows // 4 if rows % 64 == 0 else rows
+
+    def spec(width):
+        return pl.BlockSpec((block, width), lambda i: (i, 0))
+
+    return pl.pallas_call(
+        near_sum_kernel,
+        grid=(rows // block,),
+        in_specs=[spec(part.shape[1]) for part in kept] + [spec(columns)],
+        out_specs=spec(columns),
+        out_shape=jax.ShapeDtypeStruct(got.shape, BF16),
+        compiler_params=pltpu.CompilerParams(vmem_limit_bytes=KERNEL_VMEM),
+        cost_estimate=SMALL_COST,
+    )(*kept, got)
+
+
+def other_half_kernel(places, *refs):
+    out, at = refs[-1], 0
+    for ref in refs[:-1]:
+        out[at : at + ref.shape[0], :] = ref[...]
+        at += ref.shape[0]
+
+
+def other_half(places, width, *parts):
+    half = width // 2
+    rows = sum(part.shape[0] for part in parts)
+    return pl.pallas_call(
+        other_half_kernel,
+        grid_spec=pltpu.PrefetchScalarGridSpec(
+            num_scalar_prefetch=1,
+            grid=(1,),
+            in_specs=[
+                pl.BlockSpec((part.shape[0], half), lambda i, places: (0, 1 - places[1]))
+                for part in parts
+            ],
+            out_specs=pl.BlockSpec((rows, half), lambda i, places: (0, 0)),
+        ),
+        out_shape=jax.ShapeDtypeStruct((rows, half), BF16),
+        compiler_params=pltpu.CompilerParams(vmem_limit_bytes=KERNEL_VMEM),
+        cost_estimate=SMALL_COST,
+    )(places, *parts)
+
+
+def mixed_back_kernel(g_in, own_w, peer_w, own_out, peer_out):
+    own_out[...] = dot(g_in[...], own_w[...], 1, 0).astype(BF16)
+    peer_out[...] = dot(g_in[...], peer_w[...], 1, 0).astype(BF16)
+
+
+def mixed_back(grads, weights, at, peer_weights):
+    rows, depth = grads.shape
+    width = peer_weights.shape[1]
+    half = width // 2
+    act = jax.ShapeDtypeStruct((rows, width), BF16)
+    return pl.pallas_call(
+        mixed_back_kernel,
+        grid=(2,),
+        in_specs=[
+            pl.BlockSpec((rows, depth), lambda i: (0, 0)),
+            pl.BlockSpec((depth, half), lambda i: (0, 2 * at + i)),
+            pl.BlockSpec((depth, half), lambda i: (0, i)),
+        ],
+        out_specs=[pl.BlockSpec((rows, half), lambda i: (0, i))] * 2,
+        out_shape=[act, act],
+        compiler_params=pltpu.CompilerParams(vmem_limit_bytes=KERNEL_VMEM),
+        cost_estimate=SMALL_COST,
+    )(grads, weights, peer_weights)
+
+
+def pull_query_kernel(g_in, own_w, peer_w, out):
+    width = own_w.shape[1]
+    out[...] = dot(g_in[:, :width], own_w[...], 1, 1) + dot(g_in[:, width:], peer_w[...], 1, 1)
+
+
+def pull_query(grads, weights, at, peer_weights):
+    rows = grads.shape[0]
+    depth, width = peer_weights.shape
+    return pl.pallas_call(
+        pull_query_kernel,
+        grid=(depth // PULL_ROWS,),
+        in_specs=[
+            pl.BlockSpec(grads.shape, lambda i: (0, 0)),
+            pl.BlockSpec((PULL_ROWS, width), lambda i: (i, at)),
+            pl.BlockSpec((PULL_ROWS, width), lambda i: (i, 0)),
+        ],
+        out_specs=pl.BlockSpec((rows, PULL_ROWS), lambda i: (0, i)),
+        out_shape=jax.ShapeDtypeStruct((rows, depth), F32),
+        compiler_params=pltpu.CompilerParams(vmem_limit_bytes=KERNEL_VMEM),
+        cost_estimate=SMALL_COST,
+    )(grads, weights, peer_weights)
+
+
 def pull_kernel(gate_in, up_in, weights, out):
     width = gate_in.shape[1]
     total = dot(gate_in[...], weights[:, :width], 1, 1) + dot(up_in[...], weights[:, width:], 1, 1)
@@ -489,6 +612,10 @@
         compiler_params=pltpu.CompilerParams(vmem_limit_bytes=GRAD_VMEM),
         cost_estimate=SMALL_COST,
     )(grad_gate, grad_upper, weights)
+
+
+def meet(*values):
+    return lax.optimization_barrier(values)
 
 
 def pack_attention_kernel(q_in, k_in, v_in, o_in, cq_in, ck_in, cv_in, co_in, gains, mask, out):
@@ -636,13 +763,6 @@
     order = lax.iota(jnp.int32, length)
     positions = jnp.where(order < rows, order + share * rows, order - share * rows)
     cosines, sines = rotary_tables(positions)
-    def half_of(values, index):
-        half = values.shape[1] // 2
-        return lax.dynamic_slice(values, (0, index * half), (values.shape[0], half))
-
-    def other_half(values):
-        return to_core(half_of(values, 1 - pair))
-
     def project(values, weight, weight_dim, *meanwhile):
         away = to_peer(dot(values[rows:], weight, 1, weight_dim).astype(BF16))
         mine = dot(values[:rows], weight, 1, weight_dim)
@@ -674,7 +794,7 @@
     normed_three, _ = norm_stats(hidden_two)
     own_three = (normed_three * gains[2]).astype(BF16)
     peer_three = to_peer(own_three)
-    core_mixed_self, core_cond = other_half(mixed_self), to_core(cond_rows)
+    core_mixed_self, core_cond = to_core(other_half(places, heads_width, mixed_self)), to_core(cond_rows)
     peer_three = after(peer_three, core_mixed_self, core_cond)
     input_three = jnp.concatenate([own_three, peer_three], axis=0)
     weight_gate = gath_b[:, :ff_width]
@@ -685,7 +805,8 @@
     gate_sum = gate_pre.astype(F32)
     hidden_ff = (gate_sum * jax.nn.sigmoid(gate_sum) * up_sum).astype(BF16)
     up_pre = up_sum.astype(BF16)
-    core_three, core_hidden = to_core(input_three), other_half(hidden_ff)
+    core_three = to_core(input_three)
+    core_hidden = to_core(other_half(places, ff_width, hidden_ff))
     block_out = hidden_two + project(hidden_ff, weight_down, 1, core_three, core_hidden)
 
     error_diff = block_out - teacher[0].astype(F32)
@@ -696,15 +817,13 @@
     def grad_of(pieces, *parts):
         return weight_grad(places, far, pieces, parts)
 
-    landed, scattered = [], []
-
-    def launch(sent, *events):
-        return to_near(after(sent, *events))
-
-    def land(got, kept, *events):
-        got = after(got, *events, *scattered[:-1])
-        landed.append((kept.astype(F32) + got.astype(F32)).astype(BF16))
-        scattered.append(scatter(landed[-1]))
+    scattered = []
+
+    def add_pair(kept, got):
+        return near_sum(kept, after(got, *scattered[:-1]))
+
+    def scatter_on(summed):
+        scattered.append(scatter(summed))
         return scattered[-1]
 
     def scatter(summed):
@@ -731,130 +850,177 @@
         return gains[index : index + 1]
 
     dgate_own, dup_own, halves_own = feed_back(places, own_e3, gath_b, gate_pre, up_pre, 0)
-    core_own_halves = to_core(halves_own)
-    pulled_own = pull(dgate_own, dup_own, gath_b, F32)
-    peer_e3 = after(peer_e3, pulled_own)
-    core_peer_e3 = to_core(peer_e3)
-    peer_two = to_peer(after(own_two, peer_e3))
-    peer_mixed = to_peer(after(mixed_cross, peer_e3)[:, heads_width:])
-    dgate_peer, dup_peer, halves_peer = feed_back(places, peer_e3, gath_b, gate_pre, up_pre, 1)
+    dgate_own, dup_own, halves_own, pulled_own, peer_e3, core_own_e3 = meet(
+        dgate_own, dup_own, halves_own, pull(dgate_own, dup_own, gath_b, F32), peer_e3, core_own_e3
+    )
+    dgate_peer, dup_peer, halves_peer, core_peer_e3, core_own_halves = meet(
+        *feed_back(places, peer_e3, gath_b, gate_pre, up_pre, 1),
+        to_core(peer_e3),
+        to_core(halves_own),
+    )
     kept_down, sent_down = grad_of(
         DOWN_PIECES,
         (own_e3, (hidden_ff, 0), None),
-        (after(peer_e3, dgate_peer), (hidden_ff, 1), None),
+        (peer_e3, (hidden_ff, 1), None),
         (core_own_e3, (core_hidden, 0), 0),
         (core_peer_e3, (core_hidden, 1), 0),
     )
-    near_down = launch(sent_down[0])
-    dgate_peer, dup_peer, _ = lax.optimization_barrier((dgate_peer, dup_peer, sent_down[0]))
-    core_peer_halves = to_core(halves_peer)
-    pulled_peer, peer_two, peer_mixed = lax.optimization_barrier(
-        (pull(dgate_peer, dup_peer, gath_b, BF16), peer_two, peer_mixed)
+    *sent_down, dgate_peer, dup_peer, halves_peer = meet(
+        *sent_down, dgate_peer, dup_peer, halves_peer
+    )
+    near_a = to_near(sent_down[0])
+    pulled_peer, core_peer_halves = meet(
+        pull(dgate_peer, dup_peer, gath_b, BF16), to_core(halves_peer)
     )
     away = to_peer(pulled_peer)
 
-    def feed_grad(pieces, own, peer, at, *earlier):
-        return grad_of(
+    def feed_grad(pieces, own, peer, at):
+        kept, sent = grad_of(
             pieces,
-            (own_three, after(own, *earlier), None),
+            (own_three, own, None),
             (peer_three, peer, None),
             ((core_three, 0), core_own_halves, at),
             ((core_three, 1), core_peer_halves, at),
         )
-
-    kept_gate, sent_gate = feed_grad(GATE_PIECES, dgate_own, dgate_peer, 0, pulled_peer)
-    scat_down = [land(near_down, kept_down[0], sent_gate[0])]
-    near_down = launch(sent_down[1], landed[-1])
-    kept_up, sent_up = feed_grad(UP_PIECES, dup_own, dup_peer, 1, sent_gate[0])
-    scat_down.append(land(near_down, kept_down[1], sent_up[0]))
-    near_gate = launch(sent_gate[0], landed[-1])
-    grad_two, own_e2, gain_three = norm_back(
-        pulled_own, after(away, landed[-1]), hidden_two, row(2), grad_out
-    )
-
-    grad_mixed = tuple(
-        dot(own_e2, weight, 1, 0).astype(BF16) for weight in (cross_o_own, cross_o_peer)
-    )
+        return kept + sent
+
+    *gate_w, near_a = meet(
+        *feed_grad(GATE_PIECES, dgate_own, after(dgate_peer, pulled_peer), 0), near_a
+    )
+    near_b = to_near(after(sent_down[1], near_a))
+    *up_w, sum_a, near_b, away = meet(
+        *feed_grad(UP_PIECES, dup_own, after(dup_peer, gate_w[0]), 1),
+        add_pair(kept_down[:1], near_a),
+        near_b,
+        away,
+    )
+    scat_down = [scatter_on(sum_a)]
+    near_c = to_near(after(gate_w[2], near_b))
+    peer_two = to_peer(after(own_two, away))
+    peer_mixed = to_peer(after(mixed_cross, away)[:, heads_width:])
+    grad_two, own_e2, gain_three = norm_back(pulled_own, away, hidden_two, row(2), grad_out)
+
+    grad_mixed = mixed_back(own_e2, gath_a, 7, cross_o_peer)
     grad_qc, grad_kv = cross_back(query_cross, grad_mixed, keyvals, logs_cross, ctx_len)
-    pulled_two = dot(grad_qc[:, :heads_width], cross_q_own, 1, 1) + dot(
-        grad_qc[:, heads_width:], cross_q_peer, 1, 1
-    )
+    pulled_two = pull_query(grad_qc, gath_a, 6, cross_q_peer)
     grad_one, own_e1, gain_two = norm_back(pulled_two, None, hidden_one, row(1), grad_two)
-
+    sum_b = add_pair(kept_down[1:2], near_b)
+    scat_down.append(scatter_on(sum_b))
+    sent_d = up_w[2]
+    grad_one, own_e1, gain_two, sum_b, own_e2, sent_d, near_c, peer_two, peer_mixed = meet(
+        grad_one, own_e1, gain_two, sum_b, own_e2, sent_d, near_c, peer_two, peer_mixed
+    )
+
+    near_d = to_near(sent_d)
     peer_e1 = to_peer(own_e1)
-    scat_gate = [land(near_gate, kept_gate[0], own_e1)]
-    near_mid = launch(jnp.concatenate([sent_gate[1], sent_up[0]], axis=1), landed[-1])
-    mid = land(near_mid, jnp.concatenate([kept_gate[1], kept_up[0]], axis=1), peer_e1)
-    peer_e1 = after(peer_e1, landed[-1])
-    near_up = launch(jnp.concatenate([sent_up[1], sent_down[2]], axis=1), landed[-1])
-    peer_e2, peer_qc = to_peer(after(own_e2, peer_e1)), to_peer(after(grad_qc, peer_e1)[:, heads_width:])
-    peer_kv = to_peer(after(grad_kv, peer_e1)[:, 2 * heads_width :])
-    grad_qkv, halves_qkv, pulled_own, pulled_peer = self_back(
-        places,
-        query_self,
-        key_self,
-        value_self,
-        own_e1,
+    input_two = join(0, own_two, peer_two)
+    mixed_two = join(0, mixed_cross[:, :heads_width], peer_mixed)
+    sum_c = add_pair(gate_w[:1], near_c)
+    scat_gate = [scatter_on(sum_c)]
+    sum_c, peer_e1, near_d, input_two, mixed_two, half_mixed = meet(
+        sum_c,
         peer_e1,
-        gath_a,
-        logs_self,
-        cosines,
-        sines,
-    )
-    peer_e2, peer_qc, peer_kv, pulled_peer, grad_qkv = lax.optimization_barrier(
-        (peer_e2, peer_qc, peer_kv, pulled_peer, grad_qkv)
+        near_d,
+        input_two,
+        mixed_two,
+        other_half(places, heads_width, mixed_two),
+    )
+    own_e2, grad_qc, _ = meet(own_e2, grad_qc, peer_e1)
+
+    def head_grad(*parts):
+        kept, sent = grad_of((half_heads,), *parts)
+        return kept[0], sent[0]
+
+    sum_d = add_pair([up_w[0]], near_d)
+    mid = scatter_on(sum_d)
+    branch_one = join(0, own_e1, peer_e1)
+    sum_d, core_e1, branch_one = meet(sum_d, to_core(branch_one), branch_one)
+    kept_wo, sent_wo = head_grad(
+        (branch_one, mixed_self, None), (core_e1, core_mixed_self, 0)
+    )
+    kept_wo, sent_e = meet(kept_wo, join(1, up_w[3], sent_down[2], gate_w[3], sent_wo))
+    near_e = to_near(sent_e)
+    grad_qkv, halves_qkv, pulled_own, pulled_peer, peer_e2, peer_qc, near_e = meet(
+        *self_back(
+            places,
+            query_self,
+            key_self,
+            value_self,
+            own_e1,
+            after(peer_e1, sent_e),
+            gath_a,
+            logs_self,
+            cosines,
+            sines,
+        ),
+        to_peer(own_e2),
+        to_peer(grad_qc[:, heads_width:]),
+        near_e,
     )
     away = to_peer(pulled_peer)
-    core_qkv = to_core(halves_qkv)
-    last_ff = land(near_up, jnp.concatenate([kept_up[1], kept_down[2]], axis=1), pulled_peer)
+    sum_e = add_pair([up_w[1], kept_down[2], gate_w[1], kept_wo], near_e)
+    last_ff = scatter_on(sum_e)
+    sum_e, core_qkv = meet(sum_e, to_core(halves_qkv))
+    piece = 3 * half_heads // 2 // PAIR * PAIR
     kept_qkv, sent_qkv = grad_of(
-        (3 * half_heads,),
-        (input_one, after(grad_qkv, landed[-1]), None),
+        (piece, 3 * half_heads - piece),
+        (input_one, after(grad_qkv, sum_e), None),
         (core_one, core_qkv, 0),
     )
-    near_qkv = launch(sent_qkv[0])
-    branch_one = jnp.concatenate([own_e1, peer_e1], axis=0)
-    branch_two = jnp.concatenate([own_e2, peer_e2], axis=0)
-    input_two = jnp.concatenate([own_two, peer_two], axis=0)
-    mixed_two = jnp.concatenate([mixed_cross[:, :heads_width], peer_mixed], axis=0)
-    both_qc = jnp.concatenate([grad_qc[:, :heads_width], peer_qc], axis=0)
-    sum_kv = (grad_kv[:, : 2 * heads_width].astype(F32) + peer_kv.astype(F32)).astype(BF16)
-    kept_wo, sent_wo = grad_of(
-        (half_heads,),
-        (branch_one, after(mixed_self, sent_qkv[0]), None),
-        (to_core(after(branch_one, grad_qkv)), core_mixed_self, 0),
-    )
-    kept_co, sent_co = grad_of(
-        (half_heads,),
-        (branch_two, after(mixed_two, sent_wo[0]), None),
-        (to_core(after(branch_two, sent_qkv[0])), other_half(mixed_two), 0),
-    )
-    kept_cq, sent_cq = grad_of(
-        (half_heads,),
-        (input_two, after(both_qc, sent_co[0]), None),
-        (to_core(after(input_two, sent_wo[0])), other_half(both_qc), 0),
-    )
+    *kept_qkv, sent_f, sent_g = meet(*kept_qkv, *sent_qkv)
+    near_f = to_near(sent_f)
+    both_qc = join(0, grad_qc[:, :heads_width], after(peer_qc, sent_f))
+    branch_two, both_qc, half_qc, away, near_f = meet(
+        join(0, own_e2, after(peer_e2, sent_f)),
+        both_qc,
+        other_half(places, heads_width, both_qc),
+        away,
+        near_f,
+    )
+    near_g = to_near(sent_g)
+    sum_f = add_pair([kept_qkv[0]], near_f)
+    scat_qkv = [scatter_on(sum_f)]
+    core_e2, core_qc, core_two, core_mixed = (
+        to_core(after(part, branch_two)) for part in (branch_two, half_qc, input_two, half_mixed)
+    )
+    sum_f, core_e2, core_mixed, core_qc, core_two = meet(
+        sum_f, core_e2, core_mixed, core_qc, core_two
+    )
+    peer_kv = to_peer(after(grad_kv, sum_f)[:, 2 * heads_width :])
+    kept_co, sent_co = head_grad((branch_two, mixed_two, None), (core_e2, core_mixed, 0))
+    kept_cq, sent_cq = head_grad(
+        (input_two, after(both_qc, sent_co), None), (core_two, core_qc, 0)
+    )
+    kept_co, kept_cq, sent_w, near_g, peer_kv = meet(
+        kept_co, kept_cq, join(1, sent_co, sent_cq), near_g, peer_kv
+    )
+    near_w = to_near(sent_w)
+    sum_g = add_pair([kept_qkv[1]], near_g)
+    scat_qkv.append(scatter_on(sum_g))
+    sum_kv = near_sum([grad_kv[:, : 2 * heads_width]], after(peer_kv, sum_g))
+    sum_kv, half_kv = meet(sum_kv, other_half(places, 2 * heads_width, sum_kv))
+    grad_rows, _, gain_one = norm_back(
+        pulled_own, after(away, half_kv), x_bf, row(0), grad_one
+    )
+    grad_rows, gain_one, core_kv = meet(grad_rows, gain_one, to_core(half_kv))
     kept_ckv, sent_ckv = grad_of(
-        (heads_width,),
-        (cond_rows, after(sum_kv, sent_cq[0]), None),
-        (core_cond, other_half(sum_kv), 0),
-    )
-    near_w = launch(jnp.concatenate(sent_wo + sent_co, axis=1))
-    near_c = launch(jnp.concatenate(sent_cq + sent_ckv, axis=1))
-    scat_qkv = land(near_qkv, kept_qkv[0], sent_ckv[0])
-    grad_rows, _, gain_one = norm_back(
-        pulled_own, after(away, landed[-1]), x_bf, row(0), grad_one
-    )
-    scat_w = land(near_w, jnp.concatenate(kept_wo + kept_co, axis=1), grad_rows)
-    cond_part = dot(after(sum_kv, landed[-1]), cross_kv, 1, 1)[:ctx_len].astype(BF16)
+        (heads_width,), (cond_rows, after(sum_kv, grad_rows), None), (core_cond, core_kv, 0)
+    )
+    kept_ckv, sent_ckv, near_w, last_ff = meet(kept_ckv[0], sent_ckv[0], near_w, last_ff)
+    near_c = to_near(sent_ckv)
+    sum_w, *scat_qkv = meet(near_sum([kept_co, kept_cq], near_w), *scat_qkv)
+    scat_w = scatter(sum_w)
+    cond_part = dot(after(sum_kv, sum_w), cross_kv, 1, 1)[:ctx_len].astype(BF16)
+    near_c, cond_part = meet(near_c, cond_part)
     cond_sum = cond_part.astype(F32) + to_peer(cond_part).astype(F32)
-    scat_c = land(near_c, jnp.concatenate(kept_cq + kept_ckv, axis=1), cond_part)
+    sum_c = near_sum([kept_ckv], near_c)
+    scat_c = scatter(sum_c)
 
     small = jnp.concatenate(
         [gain_one, gain_two, gain_three, jnp.full((1, width), local_error, F32)],
         axis=0,
     )
-    small = after(small, landed[-1])
+    small = after(small, scat_w)
     for axis in ("tensor", "core", "near", "far"):
         size = lax.axis_size(axis)
         if size & (size - 1):
@@ -868,26 +1034,27 @@
     place = (lax.axis_index("far") * 4 + near_at * 2 + pair) * slab
     grad_gains = lax.dynamic_slice(small, (0, place), (3, slab))
 
-    split = GATE_PIECES[1]
-    gate_parts = scat_gate + [mid[:, :split]]
-    up_parts = [mid[:, split:], last_ff[:, : UP_PIECES[1]]]
-    down_parts = scat_down + [last_ff[:, UP_PIECES[1] :]]
+    ends = (
+        UP_PIECES[1],
+        UP_PIECES[1] + DOWN_PIECES[2],
+        UP_PIECES[1] + DOWN_PIECES[2] + GATE_PIECES[1],
+    )
+    gate_parts = scat_gate + [last_ff[:, ends[1] : ends[2]]]
+    up_parts = [mid, last_ff[:, : ends[0]]]
+    down_parts = scat_down + [last_ff[:, ends[0] : ends[1]]]
     down_t, gate_s, up_s = (
         jnp.concatenate(finish(jnp.concatenate(parts, axis=1)), axis=1)
         for parts in (down_parts, gate_parts, up_parts)
     )
-    sides = finish(scat_qkv)
+    sides = finish(jnp.concatenate(scat_qkv, axis=1))
     q_s, k_s, v_s = (
         columns_at(sides, range(i * PAIR, 3 * half_heads, 3 * PAIR), PAIR) for i in range(3)
     )
+    out_t = jnp.concatenate(finish(last_ff[:, ends[2] :]), axis=1)
     sides = finish(scat_w)
-    out_t, co_t = (columns_at(sides, [i * half_heads], half_heads) for i in range(2))
+    co_t, cq_s = (columns_at(sides, [i * half_heads], half_heads) for i in range(2))
     sides = finish(scat_c)
-    cq_s = columns_at(sides, [0], half_heads)
-    ck_s, cv_s = (
-        columns_at(sides, range(half_heads + i * PAIR, 3 * half_heads, 2 * PAIR), PAIR)
-        for i in range(2)
-    )
+    ck_s, cv_s = (columns_at(sides, range(i * PAIR, heads_width, 2 * PAIR), PAIR) for i in range(2))
     return (
         block_out.astype(BF16)[None],
         mean_loss,

time: 809 us -> 800 us (0.989)
  Pallas kernels: 213 us -> 334 us
  waiting for transfers between devices: 295 us -> 248 us
  local copies, waits for them, and re-layouts: 78.9 us -> 37.7 us
  other arithmetic: 68.1 us -> 35.1 us
    pallas_call x0 -> x24, Pallas kernels: none -> 83.9 us  [the longest x10 36.8 us: near_sum(): pl.pallas_call(near_sum_kernel, grid=(rows // block,), in_specs=[spec(par...]
    ppermute x18, waiting for transfers between devices: 147 us -> 112 us  [to_peer(): return lax.ppermute(values, 'tensor', swap)]
    unnamed x301 -> x158, local copies, waits for them, and re-layouts: 52.4 us -> 19.1 us
    convert_element_type x9 -> x0, other arithmetic: 23 us -> none  [the longest x8 22.9 us: land(): landed.append((kept.astype(F32) + got.astype(F32)).astype(BF16))]
    ppermute x8 -> x9, waiting for transfers between devices: 45.2 us -> 26.3 us  [to_near(): return lax.ppermute(values, 'near', swap)]
    pallas_call x8, Pallas kernels: 72.1 us -> 85.4 us  [weight_grad(): pl.pallas_call(functools.partial(weight_grad_kernel, len(parts), pieces,...]
    pallas_call x3, Pallas kernels: 8.76 us -> 20.4 us  [norm_back(): pl.pallas_call(functools.partial(norm_back_kernel, len(arrays) - 1), grid...]
    concatenate x9 -> x2, other arithmetic: 11.9 us -> 3.1 us  [join_cores(): jnp.concatenate([jnp.where(pair == 0, got, other), jnp.where(pair == 0, o...]
  transfers between devices with their start and end apart: 65 -> 68, of which waited for: 25 -> 25; matrix products, arithmetic and copies ran while one was open for 21% -> 16% of each run, Pallas kernels for 26% -> 40%
where the time goes in v3:
time: 800 us; the launch traced here: 791 us
  Pallas kernels  334 us (42%)
  waiting for transfers between devices  248 us (31%)
  matrix products  76.7 us (10%)
  starting transfers between devices  40.2 us (5%)
  local copies, waits for them, and re-layouts  37.7 us (5%)
  other arithmetic  35.1 us (4%)
  between operations  19.7 us (2%)
    ppermute x18, waiting for transfers between devices, to_peer(): return lax.ppermute(values, 'tensor', swap)  112 us
    pallas_call x8, Pallas kernels, weight_grad(): pl.pallas_call(functools.partial(weight_grad_kernel, len(parts), pieces,...  85.4 us
    dot_general x13, matrix products, dot(): lax.dot_general(left, right, (((left_dim,), (right_dim,)), ((), ())), pre...  76.7 us
    all_gather x2, waiting for transfers between devices, gather(): return lax.all_gather(values, dp_axes, axis=0, tiled=True)  74.7 us
    pallas_call x1, Pallas kernels, self_back(): pl.pallas_call(self_back_kernel, grid_spec=pltpu.PrefetchScalarGridSpec(n...  44.4 us
    pallas_call x10, Pallas kernels, near_sum(): pl.pallas_call(near_sum_kernel, grid=(rows // block,), in_specs=[spec(par...  36.8 us
    pallas_call x2, Pallas kernels, pull(): pl.pallas_call(pull_kernel, grid=(depth // PULL_ROWS,), in_specs=[whole,...  28.1 us
    ppermute x9, waiting for transfers between devices, to_near(): return lax.ppermute(values, 'near', swap)  26.3 us
  transfers between devices with their start and end apart: 68, of which 25 were waited for; matrix products, arithmetic and copies ran while one was open for 16% of the time, Pallas kernels for 40%

profile of v3, /device:TPU:0, one launch (start us, length us, event | category | flops | bytes accessed | tf_op | source)
XLA Modules:
  0.0 791.5 jit_solution(11152224792639458071)
XLA Ops:
  16.0 3.1 shard_map.283
  19.1 3.0 collective-permute-start
  25.9 22.2 %collective-permute-done = bf16[384,1536]{1,0:T(8,128)(2,1)S(1)} collective-permute-done((bf16[384,1536]{1,0:T(8,128)(2,1)S(1)}, bf16[384,1536]{1,0:T(8,128)(2,1)S(1)}, u32[]{:S(2)}, u32[]{:S(2)}) %collective-permute-start) | collective-permute-done | bytes 1179680 | tf_op jit(solution)/shard_map/ppermute | solution.py:688
  48.8 69.6 %all-gather.3.cloned.1.call-done.own_w.out_w.qkv_w = bf16[1536,6272]{1,0:T(8,128)(2,1)} async-done(((bf16[96,6272]{1,0:T(8,128)(2,1)}), bf16[1536,6272]{1,0:T(8,128)(2,1)}) %all-gather.3.cloned.1.call-update) | async-done | bytes 19267600 | tf_op jit(solution)/shard_map/all_gather | solution.py:697
  119.6 3.2 constant_dynamic-slice_fusion.6
  126.5 12.3 %fusion.13.qkv = f32[768,2304]{1,0:T(8,128)} fusion(bf16[1536,6272]{1,0:T(8,128)(2,1)} %all-gather.3.cloned.1.call-done.own_w.out_w.qkv_w, bf16[384,1536]{1,0:T(8,128)(2,1)S(1)} %get-tuple-element.481, bf16[384,1536]{1,0:T(8,128)(2,1)S(1)} %get-tuple-element.480), kind=kOutput, calls=%fused_computation.15 | convolution fusion | flops 5440536576 | bytes 16515072 | tf_op jit(solution)/shard_map/dot_general | solution.py:31
  138.8 15.5 %shard_map.280 = (bf16[768,768]{1,0:T(8,128)(2,1)}, bf16[768,768]{1,0:T(8,128)(2,1)}, bf16[768,768]{1,0:T(8,128)(2,1)}, bf16[768,768]{1,0:T(8,128)(2,1)}, f32[6,2,768]{2,1,0:T(2,128)}) custom-call(f32[768,2304]{1,0:T(8,128)} %fusion.13.qkv, f32[768,128]{1,0:T(8,128)} %get-tuple-element.487.cos_in, f32[768,128]{1,0:T(8,128)} %get-tuple-element.488.sin_in), custom_call_target="tpu_custom_call" | custom-call | flops 1048576 | bytes 16384 | tf_op jit(solution)/shard_map/pallas_call | solution.py:186
  154.6 3.0 convolution_convert_fusion
  158.9 3.3 fusion.29.kv_own
  170.7 15.8 %collective-permute-done.1 = bf16[384,1536]{1,0:T(8,128)(2,1)S(1)} collective-permute-done((bf16[384,1536]{1,0:T(8,128)(2,1)S(1)}, bf16[384,1536]{1,0:T(8,128)(2,1)S(1)}, u32[]{:S(2)}, u32[]{:S(2)}) %collective-permute-start.1) | collective-permute-done | bytes 1179680 | tf_op jit(solution)/shard_map/ppermute | solution.py:688
  187.8 8.2 %collective-permute-done.5.kv_peer = bf16[144,1536]{1,0:T(8,128)(2,1)S(1)} collective-permute-done((bf16[144,1536]{1,0:T(8,128)(2,1)S(1)}, bf16[144,1536]{1,0:T(8,128)(2,1)S(1)}, u32[]{:S(2)}, u32[]{:S(2)}) %collective-permute-start.5) | collective-permute-done | bytes 442400 | tf_op jit(solution)/shard_map/ppermute | solution.py:688
  197.9 3.6 fusion.48.q_own
  201.5 12.3 %shard_map.281 = (bf16[384,1536]{1,0:T(8,128)(2,1)}, f32[12,2,384]{2,1,0:T(2,128)}) custom-call(bf16[384,768]{1,0:T(8,128)(2,1)} %fusion.48.q_own, bf16[384,768]{1,0:T(8,128)(2,1)} %convolution_convert_fusion.1.q_peer, bf16[144,1536]{1,0:T(8,128)(2,1)} %copy-done.34, bf16[144,1536]{1,0:T(8,128)(2,1)} %copy-done.35), custom_call_target="tpu_custom_call" | custom-call | flops 1048576 | bytes 16384 | tf_op jit(solution)/shard_map/pallas_call | solution.py:270
  213.8 6.9 collective-permute-done.6
  220.7 3.0 convolution_add_fusion.1
  236.4 20.2 %collective-permute-done.14 = f32[8,128]{1,0:T(8,128)S(1)} collective-permute-done((f32[8,128]{1,0:T(8,128)S(1)}, f32[8,128]{1,0:T(8,128)S(1)}, u32[]{:S(2)}, u32[]{:S(2)}) %collective-permute-start.14) | collective-permute-done | bytes 4128 | tf_op jit(solution)/shard_map/ppermute | solution.py:688
  261.4 5.1 all-gather.5.cloned.1.call-done.weights
  266.5 11.6 %fusion.15.gate_in = bf16[768,3072]{1,0:T(8,128)(2,1)S(1)} fusion(bf16[1536,9216]{1,0:T(8,128)(2,1)} %all-gather.5.cloned.1.call-done.weights, bf16[384,1536]{1,0:T(8,128)(2,1)} %copy-done.7, bf16[384,1536]{1,0:T(8,128)(2,1)S(1)} %multiply_convert_fusion.refs_0_), kind=kOutput, calls=%fused_computation.17 | convolution fusion | flops 7254835200 | bytes 16515072 | tf_op jit(solution)/shard_map/dot_general | solution.py:31
  278.1 14.9 %fusion.64 = (bf16[768,3072]{1,0:T(8,128)(2,1)}, bf16[768,3072]{1,0:T(8,128)(2,1)}) fusion(bf16[768,3072]{1,0:T(8,128)(2,1)S(1)} %fusion.15.gate_in, bf16[1536,9216]{1,0:T(8,128)(2,1)} %all-gather.5.cloned.1.call-done.weights, bf16[384,1536]{1,0:T(8,128)(2,1)S(1)} %copy-done.8, bf16[384,1536]{1,0:T(8,128)(2,1)S(1)} %multiply_convert_fusion.refs_0_), kind=kOutput, calls=%fused_computation.180 | convolution fusion | flops 7271350272 | bytes 25952256 | tf_op jit(solution)/shard_map/dot_general | solution.py:31
  293.1 4.0 shard_map.284
  297.4 8.4 %fusion.26 = bf16[384,1536]{1,0:T(8,128)(2,1)S(1)} fusion(bf16[1536,9216]{1,0:T(8,128)(2,1)} %all-gather.5.cloned.1.call-done.weights, bf16[768,3072]{1,0:T(8,128)(2,1)} %get-tuple-element.421.refs_0_.refs_1_.refs_3_), kind=kOutput, calls=%fused_computation.34 | convolution fusion | flops 3624468480 | bytes 12976128 | tf_op jit(solution)/shard_map/dot_general | solution.py:31
  307.2 6.6 fusion.11
  313.8 20.2 %collective-permute-done.11 = bf16[384,1536]{1,0:T(8,128)(2,1)S(1)} collective-permute-done((bf16[384,1536]{1,0:T(8,128)(2,1)S(1)}, bf16[384,1536]{1,0:T(8,128)(2,1)S(1)}, u32[]{:S(2)}, u32[]{:S(2)}) %collective-permute-start.11) | collective-permute-done | bytes 1179680 | tf_op jit(solution)/shard_map/ppermute | solution.py:688
  339.3 12.7 %shard_map.285 = (bf16[384,3072]{1,0:T(8,128)(2,1)}, bf16[384,3072]{1,0:T(8,128)(2,1)}, bf16[2,384,1536]{2,1,0:T(8,128)(2,1)}) custom-call(s32[2]{0:T(128)} %pad_add_fusion.places, bf16[384,1536]{1,0:T(8,128)(2,1)} %copy-done.9, bf16[1536,9216]{1,0:T(8,128)(2,1)} %all-gather.5.cloned.1.call-done.weights, bf16[768,3072]{1,0:T(8,128)(2,1)} %copy-done.5, ...), custom_call_target="tpu_custom_call" | custom-call | flops 1048576 | bytes 16384 | tf_op jit(solution)/shard_map/pallas_call | solution.py:376
  352.0 14.2 %shard_map.286.refs_0_ = f32[384,1536]{1,0:T(8,128)} custom-call(bf16[384,3072]{1,0:T(8,128)(2,1)} %get-tuple-element.217.gate_in.refs_1_, bf16[384,3072]{1,0:T(8,128)(2,1)} %get-tuple-element.202.up_in.refs_1_, bf16[1536,9216]{1,0:T(8,128)(2,1)} %all-gather.5.cloned.1.call-done.weights), custom_call_target="tpu_custom_call" | custom-call | flops 1048576 | bytes 16384 | tf_op jit(solution)/shard_map/pallas_call | solution.py:606
  368.0 12.7 %shard_map.287 = (bf16[384,3072]{1,0:T(8,128)(2,1)}, bf16[384,3072]{1,0:T(8,128)(2,1)}, bf16[2,384,1536]{2,1,0:T(8,128)(2,1)}) custom-call(s32[2]{0:T(128)} %pad_add_fusion.places, bf16[384,1536]{1,0:T(8,128)(2,1)} %copy-done.26, bf16[1536,9216]{1,0:T(8,128)(2,1)} %all-gather.5.cloned.1.call-done.weights, bf16[768,3072]{1,0:T(8,128)(2,1)} %copy-done.5, ...), custom_call_target="tpu_custom_call" | custom-call | flops 1048576 | bytes 16384 | tf_op jit(solution)/shard_map/pallas_call | solution.py:376
  380.7 15.7 %shard_map.288 = (bf16[768,768]{1,0:T(8,128)(2,1)}, bf16[768,512]{1,0:T(8,128)(2,1)}, bf16[768,256]{1,0:T(8,128)(2,1)}, bf16[768,768]{1,0:T(8,128)(2,1)}, bf16[7...) custom-call(s32[2]{0:T(128)} %pad_add_fusion.places, bf16[384,1536]{1,0:T(8,128)(2,1)} %copy-done.9, ...), custom_call_target="tpu_custom_call" | custom-call | flops 1048576 | bytes 16384 | tf_op jit(solution)/shard_map/pallas_call | solution.py:456
  398.3 13.9 %shard_map.289 = bf16[384,1536]{1,0:T(8,128)(2,1)} custom-call(bf16[384,3072]{1,0:T(8,128)(2,1)} %get-tuple-element.221.gate_in.refs_3_, bf16[384,3072]{1,0:T(8,128)(2,1)} %get-tuple-element.230.up_in.refs_3_, bf16[1536,9216]{1,0:T(8,128)(2,1)} %all-gather.5.cloned.1.call-done.weights), custom_call_target="tpu_custom_call" | custom-call | flops 1048576 | bytes 16384 | tf_op jit(solution)/shard_map/pallas_call | solution.py:606
  413.6 15.7 %shard_map.290 = (bf16[768,1408]{1,0:T(8,128)(2,1)}, bf16[768,128]{1,0:T(8,128)(2,1)}, bf16[768,1408]{1,0:T(8,128)(2,1)}, bf16[768,128]{1,0:T(8,128)(2,1)}) custom-call(s32[2]{0:T(128)} %pad_add_fusion.places, bf16[384,1536]{1,0:T(8,128)(2,1)} %copy-done.6, bf16[384,3072]{1,0:T(8,128)(2,1)} %get-tuple-element.217.gate_in.refs_1_, ...), custom_call_target="tpu_custom_call" | custom-call | flops 1048576 | bytes 16384 | tf_op jit(solution)/shard_map/pallas_call | solution.py:456
  430.4 3.7 shard_map.292
  434.1 15.9 %shard_map.291 = (bf16[768,768]{1,0:T(8,128)(2,1)}, bf16[768,768]{1,0:T(8,128)(2,1)}, bf16[768,768]{1,0:T(8,128)(2,1)}, bf16[768,768]{1,0:T(8,128)(2,1)}) custom-call(s32[2]{0:T(128)} %pad_add_fusion.places, bf16[384,1536]{1,0:T(8,128)(2,1)} %copy-done.6, bf16[384,3072]{1,0:T(8,128)(2,1)} %get-tuple-element.202.up_in.refs_1_, bf16[384,1536]{1,0:T(8,128)(2,1)} %copy-done.7, ...), custom_call_target="tpu_custom_call" | custom-call | flops 1048576 | bytes 16384 | tf_op jit(solution)/shard_map/pallas_call | solution.py:456
  452.1 3.5 shard_map.298
  461.3 6.9 shard_map.293
  468.2 5.6 shard_map.294
  473.8 13.2 %shard_map.295 = (bf16[384,1536]{1,0:T(8,128)(2,1)}, bf16[144,3072]{1,0:T(8,128)(2,1)}) custom-call(bf16[384,768]{1,0:T(8,128)(2,1)} %fusion.48.q_own, bf16[384,768]{1,0:T(8,128)(2,1)} %convolution_convert_fusion.1.q_peer, bf16[384,768]{1,0:T(8,128)(2,1)} %get-tuple-element.241.g_own, bf16[384,768]{1,0:T(8,128)(2,1)} %get-tuple-element.242.g_peer, ...), custom_call_target="tpu_custom_call" | custom-call | flops 1048576 | bytes 16384 | tf_op jit(solution)/shard_map/pallas_call | solution.py:270
  487.0 7.0 shard_map.296.refs_0_
  494.0 6.7 shard_map.297
  500.8 4.5 shard_map.299
  513.2 3.2 shard_map.300.refs_0_
  516.5 15.8 %collective-permute-done.26.refs_1_.peer_in = bf16[384,1536]{1,0:T(8,128)(2,1)S(1)} collective-permute-done((bf16[384,1536]{1,0:T(8,128)(2,1)S(1)}, bf16[384,1536]{1,0:T(8,128)(2,1)S(1)}, u32[]{:S(2)}, u32[]{:S(2)}) %collective-permute-start.26) | collective-permute-done | bytes 1179680 | tf_op jit(solution)/shard_map/ppermute | solution.py:688
  533.3 3.2 shard_map.304.refs_0_
  536.5 3.7 shard_map.303
  542.6 7.1 shard_map.305
  549.7 3.4 shard_map.306
  557.2 44.4 %shard_map.307 = (bf16[768,2304]{1,0:T(8,128)(2,1)}, bf16[768,1152]{1,0:T(8,128)(2,1)}, f32[384,1536]{1,0:T(8,128)}, bf16[384,1536]{1,0:T(8,128)(2,1)}) custom-call(s32[2]{0:T(128)} %pad_add_fusion.places, bf16[768,768]{1,0:T(8,128)(2,1)} %get-tuple-element.195.q_in, bf16[768,768]{1,0:T(8,128)(2,1)} %get-tuple-element.196.k_in, ...), custom_call_target="tpu_custom_call" | custom-call | flops 1048576 | bytes 16384 | tf_op jit(solution)/shard_map/pallas_call | solution.py:220
  602.4 4.2 collective-permute-done.31.refs_4_
  606.6 4.5 shard_map.308
  616.4 11.4 %shard_map.309 = (bf16[768,512]{1,0:T(8,128)(2,1)}, bf16[768,640]{1,0:T(8,128)(2,1)}, bf16[768,512]{1,0:T(8,128)(2,1)}, bf16[768,640]{1,0:T(8,128)(2,1)}) custom-call(s32[2]{0:T(128)} %pad_add_fusion.places, bf16[768,1536]{1,0:T(8,128)(2,1)} %copy-done.12, bf16[768,2304]{1,0:T(8,128)(2,1)} %get-tuple-element.286.refs_1_, ...), custom_call_target="tpu_custom_call" | custom-call | flops 1048576 | bytes 16384 | tf_op jit(solution)/shard_map/pallas_call | solution.py:456
  634.0 3.4 shard_map.310.refs_0_
  639.9 7.8 collective-permute-done.34.refs_1_
  649.5 3.5 shard_map.313
  659.9 7.0 shard_map.314
  666.9 7.0 shard_map.315
  678.1 3.7 shard_map.317
  687.6 6.8 shard_map.320
  695.1 5.6 shard_map.321
  709.9 3.8 shard_map.322
  721.3 4.0 fusion.18
  725.5 11.6 %collective-permute-done.48.refs_1_ = bf16[768,768]{1,0:T(8,128)(2,1)S(1)} collective-permute-done((bf16[768,768]{1,0:T(8,128)(2,1)}, bf16[768,768]{1,0:T(8,128)(2,1)S(1)}, u32[]{:S(2)}, u32[]{:S(2)}) %collective-permute-start.48) | collective-permute-done | bytes 1179680 | tf_op jit(solution)/shard_map/ppermute | solution.py:694
  738.1 3.7 shard_map.323
  741.9 6.2 reduce-scatter.24.cloned.1.call-done
  758.4 3.9 collective-permute-done.46
  764.5 4.0 collective-permute-done.47
  770.5 8.8 %reduce-scatter.26.cloned.1.call-done = bf16[192,768]{1,0:T(8,128)(2,1)} async-done(((bf16[768,768]{1,0:T(8,128)(2,1)}), bf16[192,768]{1,0:T(8,128)(2,1)}) %reduce-scatter.26.cloned.1.call-update) | async-done | bytes 294928 | tf_op jit(solution)/shard_map/reduce_scatter | solution.py:830
  (391 shorter events, 151.9 us)
Async XLA Ops:
  7.2 111.2 %all-gather.3.cloned.1.call-start = ((), (), s32[]{:S(2)}) async-start(), calls=%async_computation.9 | async-start | bytes 20471808 | tf_op jit(solution)/shard_map/all_gather | solution.py:697
  14.7 251.7 %all-gather.5.cloned.1.call-start = ((), (), s32[]{:S(2)}) async-start(), calls=%async_computation.10 | async-start | bytes 30081024 | tf_op jit(solution)/shard_map/all_gather | solution.py:697
  19.0 481.7 %reduce-scatter.10.cloned.1.call-start = ((), (), s32[]{:S(2)}) async-start(), calls=%async_computation.11 | async-start | bytes 1474560 | tf_op jit(solution)/shard_map/reduce_scatter | solution.py:830
  19.1 29.0 %collective-permute-start = (bf16[384,1536]{1,0:T(8,128)(2,1)S(1)}, bf16[384,1536]{1,0:T(8,128)(2,1)S(1)}, u32[]{:S(2)}, u32[]{:S(2)}) collective-permute-start(bf16[384,1536]{1,0:T(8,128)(2,1)S(1)} %bitcast.35), channel_id=1, source_target_pairs={{0,1},{1,0},{2,3},{3,2},{4,5},{5,4},{6,7},{7,6},{8,9},{9,8},{10,11... | collective-permute-start | bytes 3538952 | tf_op jit(solution)/shard_map/ppermute | solution.py:688
  122.8 31.5 %collective-permute-start.3 = (bf16[768,768]{1,0:T(8,128)(2,1)}, bf16[768,768]{1,0:T(8,128)(2,1)}, u32[]{:S(2)}, u32[]{:S(2)}) collective-permute-start(bf16[768,768]{1,0:T(8,128)(2,1)} %get-tuple-element.419), channel_id=1, source_target_pairs={{0,1},{1,0},{2,3},{3,2},{4,5},{5,4},{6,7},{7,6},{8,9},{9,8},{10,11... | collective-permute-start | bytes 3538952 | tf_op jit(solution)/shard_map/ppermute | solution.py:688
  126.4 60.1 %collective-permute-start.2 = (bf16[768,1536]{1,0:T(8,128)(2,1)S(1)}, bf16[768,1536]{1,0:T(8,128)(2,1)}, u32[]{:S(2)}, u32[]{:S(2)}) collective-permute-start(bf16[768,1536]{1,0:T(8,128)(2,1)S(1)} %pad_maximum_fusion.refs_0_), channel_id=1, source_target_pairs={{0,2},{2,0},{1,3},{3,1},{4,6},{6,4},{5,7},{7,5},{8,10},{10,8},{9,1... | collective-permute-start | bytes 7077896 | tf_op jit(solution)/shard_map/ppermute | solution.py:691
  154.3 12.8 %collective-permute-start.4 = (bf16[768,768]{1,0:T(8,128)(2,1)}, bf16[768,768]{1,0:T(8,128)(2,1)}, u32[]{:S(2)}, u32[]{:S(2)}) collective-permute-start(bf16[768,768]{1,0:T(8,128)(2,1)} %collective-permute-done.3), channel_id=1, source_target_pairs={{0,2},{2,0},{1,3},{3,1},{4,6},{6,4},{5,7},{7,5},{8,10},{10,8},{9,1... | collective-permute-start | bytes 3538952 | tf_op jit(solution)/shard_map/ppermute | solution.py:691
  157.7 28.9 %collective-permute-start.1 = (bf16[384,1536]{1,0:T(8,128)(2,1)S(1)}, bf16[384,1536]{1,0:T(8,128)(2,1)S(1)}, u32[]{:S(2)}, u32[]{:S(2)}) collective-permute-start(bf16[384,1536]{1,0:T(8,128)(2,1)S(1)} %convolution_convert_fusion), channel_id=1, source_target_pairs={{0,1},{1,0},{2,3},{3,2},{4,5},{5,4},{6,7},{7,6},{8,9},{9,8},{10,11... | collective-permute-start | bytes 3538952 | tf_op jit(solution)/shard_map/ppermute | solution.py:688
  162.2 33.8 %collective-permute-start.5 = (bf16[144,1536]{1,0:T(8,128)(2,1)S(1)}, bf16[144,1536]{1,0:T(8,128)(2,1)S(1)}, u32[]{:S(2)}, u32[]{:S(2)}) collective-permute-start(bf16[144,1536]{1,0:T(8,128)(2,1)S(1)} %fusion.29.kv_own), channel_id=1, source_target_pairs={{0,1},{1,0},{2,3},{3,2},{4,5},{5,4},{6,7},{7,6},{8,9},{9,8},{10,11... | collective-permute-start | bytes 1327112 | tf_op jit(solution)/shard_map/ppermute | solution.py:688
  163.2 57.5 %collective-permute-start.6 = (bf16[768,768]{1,0:T(8,128)(2,1)}, bf16[768,768]{1,0:T(8,128)(2,1)}, u32[]{:S(2)}, u32[]{:S(2)}) collective-permute-start(bf16[768,768]{1,0:T(8,128)(2,1)} %get-tuple-element.418), channel_id=1, source_target_pairs={{0,1},{1,0},{2,3},{3,2},{4,5},{5,4},{6,7},{7,6},{8,9},{9,8},{10,11... | collective-permute-start | bytes 3538952 | tf_op jit(solution)/shard_map/ppermute | solution.py:688
  228.4 29.5 %collective-permute-start.8 = (bf16[384,1536]{1,0:T(8,128)(2,1)S(1)}, bf16[384,1536]{1,0:T(8,128)(2,1)S(1)}, u32[]{:S(2)}, u32[]{:S(2)}) collective-permute-start(bf16[384,1536]{1,0:T(8,128)(2,1)S(1)} %multiply_convert_fusion.refs_0_), channel_id=1, source_target_pairs={{0,1},{1,0},{2,3},{3,2},{4,5},{5,4},{6,7},{7,6},{8,9},{9,8},{10,11... | collective-permute-start | bytes 3538952 | tf_op jit(solution)/shard_map/ppermute | solution.py:688
  229.7 28.3 %collective-permute-start.10 = (bf16[144,1536]{1,0:T(8,128)(2,1)S(1)}, bf16[144,1536]{1,0:T(8,128)(2,1)}, u32[]{:S(2)}, u32[]{:S(2)}) collective-permute-start(bf16[144,1536]{1,0:T(8,128)(2,1)S(1)} %pad.9.refs_0_), channel_id=1, source_target_pairs={{0,2},{2,0},{1,3},{3,1},{4,6},{6,4},{5,7},{7,5},{8,10},{10,8},{9,1... | collective-permute-start | bytes 1327112 | tf_op jit(solution)/shard_map/ppermute | solution.py:691
  233.1 24.8 %collective-permute-start.9 = (bf16[768,384]{1,0:T(8,128)(2,1)}, bf16[768,384]{1,0:T(8,128)(2,1)S(1)}, u32[]{:S(2)}, u32[]{:S(2)}) collective-permute-start(bf16[768,384]{1,0:T(8,128)(2,1)} %shard_map.282), channel_id=1, source_target_pairs={{0,2},{2,0},{1,3},{3,1},{4,6},{6,4},{5,7},{7,5},{8,10},{10,8},{9,1... | collective-permute-start | bytes 1769480 | tf_op jit(solution)/shard_map/ppermute | solution.py:691
  235.5 21.1 %collective-permute-start.14 = (f32[8,128]{1,0:T(8,128)S(1)}, f32[8,128]{1,0:T(8,128)S(1)}, u32[]{:S(2)}, u32[]{:S(2)}) collective-permute-start(f32[8,128]{1,0:T(8,128)S(1)} %broadcast_in_dim.11), channel_id=1, source_target_pairs={{0,1},{1,0},{2,3},{3,2},{4,5},{5,4},{6,7},{7,6},{8,9},{9,8},{10,11... | collective-permute-start | bytes 12296 | tf_op jit(solution)/shard_map/ppermute | solution.py:688
  261.4 52.4 %collective-permute-start.12 = (bf16[768,1536]{1,0:T(8,128)(2,1)}, bf16[768,1536]{1,0:T(8,128)(2,1)S(1)}, u32[]{:S(2)}, u32[]{:S(2)}) collective-permute-start(bf16[768,1536]{1,0:T(8,128)(2,1)} %pad_maximum_fusion.3), channel_id=1, source_target_pairs={{0,2},{2,0},{1,3},{3,1},{4,6},{6,4},{5,7},{7,5},{8,10},{10,8},{9,1... | collective-permute-start | bytes 7077896 | tf_op jit(solution)/shard_map/ppermute | solution.py:691
  297.1 36.9 %collective-permute-start.13 = (bf16[768,1536]{1,0:T(8,128)(2,1)}, bf16[768,1536]{1,0:T(8,128)(2,1)}, u32[]{:S(2)}, u32[]{:S(2)}) collective-permute-start(bf16[768,1536]{1,0:T(8,128)(2,1)} %shard_map.284), channel_id=1, source_target_pairs={{0,2},{2,0},{1,3},{3,1},{4,6},{6,4},{5,7},{7,5},{8,10},{10,8},{9,1... | collective-permute-start | bytes 7077896 | tf_op jit(solution)/shard_map/ppermute | solution.py:691
  305.8 28.2 %collective-permute-start.11 = (bf16[384,1536]{1,0:T(8,128)(2,1)S(1)}, bf16[384,1536]{1,0:T(8,128)(2,1)S(1)}, u32[]{:S(2)}, u32[]{:S(2)}) collective-permute-start(bf16[384,1536]{1,0:T(8,128)(2,1)S(1)} %fusion.26), channel_id=1, source_target_pairs={{0,1},{1,0},{2,3},{3,2},{4,5},{5,4},{6,7},{7,6},{8,9},{9,8},{10,11... | collective-permute-start | bytes 3538952 | tf_op jit(solution)/shard_map/ppermute | solution.py:688
  337.9 28.2 %collective-permute-start.15 = (bf16[384,1536]{1,0:T(8,128)(2,1)S(1)}, bf16[384,1536]{1,0:T(8,128)(2,1)S(1)}, u32[]{:S(2)}, u32[]{:S(2)}) collective-permute-start(bf16[384,1536]{1,0:T(8,128)(2,1)S(1)} %get-tuple-element.414.g_in.refs_0_), channel_id=1, source_target_pairs={{0,1},{1,0},{2,3},{3,2},{4,5},{5,4},{6,7},{7,6},{8,9},{9,8},{10,11... | collective-permute-start | bytes 3538952 | tf_op jit(solution)/shard_map/ppermute | solution.py:688
  339.3 26.9 %collective-permute-start.16 = (bf16[384,1536]{1,0:T(8,128)(2,1)S(1)}, bf16[384,1536]{1,0:T(8,128)(2,1)S(1)}, u32[]{:S(2)}, u32[]{:S(2)}) collective-permute-start(bf16[384,1536]{1,0:T(8,128)(2,1)S(1)} %get-tuple-element.414.g_in.refs_0_), channel_id=1, source_target_pairs={{0,2},{2,0},{1,3},{3,1},{4,6},{6,4},{5,7},{7,5},{8,10},{10,8},{9,1... | collective-permute-start | bytes 3538952 | tf_op jit(solution)/shard_map/ppermute | solution.py:691
  367.2 13.5 %collective-permute-start.18 = (bf16[2,384,1536]{2,1,0:T(8,128)(2,1)}, bf16[2,384,1536]{2,1,0:T(8,128)(2,1)S(1)}, u32[]{:S(2)}, u32[]{:S(2)}) collective-permute-start(bf16[2,384,1536]{2,1,0:T(8,128)(2,1)} %get-tuple-element.208), channel_id=1, source_target_pairs={{0,2},{2,0},{1,3},{3,1},{4,6},{6,4},{5,7},{7,5},{8,10},{10,8},{9,1... | collective-permute-start | bytes 7077896 | tf_op jit(solution)/shard_map/ppermute | solution.py:691
  368.0 12.7 %collective-permute-start.17 = (bf16[384,1536]{1,0:T(8,128)(2,1)S(1)}, bf16[384,1536]{1,0:T(8,128)(2,1)}, u32[]{:S(2)}, u32[]{:S(2)}) collective-permute-start(bf16[384,1536]{1,0:T(8,128)(2,1)S(1)} %collective-permute-done.15.g_in.refs_2_), channel_id=1, source_target_pairs={{0,2},{2,0},{1,3},{3,1},{4,6},{6,4},{5,7},{7,5},{8,10},{10,8},{9,1... | collective-permute-start | bytes 3538952 | tf_op jit(solution)/shard_map/ppermute | solution.py:691
  396.4 15.7 %collective-permute-start.19 = (bf16[2,384,1536]{2,1,0:T(8,128)(2,1)}, bf16[2,384,1536]{2,1,0:T(8,128)(2,1)S(1)}, u32[]{:S(2)}, u32[]{:S(2)}) collective-permute-start(bf16[2,384,1536]{2,1,0:T(8,128)(2,1)} %get-tuple-element.219), channel_id=1, source_target_pairs={{0,2},{2,0},{1,3},{3,1},{4,6},{6,4},{5,7},{7,5},{8,10},{10,8},{9,1... | collective-permute-start | bytes 7077896 | tf_op jit(solution)/shard_map/ppermute | solution.py:691
  397.3 32.0 %collective-permute-start.20 = (bf16[768,768]{1,0:T(8,128)(2,1)}, bf16[768,768]{1,0:T(8,128)(2,1)S(1)}, u32[]{:S(2)}, u32[]{:S(2)}) collective-permute-start(bf16[768,768]{1,0:T(8,128)(2,1)} %get-tuple-element.228), channel_id=1, source_target_pairs={{0,4},{4,0},{1,5},{5,1},{2,6},{6,2},{3,7},{7,3},{8,12},{12,8},{9,1... | collective-permute-start | bytes 3538952 | tf_op jit(solution)/shard_map/ppermute | solution.py:694
  412.2 37.9 %collective-permute-start.22 = (bf16[384,1536]{1,0:T(8,128)(2,1)}, bf16[384,1536]{1,0:T(8,128)(2,1)}, u32[]{:S(2)}, u32[]{:S(2)}) collective-permute-start(bf16[384,1536]{1,0:T(8,128)(2,1)} %shard_map.289), channel_id=1, source_target_pairs={{0,1},{1,0},{2,3},{3,2},{4,5},{5,4},{6,7},{7,6},{8,9},{9,8},{10,11... | collective-permute-start | bytes 3538952 | tf_op jit(solution)/shard_map/ppermute | solution.py:688
  429.3 20.7 %collective-permute-start.21 = (bf16[768,512]{1,0:T(8,128)(2,1)}, bf16[768,512]{1,0:T(8,128)(2,1)S(1)}, u32[]{:S(2)}, u32[]{:S(2)}) collective-permute-start(bf16[768,512]{1,0:T(8,128)(2,1)} %get-tuple-element.238), channel_id=1, source_target_pairs={{0,4},{4,0},{1,5},{5,1},{2,6},{6,2},{3,7},{7,3},{8,12},{12,8},{9,1... | collective-permute-start | bytes 2359304 | tf_op jit(solution)/shard_map/ppermute | solution.py:694
  451.0 85.5 %reduce-scatter.12.cloned.1.call-start = ((), (), s32[]{:S(2)}) async-start(), calls=%async_computation.12 | async-start | bytes 983040 | tf_op jit(solution)/shard_map/reduce_scatter | solution.py:830
  451.0 49.7 %collective-permute-start.23 = (bf16[768,1408]{1,0:T(8,128)(2,1)}, bf16[768,1408]{1,0:T(8,128)(2,1)}, u32[]{:S(2)}, u32[]{:S(2)}) collective-permute-start(bf16[768,1408]{1,0:T(8,128)(2,1)} %get-tuple-element.253), channel_id=1, source_target_pairs={{0,4},{4,0},{1,5},{5,1},{2,6},{6,2},{3,7},{7,3},{8,12},{12,8},{9,1... | collective-permute-start | bytes 6488072 | tf_op jit(solution)/shard_map/ppermute | solution.py:694
  455.6 151.0 %reduce-scatter.14.cloned.1.call-start = ((), (), s32[]{:S(2)}) async-start(), calls=%async_computation.13 | async-start | bytes 2703360 | tf_op jit(solution)/shard_map/reduce_scatter | solution.py:830
  455.7 45.1 %collective-permute-start.24 = (bf16[384,1536]{1,0:T(8,128)(2,1)S(1)}, bf16[384,1536]{1,0:T(8,128)(2,1)}, u32[]{:S(2)}, u32[]{:S(2)}) collective-permute-start(bf16[384,1536]{1,0:T(8,128)(2,1)S(1)} %copy-done.25), channel_id=1, source_target_pairs={{0,1},{1,0},{2,3},{3,2},{4,5},{5,4},{6,7},{7,6},{8,9},{9,8},{10,11... | collective-permute-start | bytes 3538952 | tf_op jit(solution)/shard_map/ppermute | solution.py:688
  458.5 42.2 %collective-permute-start.25 = (bf16[384,768]{1,0:T(8,128)(2,1)}, bf16[384,768]{1,0:T(8,128)(2,1)}, u32[]{:S(2)}, u32[]{:S(2)}) collective-permute-start(bf16[384,768]{1,0:T(8,128)(2,1)} %slice.237), channel_id=1, source_target_pairs={{0,1},{1,0},{2,3},{3,2},{4,5},{5,4},{6,7},{7,6},{8,9},{9,8},{10,11... | collective-permute-start | bytes 1769480 | tf_op jit(solution)/shard_map/ppermute | solution.py:688
  505.3 144.2 %reduce-scatter.16.cloned.1.call-start = ((), (), s32[]{:S(2)}) async-start(), calls=%async_computation.14 | async-start | bytes 1474560 | tf_op jit(solution)/shard_map/reduce_scatter | solution.py:830
  505.4 26.9 %collective-permute-start.26 = (bf16[384,1536]{1,0:T(8,128)(2,1)S(1)}, bf16[384,1536]{1,0:T(8,128)(2,1)S(1)}, u32[]{:S(2)}, u32[]{:S(2)}) collective-permute-start(bf16[384,1536]{1,0:T(8,128)(2,1)S(1)} %copy-done.17), channel_id=1, source_target_pairs={{0,1},{1,0},{2,3},{3,2},{4,5},{5,4},{6,7},{7,6},{8,9},{9,8},{10,11... | collective-permute-start | bytes 3538952 | tf_op jit(solution)/shard_map/ppermute | solution.py:688
  506.2 26.6 %collective-permute-start.27 = (bf16[768,768]{1,0:T(8,128)(2,1)}, bf16[768,768]{1,0:T(8,128)(2,1)}, u32[]{:S(2)}, u32[]{:S(2)}) collective-permute-start(bf16[768,768]{1,0:T(8,128)(2,1)} %get-tuple-element.260), channel_id=1, source_target_pairs={{0,4},{4,0},{1,5},{5,1},{2,6},{6,2},{3,7},{7,3},{8,12},{12,8},{9,1... | collective-permute-start | bytes 3538952 | tf_op jit(solution)/shard_map/ppermute | solution.py:694
  536.5 4.7 collective-permute-start.28
  553.0 53.6 %collective-permute-start.31 = (bf16[768,1536]{1,0:T(8,128)(2,1)}, bf16[768,1536]{1,0:T(8,128)(2,1)}, u32[]{:S(2)}, u32[]{:S(2)}) collective-permute-start(bf16[768,1536]{1,0:T(8,128)(2,1)} %shard_map.306), channel_id=1, source_target_pairs={{0,4},{4,0},{1,5},{5,1},{2,6},{6,2},{3,7},{7,3},{8,12},{12,8},{9,1... | collective-permute-start | bytes 7077896 | tf_op jit(solution)/shard_map/ppermute | solution.py:694
  553.9 124.1 %reduce-scatter.18.cloned.1.call-start = ((), (), s32[]{:S(2)}) async-start(), calls=%async_computation.15 | async-start | bytes 2949120 | tf_op jit(solution)/shard_map/reduce_scatter | solution.py:830
  554.0 47.6 %collective-permute-start.29 = (bf16[384,1536]{1,0:T(8,128)(2,1)S(1)}, bf16[384,1536]{1,0:T(8,128)(2,1)S(1)}, u32[]{:S(2)}, u32[]{:S(2)}) collective-permute-start(bf16[384,1536]{1,0:T(8,128)(2,1)S(1)} %copy-done.16), channel_id=1, source_target_pairs={{0,1},{1,0},{2,3},{3,2},{4,5},{5,4},{6,7},{7,6},{8,9},{9,8},{10,11... | collective-permute-start | bytes 3538952 | tf_op jit(solution)/shard_map/ppermute | solution.py:688
  556.2 45.4 %collective-permute-start.30 = (bf16[384,768]{1,0:T(8,128)(2,1)}, bf16[384,768]{1,0:T(8,128)(2,1)S(1)}, u32[]{:S(2)}, u32[]{:S(2)}) collective-permute-start(bf16[384,768]{1,0:T(8,128)(2,1)} %get-tuple-element.428), channel_id=1, source_target_pairs={{0,1},{1,0},{2,3},{3,2},{4,5},{5,4},{6,7},{7,6},{8,9},{9,8},{10,11... | collective-permute-start | bytes 1769480 | tf_op jit(solution)/shard_map/ppermute | solution.py:688
  611.2 107.6 %reduce-scatter.20.cloned.1.call-start = ((), (), s32[]{:S(2)}) async-start(), calls=%async_computation.16 | async-start | bytes 983040 | tf_op jit(solution)/shard_map/reduce_scatter | solution.py:830
  611.2 4.0 collective-permute-start.32
  611.3 28.6 %collective-permute-start.33 = (bf16[384,1536]{1,0:T(8,128)(2,1)}, bf16[384,1536]{1,0:T(8,128)(2,1)S(1)}, u32[]{:S(2)}, u32[]{:S(2)}) collective-permute-start(bf16[384,1536]{1,0:T(8,128)(2,1)} %get-tuple-element.299), channel_id=1, source_target_pairs={{0,1},{1,0},{2,3},{3,2},{4,5},{5,4},{6,7},{7,6},{8,9},{9,8},{10,11... | collective-permute-start | bytes 3538952 | tf_op jit(solution)/shard_map/ppermute | solution.py:688
  627.8 19.9 %collective-permute-start.34 = (bf16[768,512]{1,0:T(8,128)(2,1)}, bf16[768,512]{1,0:T(8,128)(2,1)}, u32[]{:S(2)}, u32[]{:S(2)}) collective-permute-start(bf16[768,512]{1,0:T(8,128)(2,1)} %get-tuple-element.295), channel_id=1, source_target_pairs={{0,4},{4,0},{1,5},{5,1},{2,6},{6,2},{3,7},{7,3},{8,12},{12,8},{9,1... | collective-permute-start | bytes 2359304 | tf_op jit(solution)/shard_map/ppermute | solution.py:694
  647.8 11.3 %collective-permute-start.38 = (bf16[768,1536]{1,0:T(8,128)(2,1)S(1)}, bf16[768,1536]{1,0:T(8,128)(2,1)}, u32[]{:S(2)}, u32[]{:S(2)}) collective-permute-start(bf16[768,1536]{1,0:T(8,128)(2,1)S(1)} %copy-done.13), channel_id=1, source_target_pairs={{0,2},{2,0},{1,3},{3,1},{4,6},{6,4},{5,7},{7,5},{8,10},{10,8},{9,1... | collective-permute-start | bytes 7077896 | tf_op jit(solution)/shard_map/ppermute | solution.py:691
  647.8 12.1 %collective-permute-start.35 = (bf16[768,1536]{1,0:T(8,128)(2,1)}, bf16[768,1536]{1,0:T(8,128)(2,1)}, u32[]{:S(2)}, u32[]{:S(2)}) collective-permute-start(bf16[768,1536]{1,0:T(8,128)(2,1)} %shard_map.310.refs_0_), channel_id=1, source_target_pairs={{0,2},{2,0},{1,3},{3,1},{4,6},{6,4},{5,7},{7,5},{8,10},{10,8},{9,1... | collective-permute-start | bytes 7077896 | tf_op jit(solution)/shard_map/ppermute | solution.py:691
  648.3 9.4 %collective-permute-start.37 = (bf16[768,384]{1,0:T(8,128)(2,1)}, bf16[768,384]{1,0:T(8,128)(2,1)}, u32[]{:S(2)}, u32[]{:S(2)}) collective-permute-start(bf16[768,384]{1,0:T(8,128)(2,1)} %shard_map.312), channel_id=1, source_target_pairs={{0,2},{2,0},{1,3},{3,1},{4,6},{6,4},{5,7},{7,5},{8,10},{10,8},{9,1... | collective-permute-start | bytes 1769480 | tf_op jit(solution)/shard_map/ppermute | solution.py:691
  648.3 28.1 %collective-permute-start.39 = (bf16[768,640]{1,0:T(8,128)(2,1)}, bf16[768,640]{1,0:T(8,128)(2,1)}, u32[]{:S(2)}, u32[]{:S(2)}) collective-permute-start(bf16[768,640]{1,0:T(8,128)(2,1)} %get-tuple-element.324), channel_id=1, source_target_pairs={{0,4},{4,0},{1,5},{5,1},{2,6},{6,2},{3,7},{7,3},{8,12},{12,8},{9,1... | collective-permute-start | bytes 2949128 | tf_op jit(solution)/shard_map/ppermute | solution.py:694
  653.0 65.8 %reduce-scatter.22.cloned.1.call-start = ((), (), s32[]{:S(2)}) async-start(), calls=%async_computation.17 | async-start | bytes 1228800 | tf_op jit(solution)/shard_map/reduce_scatter | solution.py:830
  653.1 6.0 collective-permute-start.36
  657.7 18.6 %collective-permute-start.40 = (bf16[144,1536]{1,0:T(8,128)(2,1)}, bf16[144,1536]{1,0:T(8,128)(2,1)}, u32[]{:S(2)}, u32[]{:S(2)}) collective-permute-start(bf16[144,1536]{1,0:T(8,128)(2,1)} %slice.300), channel_id=1, source_target_pairs={{0,1},{1,0},{2,3},{3,2},{4,5},{5,4},{6,7},{7,6},{8,9},{9,8},{10,11... | collective-permute-start | bytes 1327112 | tf_op jit(solution)/shard_map/ppermute | solution.py:688
  676.3 28.0 %collective-permute-start.42 = (bf16[768,768]{1,0:T(8,128)(2,1)}, bf16[768,768]{1,0:T(8,128)(2,1)S(1)}, u32[]{:S(2)}, u32[]{:S(2)}) collective-permute-start(bf16[768,768]{1,0:T(8,128)(2,1)} %shard_map.316), channel_id=1, source_target_pairs={{0,4},{4,0},{1,5},{5,1},{2,6},{6,2},{3,7},{7,3},{8,12},{12,8},{9,1... | collective-permute-start | bytes 3538952 | tf_op jit(solution)/shard_map/ppermute | solution.py:694
  686.1 8.3 %collective-permute-start.41 = (bf16[144,768]{1,0:T(8,128)(2,1)}, bf16[144,768]{1,0:T(8,128)(2,1)S(1)}, u32[]{:S(2)}, u32[]{:S(2)}) collective-permute-start(bf16[144,768]{1,0:T(8,128)(2,1)} %shard_map.319), channel_id=1, source_target_pairs={{0,2},{2,0},{1,3},{3,1},{4,6},{6,4},{5,7},{7,5},{8,10},{10,8},{9,1... | collective-permute-start | bytes 663560 | tf_op jit(solution)/shard_map/ppermute | solution.py:691
  687.5 60.5 %reduce-scatter.24.cloned.1.call-start = ((), (), s32[]{:S(2)}) async-start(), calls=%async_computation.18 | async-start | bytes 1474560 | tf_op jit(solution)/shard_map/reduce_scatter | solution.py:830
  706.3 9.0 %collective-permute-start.56 = (bf16[96,1536]{1,0:T(8,128)(2,1)}, bf16[96,1536]{1,0:T(8,128)(2,1)}, u32[]{:S(2)}, u32[]{:S(2)}) collective-permute-start(bf16[96,1536]{1,0:T(8,128)(2,1)} %constant_dynamic-slice_fusion.1), channel_id=1, source_target_pairs={{0,2},{2,0},{1,3},{3,1},{4,6},{6,4},{5,7},{7,5},{8,10},{10,8},{9,1... | collective-permute-start | bytes 884744 | tf_op jit(solution)/shard_map/ppermute | solution.py:691
  707.1 9.4 %collective-permute-start.55 = (bf16[96,1536]{1,0:T(8,128)(2,1)}, bf16[96,1536]{1,0:T(8,128)(2,1)}, u32[]{:S(2)}, u32[]{:S(2)}) collective-permute-start(bf16[96,1536]{1,0:T(8,128)(2,1)} %fusion.56), channel_id=1, source_target_pairs={{0,2},{2,0},{1,3},{3,1},{4,6},{6,4},{5,7},{7,5},{8,10},{10,8},{9,1... | collective-permute-start | bytes 884744 | tf_op jit(solution)/shard_map/ppermute | solution.py:691
  707.6 6.1 collective-permute-start.51
  708.4 10.2 %collective-permute-start.54 = (bf16[96,1536]{1,0:T(8,128)(2,1)}, bf16[96,1536]{1,0:T(8,128)(2,1)S(1)}, u32[]{:S(2)}, u32[]{:S(2)}) collective-permute-start(bf16[96,1536]{1,0:T(8,128)(2,1)} %fusion.54), channel_id=1, source_target_pairs={{0,2},{2,0},{1,3},{3,1},{4,6},{6,4},{5,7},{7,5},{8,10},{10,8},{9,1... | collective-permute-start | bytes 884744 | tf_op jit(solution)/shard_map/ppermute | solution.py:691
  708.9 28.2 %collective-permute-start.48 = (bf16[768,768]{1,0:T(8,128)(2,1)}, bf16[768,768]{1,0:T(8,128)(2,1)S(1)}, u32[]{:S(2)}, u32[]{:S(2)}) collective-permute-start(bf16[768,768]{1,0:T(8,128)(2,1)} %get-tuple-element.350), channel_id=1, source_target_pairs={{0,4},{4,0},{1,5},{5,1},{2,6},{6,2},{3,7},{7,3},{8,12},{12,8},{9,1... | collective-permute-start | bytes 3538952 | tf_op jit(solution)/shard_map/ppermute | solution.py:694
  718.8 60.5 %reduce-scatter.26.cloned.1.call-start = ((), (), s32[]{:S(2)}) async-start(), calls=%async_computation.19 | async-start | bytes 1474560 | tf_op jit(solution)/shard_map/reduce_scatter | solution.py:830
  721.2 4.1 collective-permute-start.50
  748.0 4.1 collective-permute-start.43
  749.5 13.2 %collective-permute-start.49 = (bf16[130,1536]{1,0:T(8,128)(2,1)S(1)}, bf16[130,1536]{1,0:T(8,128)(2,1)S(1)}, u32[]{:S(2)}, u32[]{:S(2)}) collective-permute-start(bf16[130,1536]{1,0:T(8,128)(2,1)S(1)} %slice.417), channel_id=1, source_target_pairs={{0,1},{1,0},{2,3},{3,2},{4,5},{5,4},{6,7},{7,6},{8,9},{9,8},{10,11... | collective-permute-start | bytes 1198088 | tf_op jit(solution)/shard_map/ppermute | solution.py:688
  757.3 5.0 collective-permute-start.46
  758.3 12.0 %collective-permute-start.52 = (bf16[96,768]{1,0:T(8,128)(2,1)S(1)}, bf16[96,768]{1,0:T(8,128)(2,1)S(1)}, u32[]{:S(2)}, u32[]{:S(2)}) collective-permute-start(bf16[96,768]{1,0:T(8,128)(2,1)S(1)} %constant_dynamic-slice_fusion.3), channel_id=1, source_target_pairs={{0,2},{2,0},{1,3},{3,1},{4,6},{6,4},{5,7},{7,5},{8,10},{10,8},{9,1... | collective-permute-start | bytes 442376 | tf_op jit(solution)/shard_map/ppermute | solution.py:691
  762.3 6.2 collective-permute-start.47
  (76 other events, 641.4 us)
Sparse Core Ops, SparseCore 0:
  14.9 103.4 all-gather.2
  120.0 146.4 all-gather.4
  451.1 28.7 reduce-scatter.9
  482.0 22.0 reduce-scatter.11
  506.2 44.1 reduce-scatter.13
  554.0 29.1 reduce-scatter.15
  611.3 47.7 reduce-scatter.17
  661.6 22.7 reduce-scatter.19
  687.6 26.0 reduce-scatter.21
  719.0 28.9 reduce-scatter.23
  750.3 28.9 reduce-scatter.25

commit v4 on v3

--- a/solution.py
+++ b/solution.py
@@ -18,7 +18,7 @@
 PACK_VMEM = 60 << 20
 GRAD_VMEM = 60 << 20
 BACK_VMEM = 60 << 20
-DOWN_PIECES = (768, 512, 256)
+DOWN_PIECES = (896, 640)
 GATE_PIECES = (1408, 128)
 UP_PIECES = (768, 768)
 PULL_ROWS = 256
@@ -804,10 +804,11 @@
     up_sum = dot(input_three, weight_up, 1, 0)
     gate_sum = gate_pre.astype(F32)
     hidden_ff = (gate_sum * jax.nn.sigmoid(gate_sum) * up_sum).astype(BF16)
+    core_own_two = to_core(own_two)
     up_pre = up_sum.astype(BF16)
     core_three = to_core(input_three)
     core_hidden = to_core(other_half(places, ff_width, hidden_ff))
-    block_out = hidden_two + project(hidden_ff, weight_down, 1, core_three, core_hidden)
+    block_out = hidden_two + project(hidden_ff, weight_down, 1, core_three, core_hidden, core_own_two)
 
     error_diff = block_out - teacher[0].astype(F32)
     local_error = jnp.sum(mask_float[:, None] * error_diff * error_diff)
@@ -865,12 +866,18 @@
         (core_own_e3, (core_hidden, 0), 0),
         (core_peer_e3, (core_hidden, 1), 0),
     )
-    *sent_down, dgate_peer, dup_peer, halves_peer = meet(
-        *sent_down, dgate_peer, dup_peer, halves_peer
+    *sent_down, dgate_peer, dup_peer, halves_peer, peer_mixed = meet(
+        *sent_down,
+        dgate_peer,
+        dup_peer,
+        halves_peer,
+        to_peer(after(mixed_cross, dgate_peer)[:, heads_width:]),
     )
     near_a = to_near(sent_down[0])
-    pulled_peer, core_peer_halves = meet(
-        pull(dgate_peer, dup_peer, gath_b, BF16), to_core(halves_peer)
+    half_mixed = other_half(places, heads_width, mixed_cross, peer_mixed)
+    peer_two = to_peer(after(own_two, half_mixed))
+    pulled_peer, core_peer_halves, core_mixed = meet(
+        pull(dgate_peer, dup_peer, gath_b, BF16), to_core(halves_peer), to_core(half_mixed)
     )
     away = to_peer(pulled_peer)
 
@@ -888,16 +895,15 @@
         *feed_grad(GATE_PIECES, dgate_own, after(dgate_peer, pulled_peer), 0), near_a
     )
     near_b = to_near(after(sent_down[1], near_a))
-    *up_w, sum_a, near_b, away = meet(
+    *up_w, sum_a, near_b, peer_two, away = meet(
         *feed_grad(UP_PIECES, dup_own, after(dup_peer, gate_w[0]), 1),
         add_pair(kept_down[:1], near_a),
         near_b,
+        peer_two,
         away,
     )
     scat_down = [scatter_on(sum_a)]
     near_c = to_near(after(gate_w[2], near_b))
-    peer_two = to_peer(after(own_two, away))
-    peer_mixed = to_peer(after(mixed_cross, away)[:, heads_width:])
     grad_two, own_e2, gain_three = norm_back(pulled_own, away, hidden_two, row(2), grad_out)
 
     grad_mixed = mixed_back(own_e2, gath_a, 7, cross_o_peer)
@@ -907,40 +913,41 @@
     sum_b = add_pair(kept_down[1:2], near_b)
     scat_down.append(scatter_on(sum_b))
     sent_d = up_w[2]
-    grad_one, own_e1, gain_two, sum_b, own_e2, sent_d, near_c, peer_two, peer_mixed = meet(
-        grad_one, own_e1, gain_two, sum_b, own_e2, sent_d, near_c, peer_two, peer_mixed
-    )
-
-    near_d = to_near(sent_d)
-    peer_e1 = to_peer(own_e1)
-    input_two = join(0, own_two, peer_two)
-    mixed_two = join(0, mixed_cross[:, :heads_width], peer_mixed)
-    sum_c = add_pair(gate_w[:1], near_c)
-    scat_gate = [scatter_on(sum_c)]
-    sum_c, peer_e1, near_d, input_two, mixed_two, half_mixed = meet(
-        sum_c,
-        peer_e1,
-        near_d,
-        input_two,
-        mixed_two,
-        other_half(places, heads_width, mixed_two),
-    )
-    own_e2, grad_qc, _ = meet(own_e2, grad_qc, peer_e1)
+    grad_one, own_e1, gain_two, sum_b, own_e2, peer_e2, core_own_e2, near_c = meet(
+        grad_one, own_e1, gain_two, sum_b, own_e2, to_peer(own_e2), to_core(own_e2), near_c
+    )
 
     def head_grad(*parts):
         kept, sent = grad_of((half_heads,), *parts)
         return kept[0], sent[0]
 
+    near_d = to_near(sent_d)
+    peer_e1 = to_peer(own_e1)
+    sum_c = add_pair(gate_w[:1], near_c)
+    scat_gate = [scatter_on(sum_c)]
+    core_peer_e2 = to_core(peer_e2)
+    kept_co, sent_co = head_grad(
+        (own_e2, mixed_cross, None),
+        (peer_e2, peer_mixed, None),
+        (core_own_e2, (core_mixed, 0), 0),
+        (core_peer_e2, (core_mixed, 1), 0),
+    )
+    sum_c, peer_e1, near_d, core_own_e1, kept_co, sent_co = meet(
+        sum_c, peer_e1, near_d, to_core(own_e1), kept_co, sent_co
+    )
+    grad_qc, grad_kv, _ = meet(grad_qc, grad_kv, peer_e1)
     sum_d = add_pair([up_w[0]], near_d)
     mid = scatter_on(sum_d)
-    branch_one = join(0, own_e1, peer_e1)
-    sum_d, core_e1, branch_one = meet(sum_d, to_core(branch_one), branch_one)
+    sum_d, core_peer_e1 = meet(sum_d, to_core(peer_e1))
     kept_wo, sent_wo = head_grad(
-        (branch_one, mixed_self, None), (core_e1, core_mixed_self, 0)
-    )
-    kept_wo, sent_e = meet(kept_wo, join(1, up_w[3], sent_down[2], gate_w[3], sent_wo))
+        (own_e1, (mixed_self, 0), None),
+        (peer_e1, (mixed_self, 1), None),
+        (core_own_e1, (core_mixed_self, 0), 0),
+        (core_peer_e1, (core_mixed_self, 1), 0),
+    )
+    kept_wo, sent_e = meet(kept_wo, join(1, up_w[3], gate_w[3], sent_wo))
     near_e = to_near(sent_e)
-    grad_qkv, halves_qkv, pulled_own, pulled_peer, peer_e2, peer_qc, near_e = meet(
+    grad_qkv, halves_qkv, pulled_own, pulled_peer, peer_qc, peer_kv, near_e = meet(
         *self_back(
             places,
             query_self,
@@ -953,74 +960,61 @@
             cosines,
             sines,
         ),
-        to_peer(own_e2),
         to_peer(grad_qc[:, heads_width:]),
+        to_peer(grad_kv[:, 2 * heads_width :]),
         near_e,
     )
+    near_co = to_near(after(sent_co, near_e))
     away = to_peer(pulled_peer)
-    sum_e = add_pair([up_w[1], kept_down[2], gate_w[1], kept_wo], near_e)
+    sum_e = add_pair([up_w[1], gate_w[1], kept_wo], near_e)
     last_ff = scatter_on(sum_e)
     sum_e, core_qkv = meet(sum_e, to_core(halves_qkv))
-    piece = 3 * half_heads // 2 // PAIR * PAIR
     kept_qkv, sent_qkv = grad_of(
-        (piece, 3 * half_heads - piece),
-        (input_one, after(grad_qkv, sum_e), None),
-        (core_one, core_qkv, 0),
-    )
-    *kept_qkv, sent_f, sent_g = meet(*kept_qkv, *sent_qkv)
+        (3 * half_heads,), (input_one, after(grad_qkv, sum_e), None), (core_one, core_qkv, 0)
+    )
+    kept_qkv, sent_f, near_co = meet(kept_qkv[0], sent_qkv[0], near_co)
     near_f = to_near(sent_f)
-    both_qc = join(0, grad_qc[:, :heads_width], after(peer_qc, sent_f))
-    branch_two, both_qc, half_qc, away, near_f = meet(
-        join(0, own_e2, after(peer_e2, sent_f)),
-        both_qc,
-        other_half(places, heads_width, both_qc),
-        away,
-        near_f,
-    )
-    near_g = to_near(sent_g)
-    sum_f = add_pair([kept_qkv[0]], near_f)
-    scat_qkv = [scatter_on(sum_f)]
-    core_e2, core_qc, core_two, core_mixed = (
-        to_core(after(part, branch_two)) for part in (branch_two, half_qc, input_two, half_mixed)
-    )
-    sum_f, core_e2, core_mixed, core_qc, core_two = meet(
-        sum_f, core_e2, core_mixed, core_qc, core_two
-    )
-    peer_kv = to_peer(after(grad_kv, sum_f)[:, 2 * heads_width :])
-    kept_co, sent_co = head_grad((branch_two, mixed_two, None), (core_e2, core_mixed, 0))
+    sum_co = add_pair([kept_co], near_co)
+    scat_co = scatter_on(sum_co)
+    sum_kv = near_sum([grad_kv[:, : 2 * heads_width]], after(peer_kv, sent_f))
+    sum_kv, half_kv, half_qc = meet(
+        sum_kv,
+        other_half(places, 2 * heads_width, sum_kv),
+        other_half(places, heads_width, grad_qc, after(peer_qc, sent_f)),
+    )
+    sum_co, core_kv, core_qc, core_peer_two = meet(
+        sum_co, to_core(half_kv), to_core(half_qc), to_core(after(peer_two, half_qc))
+    )
     kept_cq, sent_cq = head_grad(
-        (input_two, after(both_qc, sent_co), None), (core_two, core_qc, 0)
-    )
-    kept_co, kept_cq, sent_w, near_g, peer_kv = meet(
-        kept_co, kept_cq, join(1, sent_co, sent_cq), near_g, peer_kv
+        (own_two, after(grad_qc, sum_co), None),
+        (peer_two, peer_qc, None),
+        (core_own_two, (core_qc, 0), 0),
+        (core_peer_two, (core_qc, 1), 0),
+    )
+    kept_ckv, sent_ckv = grad_of(
+        (heads_width,), (cond_rows, after(sum_kv, sent_cq), None), (core_cond, core_kv, 0)
+    )
+    kept_cq, kept_ckv, sent_w, near_f = meet(
+        kept_cq, kept_ckv[0], join(1, sent_cq, sent_ckv[0]), near_f
     )
     near_w = to_near(sent_w)
-    sum_g = add_pair([kept_qkv[1]], near_g)
-    scat_qkv.append(scatter_on(sum_g))
-    sum_kv = near_sum([grad_kv[:, : 2 * heads_width]], after(peer_kv, sum_g))
-    sum_kv, half_kv = meet(sum_kv, other_half(places, 2 * heads_width, sum_kv))
+    sum_f = add_pair([kept_qkv], near_f)
+    scat_qkv = scatter_on(sum_f)
+    cond_part = dot(after(sum_kv, sum_f), cross_kv, 1, 1)[:ctx_len].astype(BF16)
     grad_rows, _, gain_one = norm_back(
-        pulled_own, after(away, half_kv), x_bf, row(0), grad_one
-    )
-    grad_rows, gain_one, core_kv = meet(grad_rows, gain_one, to_core(half_kv))
-    kept_ckv, sent_ckv = grad_of(
-        (heads_width,), (cond_rows, after(sum_kv, grad_rows), None), (core_cond, core_kv, 0)
-    )
-    kept_ckv, sent_ckv, near_w, last_ff = meet(kept_ckv[0], sent_ckv[0], near_w, last_ff)
-    near_c = to_near(sent_ckv)
-    sum_w, *scat_qkv = meet(near_sum([kept_co, kept_cq], near_w), *scat_qkv)
+        pulled_own, after(away, sum_f), x_bf, row(0), grad_one
+    )
+    near_w, cond_part, last_ff, scat_co, grad_rows, gain_one = meet(
+        near_w, cond_part, last_ff, scat_co, grad_rows, gain_one
+    )
+    cond_sum = cond_part.astype(F32) + to_peer(cond_part).astype(F32)
+    sum_w = near_sum([kept_cq, kept_ckv], near_w)
     scat_w = scatter(sum_w)
-    cond_part = dot(after(sum_kv, sum_w), cross_kv, 1, 1)[:ctx_len].astype(BF16)
-    near_c, cond_part = meet(near_c, cond_part)
-    cond_sum = cond_part.astype(F32) + to_peer(cond_part).astype(F32)
-    sum_c = near_sum([kept_ckv], near_c)
-    scat_c = scatter(sum_c)
 
     small = jnp.concatenate(
-        [gain_one, gain_two, gain_three, jnp.full((1, width), local_error, F32)],
-        axis=0,
-    )
-    small = after(small, scat_w)
+        [gain_one, gain_two, gain_three, jnp.full((1, width), local_error, F32)], axis=0
+    )
+    small = after(small, sum_w)
     for axis in ("tensor", "core", "near", "far"):
         size = lax.axis_size(axis)
         if size & (size - 1):
@@ -1034,27 +1028,26 @@
     place = (lax.axis_index("far") * 4 + near_at * 2 + pair) * slab
     grad_gains = lax.dynamic_slice(small, (0, place), (3, slab))
 
-    ends = (
-        UP_PIECES[1],
-        UP_PIECES[1] + DOWN_PIECES[2],
-        UP_PIECES[1] + DOWN_PIECES[2] + GATE_PIECES[1],
-    )
-    gate_parts = scat_gate + [last_ff[:, ends[1] : ends[2]]]
+    ends = (UP_PIECES[1], UP_PIECES[1] + GATE_PIECES[1])
+    gate_parts = scat_gate + [last_ff[:, ends[0] : ends[1]]]
     up_parts = [mid, last_ff[:, : ends[0]]]
-    down_parts = scat_down + [last_ff[:, ends[0] : ends[1]]]
+    down_parts = scat_down
     down_t, gate_s, up_s = (
         jnp.concatenate(finish(jnp.concatenate(parts, axis=1)), axis=1)
         for parts in (down_parts, gate_parts, up_parts)
     )
-    sides = finish(jnp.concatenate(scat_qkv, axis=1))
+    sides = finish(scat_qkv)
     q_s, k_s, v_s = (
         columns_at(sides, range(i * PAIR, 3 * half_heads, 3 * PAIR), PAIR) for i in range(3)
     )
-    out_t = jnp.concatenate(finish(last_ff[:, ends[2] :]), axis=1)
+    out_t = jnp.concatenate(finish(last_ff[:, ends[1] :]), axis=1)
+    co_t = jnp.concatenate(finish(scat_co), axis=1)
     sides = finish(scat_w)
-    co_t, cq_s = (columns_at(sides, [i * half_heads], half_heads) for i in range(2))
-    sides = finish(scat_c)
-    ck_s, cv_s = (columns_at(sides, range(i * PAIR, heads_width, 2 * PAIR), PAIR) for i in range(2))
+    cq_s = columns_at(sides, [0], half_heads)
+    ck_s, cv_s = (
+        columns_at(sides, range(half_heads + i * PAIR, 3 * half_heads, 2 * PAIR), PAIR)
+        for i in range(2)
+    )
     return (
         block_out.astype(BF16)[None],
         mean_loss,

time: 800 us -> 782 us (0.978)
  Pallas kernels: 334 us -> 318 us
    pallas_call x7 -> x2, Pallas kernels: 20.3 us -> 5.91 us  [whole_call(): pl.pallas_call(kernel, out_shape=out_shape, compiler_params=pltpu.Compile...]
    ppermute x9 -> x8, waiting for transfers between devices: 26.3 us -> 36 us  [to_near(): return lax.ppermute(values, 'near', swap)]
    unnamed x158 -> x156, local copies, waits for them, and re-layouts: 19.1 us -> 22.3 us
    pallas_call x10 -> x9, Pallas kernels: 36.8 us -> 33.7 us  [near_sum(): pl.pallas_call(near_sum_kernel, grid=(rows // block,), in_specs=[spec(par...]
  transfers between devices with their start and end apart: 68 -> 69, of which waited for: 25 -> 26; matrix products, arithmetic and copies ran while one was open for 16% -> 15% of each run, Pallas kernels for 40% -> 41%
where the time goes in v4:
time: 782 us; the launch traced here: 774 us
  Pallas kernels  318 us (41%)
  waiting for transfers between devices  253 us (32%)
  matrix products  78.5 us (10%)
  starting transfers between devices  39 us (5%)
  local copies, waits for them, and re-layouts  36.3 us (5%)
  other arithmetic  29.4 us (4%)
  between operations  19.9 us (3%)
    ppermute x18, waiting for transfers between devices, to_peer(): return lax.ppermute(values, 'tensor', swap)  114 us
    pallas_call x8, Pallas kernels, weight_grad(): pl.pallas_call(functools.partial(weight_grad_kernel, len(parts), pieces,...  87 us
    dot_general x13, matrix products, dot(): lax.dot_general(left, right, (((left_dim,), (right_dim,)), ((), ())), pre...  78.5 us
    all_gather x2, waiting for transfers between devices, gather(): return lax.all_gather(values, dp_axes, axis=0, tiled=True)  71.7 us
    pallas_call x1, Pallas kernels, self_back(): pl.pallas_call(self_back_kernel, grid_spec=pltpu.PrefetchScalarGridSpec(n...  43.8 us
    ppermute x8, waiting for transfers between devices, to_near(): return lax.ppermute(values, 'near', swap)  36 us
    pallas_call x9, Pallas kernels, near_sum(): pl.pallas_call(near_sum_kernel, grid=(rows // block,), in_specs=[spec(par...  33.7 us
    pallas_call x2, Pallas kernels, pull(): pl.pallas_call(pull_kernel, grid=(depth // PULL_ROWS,), in_specs=[whole,...  28.1 us
  transfers between devices with their start and end apart: 69, of which 26 were waited for; matrix products, arithmetic and copies ran while one was open for 15% of the time, Pallas kernels for 41%

profile of v4, /device:TPU:0, one launch (start us, length us, event | category | flops | bytes accessed | tf_op | source)
XLA Modules:
  0.0 773.5 jit_solution(14600560267172165753)
XLA Ops:
  12.0 2.7 shard_map.279
  16.0 3.1 shard_map.283
  19.1 3.0 collective-permute-start
  25.9 22.2 %collective-permute-done = bf16[384,1536]{1,0:T(8,128)(2,1)S(1)} collective-permute-done((bf16[384,1536]{1,0:T(8,128)(2,1)S(1)}, bf16[384,1536]{1,0:T(8,128)(2,1)S(1)}, u32[]{:S(2)}, u32[]{:S(2)}) %collective-permute-start) | collective-permute-done | bytes 1179680 | tf_op jit(solution)/shard_map/ppermute | solution.py:688
  48.8 69.6 %all-gather.3.cloned.1.call-done.own_w.out_w.qkv_w = bf16[1536,6272]{1,0:T(8,128)(2,1)} async-done(((bf16[96,6272]{1,0:T(8,128)(2,1)}), bf16[1536,6272]{1,0:T(8,128)(2,1)}) %all-gather.3.cloned.1.call-update) | async-done | bytes 19267600 | tf_op jit(solution)/shard_map/all_gather | solution.py:697
  119.6 3.2 constant_dynamic-slice_fusion.6
  126.5 12.3 %fusion.13.qkv = f32[768,2304]{1,0:T(8,128)} fusion(bf16[1536,6272]{1,0:T(8,128)(2,1)} %all-gather.3.cloned.1.call-done.own_w.out_w.qkv_w, bf16[384,1536]{1,0:T(8,128)(2,1)S(1)} %get-tuple-element.443, bf16[384,1536]{1,0:T(8,128)(2,1)S(1)} %get-tuple-element.442), kind=kOutput, calls=%fused_computation.15 | convolution fusion | flops 5440536576 | bytes 16515072 | tf_op jit(solution)/shard_map/dot_general | solution.py:31
  138.8 15.5 %shard_map.280 = (bf16[768,768]{1,0:T(8,128)(2,1)}, bf16[768,768]{1,0:T(8,128)(2,1)}, bf16[768,768]{1,0:T(8,128)(2,1)}, bf16[768,768]{1,0:T(8,128)(2,1)}, f32[6,2,768]{2,1,0:T(2,128)}) custom-call(f32[768,2304]{1,0:T(8,128)} %fusion.13.qkv, f32[768,128]{1,0:T(8,128)} %get-tuple-element.449.cos_in, f32[768,128]{1,0:T(8,128)} %get-tuple-element.450.sin_in), custom_call_target="tpu_custom_call" | custom-call | flops 1048576 | bytes 16384 | tf_op jit(solution)/shard_map/pallas_call | solution.py:186
  154.6 3.0 convolution_convert_fusion
  158.9 3.4 fusion.29.kv_own
  164.3 2.8 fusion.45
  170.7 15.8 %collective-permute-done.1 = bf16[384,1536]{1,0:T(8,128)(2,1)S(1)} collective-permute-done((bf16[384,1536]{1,0:T(8,128)(2,1)S(1)}, bf16[384,1536]{1,0:T(8,128)(2,1)S(1)}, u32[]{:S(2)}, u32[]{:S(2)}) %collective-permute-start.1) | collective-permute-done | bytes 1179680 | tf_op jit(solution)/shard_map/ppermute | solution.py:688
  188.8 7.2 collective-permute-done.5.kv_peer
  196.0 3.3 convolution_convert_fusion.1.q_peer
  199.4 4.0 fusion.48.q_own
  203.4 12.3 %shard_map.281 = (bf16[384,1536]{1,0:T(8,128)(2,1)}, f32[12,2,384]{2,1,0:T(2,128)}) custom-call(bf16[384,768]{1,0:T(8,128)(2,1)} %fusion.48.q_own, bf16[384,768]{1,0:T(8,128)(2,1)} %convolution_convert_fusion.1.q_peer, bf16[144,1536]{1,0:T(8,128)(2,1)} %copy-done.37, bf16[144,1536]{1,0:T(8,128)(2,1)} %copy-done.38), custom_call_target="tpu_custom_call" | custom-call | flops 1048576 | bytes 16384 | tf_op jit(solution)/shard_map/pallas_call | solution.py:270
  215.7 5.0 collective-permute-done.6
  220.7 3.0 convolution_add_fusion.1
  236.5 20.2 %collective-permute-done.15 = f32[8,128]{1,0:T(8,128)S(1)} collective-permute-done((f32[8,128]{1,0:T(8,128)S(1)}, f32[8,128]{1,0:T(8,128)S(1)}, u32[]{:S(2)}, u32[]{:S(2)}) %collective-permute-start.15) | collective-permute-done | bytes 4128 | tf_op jit(solution)/shard_map/ppermute | solution.py:688
  263.9 11.5 %fusion.15.gate_in = bf16[768,3072]{1,0:T(8,128)(2,1)S(1)} fusion(bf16[1536,9216]{1,0:T(8,128)(2,1)} %all-gather.5.cloned.1.call-done.weights, bf16[384,1536]{1,0:T(8,128)(2,1)} %copy-done.8, bf16[384,1536]{1,0:T(8,128)(2,1)S(1)} %multiply_convert_fusion.refs_0_), kind=kOutput, calls=%fused_computation.17 | convolution fusion | flops 7254835200 | bytes 16515072 | tf_op jit(solution)/shard_map/dot_general | solution.py:31
  275.5 14.9 %fusion.64 = (bf16[768,3072]{1,0:T(8,128)(2,1)}, bf16[768,3072]{1,0:T(8,128)(2,1)}) fusion(bf16[768,3072]{1,0:T(8,128)(2,1)S(1)} %fusion.15.gate_in, bf16[1536,9216]{1,0:T(8,128)(2,1)} %all-gather.5.cloned.1.call-done.weights, bf16[384,1536]{1,0:T(8,128)(2,1)S(1)} %copy-done.9, bf16[384,1536]{1,0:T(8,128)(2,1)S(1)} %multiply_convert_fusion.refs_0_), kind=kOutput, calls=%fused_computation.179 | convolution fusion | flops 7271350272 | bytes 25952256 | tf_op jit(solution)/shard_map/dot_general | solution.py:31
  290.4 4.0 shard_map.284
  294.7 8.4 %fusion.26 = bf16[384,1536]{1,0:T(8,128)(2,1)S(1)} fusion(bf16[1536,9216]{1,0:T(8,128)(2,1)} %all-gather.5.cloned.1.call-done.weights, bf16[768,3072]{1,0:T(8,128)(2,1)} %get-tuple-element.387.refs_0_.refs_1_.refs_3_), kind=kOutput, calls=%fused_computation.34 | convolution fusion | flops 3624468480 | bytes 12976128 | tf_op jit(solution)/shard_map/dot_general | solution.py:31
  305.1 6.6 fusion.11
  311.7 19.8 %collective-permute-done.11 = bf16[384,1536]{1,0:T(8,128)(2,1)S(1)} collective-permute-done((bf16[384,1536]{1,0:T(8,128)(2,1)S(1)}, bf16[384,1536]{1,0:T(8,128)(2,1)S(1)}, u32[]{:S(2)}, u32[]{:S(2)}) %collective-permute-start.11) | collective-permute-done | bytes 1179680 | tf_op jit(solution)/shard_map/ppermute | solution.py:688
  337.1 12.7 %shard_map.285 = (bf16[384,3072]{1,0:T(8,128)(2,1)}, bf16[384,3072]{1,0:T(8,128)(2,1)}, bf16[2,384,1536]{2,1,0:T(8,128)(2,1)}) custom-call(s32[2]{0:T(128)} %pad_add_fusion.places, bf16[384,1536]{1,0:T(8,128)(2,1)} %copy-done.10, bf16[1536,9216]{1,0:T(8,128)(2,1)} %all-gather.5.cloned.1.call-done.weights, bf16[768,3072]{1,0:T(8,128)(2,1)} %copy-done.5, ...), custom_call_target="tpu_custom_call" | custom-call | flops 1048576 | bytes 16384 | tf_op jit(solution)/shard_map/pallas_call | solution.py:376
  349.8 14.2 %shard_map.286.refs_0_ = f32[384,1536]{1,0:T(8,128)} custom-call(bf16[384,3072]{1,0:T(8,128)(2,1)} %get-tuple-element.197.gate_in.refs_1_, bf16[384,3072]{1,0:T(8,128)(2,1)} %get-tuple-element.182.up_in.refs_1_, bf16[1536,9216]{1,0:T(8,128)(2,1)} %all-gather.5.cloned.1.call-done.weights), custom_call_target="tpu_custom_call" | custom-call | flops 1048576 | bytes 16384 | tf_op jit(solution)/shard_map/pallas_call | solution.py:606
  366.6 12.7 %shard_map.287 = (bf16[384,3072]{1,0:T(8,128)(2,1)}, bf16[384,3072]{1,0:T(8,128)(2,1)}, bf16[2,384,1536]{2,1,0:T(8,128)(2,1)}) custom-call(s32[2]{0:T(128)} %pad_add_fusion.places, bf16[384,1536]{1,0:T(8,128)(2,1)} %copy-done.24, bf16[1536,9216]{1,0:T(8,128)(2,1)} %all-gather.5.cloned.1.call-done.weights, bf16[768,3072]{1,0:T(8,128)(2,1)} %copy-done.5, ...), custom_call_target="tpu_custom_call" | custom-call | flops 1048576 | bytes 16384 | tf_op jit(solution)/shard_map/pallas_call | solution.py:376
  381.3 15.7 %shard_map.288 = (bf16[768,896]{1,0:T(8,128)(2,1)}, bf16[768,640]{1,0:T(8,128)(2,1)}, bf16[768,896]{1,0:T(8,128)(2,1)}, bf16[768,640]{1,0:T(8,128)(2,1)}) custom-call(s32[2]{0:T(128)} %pad_add_fusion.places, bf16[384,1536]{1,0:T(8,128)(2,1)} %copy-done.10, bf16[768,3072]{1,0:T(8,128)(2,1)} %get-tuple-element.387.refs_0_.refs_1_.refs_3_, ...), custom_call_target="tpu_custom_call" | custom-call | flops 1048576 | bytes 16384 | tf_op jit(solution)/shard_map/pallas_call | solution.py:456
  404.2 13.9 %shard_map.289 = bf16[384,1536]{1,0:T(8,128)(2,1)} custom-call(bf16[384,3072]{1,0:T(8,128)(2,1)} %get-tuple-element.202.gate_in.refs_3_, bf16[384,3072]{1,0:T(8,128)(2,1)} %get-tuple-element.211.up_in.refs_3_, bf16[1536,9216]{1,0:T(8,128)(2,1)} %all-gather.5.cloned.1.call-done.weights), custom_call_target="tpu_custom_call" | custom-call | flops 1048576 | bytes 16384 | tf_op jit(solution)/shard_map/pallas_call | solution.py:606
  419.5 15.7 %shard_map.291 = (bf16[768,1408]{1,0:T(8,128)(2,1)}, bf16[768,128]{1,0:T(8,128)(2,1)}, bf16[768,1408]{1,0:T(8,128)(2,1)}, bf16[768,128]{1,0:T(8,128)(2,1)}) custom-call(s32[2]{0:T(128)} %pad_add_fusion.places, bf16[384,1536]{1,0:T(8,128)(2,1)} %copy-done.6, bf16[384,3072]{1,0:T(8,128)(2,1)} %get-tuple-element.197.gate_in.refs_1_, ...), custom_call_target="tpu_custom_call" | custom-call | flops 1048576 | bytes 16384 | tf_op jit(solution)/shard_map/pallas_call | solution.py:456
  435.3 3.9 shard_map.293
  439.2 15.9 %shard_map.292 = (bf16[768,768]{1,0:T(8,128)(2,1)}, bf16[768,768]{1,0:T(8,128)(2,1)}, bf16[768,768]{1,0:T(8,128)(2,1)}, bf16[768,768]{1,0:T(8,128)(2,1)}) custom-call(s32[2]{0:T(128)} %pad_add_fusion.places, bf16[384,1536]{1,0:T(8,128)(2,1)} %copy-done.6, bf16[384,3072]{1,0:T(8,128)(2,1)} %get-tuple-element.182.up_in.refs_1_, bf16[384,1536]{1,0:T(8,128)(2,1)} %copy-done.8, ...), custom_call_target="tpu_custom_call" | custom-call | flops 1048576 | bytes 16384 | tf_op jit(solution)/shard_map/pallas_call | solution.py:456
  455.1 4.3 collective-permute-done.24.refs_1_
  460.3 3.7 shard_map.299
  464.1 7.0 shard_map.294
  473.5 5.5 shard_map.295
  479.0 13.2 %shard_map.296 = (bf16[384,1536]{1,0:T(8,128)(2,1)}, bf16[144,3072]{1,0:T(8,128)(2,1)}) custom-call(bf16[384,768]{1,0:T(8,128)(2,1)} %fusion.48.q_own, bf16[384,768]{1,0:T(8,128)(2,1)} %convolution_convert_fusion.1.q_peer, bf16[384,768]{1,0:T(8,128)(2,1)} %get-tuple-element.223.g_own, bf16[384,768]{1,0:T(8,128)(2,1)} %get-tuple-element.224.g_peer, ...), custom_call_target="tpu_custom_call" | custom-call | flops 1048576 | bytes 16384 | tf_op jit(solution)/shard_map/pallas_call | solution.py:270
  492.2 7.1 shard_map.297.refs_0_
  499.3 6.7 shard_map.298
  508.2 4.5 shard_map.300
  516.0 7.5 shard_map.301
  523.4 18.0 %collective-permute-done.31.refs_1_ = bf16[768,768]{1,0:T(8,128)(2,1)S(1)} collective-permute-done((bf16[768,768]{1,0:T(8,128)(2,1)}, bf16[768,768]{1,0:T(8,128)(2,1)S(1)}, u32[]{:S(2)}, u32[]{:S(2)}) %collective-permute-start.31) | collective-permute-done | bytes 1179680 | tf_op jit(solution)/shard_map/ppermute | solution.py:694
  542.4 3.7 shard_map.302
  547.3 7.9 %shard_map.303 = (bf16[768,384]{1,0:T(8,128)(2,1)}, bf16[768,384]{1,0:T(8,128)(2,1)}) custom-call(s32[2]{0:T(128)} %pad_add_fusion.places, bf16[384,1536]{1,0:T(8,128)(2,1)} %get-tuple-element.239.refs_0_.own_in, bf16[768,768]{1,0:T(8,128)(2,1)} %get-tuple-element.170.refs_0_.refs_1_.refs_3_, bf16[384,1536]{1,0:T(8,128)(2,1)} %copy-done.19, ...), custom_call_target="tpu_custom_call" | custom-call | flops 1048576 | bytes 16384 | tf_op jit(solution)/shard_map/pallas_call | solution.py:456
  555.3 3.1 shard_map.304
  563.3 43.8 %shard_map.305 = (bf16[768,2304]{1,0:T(8,128)(2,1)}, bf16[768,1152]{1,0:T(8,128)(2,1)}, f32[384,1536]{1,0:T(8,128)}, bf16[384,1536]{1,0:T(8,128)(2,1)}) custom-call(s32[2]{0:T(128)} %pad_add_fusion.places, bf16[768,768]{1,0:T(8,128)(2,1)} %get-tuple-element.250.q_in, bf16[768,768]{1,0:T(8,128)(2,1)} %get-tuple-element.251.k_in, ...), custom_call_target="tpu_custom_call" | custom-call | flops 1048576 | bytes 16384 | tf_op jit(solution)/shard_map/pallas_call | solution.py:220
  608.5 4.3 shard_map.306
  613.7 3.1 collective-permute-done.38.refs_3_
  618.0 11.3 %shard_map.307 = (bf16[768,1152]{1,0:T(8,128)(2,1)}, bf16[768,1152]{1,0:T(8,128)(2,1)}) custom-call(s32[2]{0:T(128)} %pad_add_fusion.places, bf16[768,1536]{1,0:T(8,128)(2,1)} %copy-done.16, bf16[768,2304]{1,0:T(8,128)(2,1)} %get-tuple-element.272.refs_1_, bf16[768,1536]{1,0:T(8,128)(2,1)} %collective-permute-done.2.refs_2_, bf16[768,1152]{1,0:T(8,128)(2,1)} %copy-done.34), custom_call_target="tpu_custom_call" | custom-call | flops 1048576 | bytes 16384 | tf_op jit(solution)/shard_map/pallas_call | solution.py:456
  637.1 3.4 shard_map.308
  645.1 7.5 shard_map.312
  652.6 5.6 shard_map.313
  658.2 2.8 shard_map.314
  661.1 9.2 %collective-permute-done.43.refs_1_ = bf16[768,1152]{1,0:T(8,128)(2,1)S(1)} collective-permute-done((bf16[768,1152]{1,0:T(8,128)(2,1)}, bf16[768,1152]{1,0:T(8,128)(2,1)S(1)}, u32[]{:S(2)}, u32[]{:S(2)}) %collective-permute-start.43) | collective-permute-done | bytes 1769504 | tf_op jit(solution)/shard_map/ppermute | solution.py:694
  671.5 4.1 shard_map.315
  680.9 23.3 %collective-permute-done.45.refs_1_ = bf16[384,1536]{1,0:T(8,128)(2,1)} collective-permute-done((bf16[384,1536]{1,0:T(8,128)(2,1)}, bf16[384,1536]{1,0:T(8,128)(2,1)}, u32[]{:S(2)}, u32[]{:S(2)}) %collective-permute-start.45) | collective-permute-done | bytes 1179680 | tf_op jit(solution)/shard_map/ppermute | solution.py:688
  704.3 4.0 fusion.18
  708.3 6.6 shard_map.316
  717.4 4.2 shard_map.317
  727.7 3.0 collective-permute-done.48
  734.3 3.0 collective-permute-done.49
  739.7 3.8 collective-permute-done.50
  750.9 9.3 %reduce-scatter.23.cloned.1.call-done = bf16[192,1152]{1,0:T(8,128)(2,1)} async-done(((bf16[768,1152]{1,0:T(8,128)(2,1)}), bf16[192,1152]{1,0:T(8,128)(2,1)}) %reduce-scatter.23.cloned.1.call-update) | async-done | bytes 442384 | tf_op jit(solution)/shard_map/reduce_scatter | solution.py:831
  (379 shorter events, 127.8 us)
Async XLA Ops:
  7.2 111.2 %all-gather.3.cloned.1.call-start = ((), (), s32[]{:S(2)}) async-start(), calls=%async_computation.8 | async-start | bytes 20471808 | tf_op jit(solution)/shard_map/all_gather | solution.py:697
  14.7 249.2 %all-gather.5.cloned.1.call-start = ((), (), s32[]{:S(2)}) async-start(), calls=%async_computation.9 | async-start | bytes 30081024 | tf_op jit(solution)/shard_map/all_gather | solution.py:697
  19.0 489.2 %reduce-scatter.9.cloned.1.call-start = ((), (), s32[]{:S(2)}) async-start(), calls=%async_computation.10 | async-start | bytes 1720320 | tf_op jit(solution)/shard_map/reduce_scatter | solution.py:831
  19.1 29.0 %collective-permute-start = (bf16[384,1536]{1,0:T(8,128)(2,1)S(1)}, bf16[384,1536]{1,0:T(8,128)(2,1)S(1)}, u32[]{:S(2)}, u32[]{:S(2)}) collective-permute-start(bf16[384,1536]{1,0:T(8,128)(2,1)S(1)} %bitcast.35), channel_id=1, source_target_pairs={{0,1},{1,0},{2,3},{3,2},{4,5},{5,4},{6,7},{7,6},{8,9},{9,8},{10,11... | collective-permute-start | bytes 3538952 | tf_op jit(solution)/shard_map/ppermute | solution.py:688
  122.8 31.5 %collective-permute-start.3 = (bf16[768,768]{1,0:T(8,128)(2,1)}, bf16[768,768]{1,0:T(8,128)(2,1)}, u32[]{:S(2)}, u32[]{:S(2)}) collective-permute-start(bf16[768,768]{1,0:T(8,128)(2,1)} %get-tuple-element.385), channel_id=1, source_target_pairs={{0,1},{1,0},{2,3},{3,2},{4,5},{5,4},{6,7},{7,6},{8,9},{9,8},{10,11... | collective-permute-start | bytes 3538952 | tf_op jit(solution)/shard_map/ppermute | solution.py:688
  126.4 60.1 %collective-permute-start.2 = (bf16[768,1536]{1,0:T(8,128)(2,1)S(1)}, bf16[768,1536]{1,0:T(8,128)(2,1)}, u32[]{:S(2)}, u32[]{:S(2)}) collective-permute-start(bf16[768,1536]{1,0:T(8,128)(2,1)S(1)} %pad_maximum_fusion.refs_0_), channel_id=1, source_target_pairs={{0,2},{2,0},{1,3},{3,1},{4,6},{6,4},{5,7},{7,5},{8,10},{10,8},{9,1... | collective-permute-start | bytes 7077896 | tf_op jit(solution)/shard_map/ppermute | solution.py:691
  154.3 12.8 %collective-permute-start.4 = (bf16[768,768]{1,0:T(8,128)(2,1)}, bf16[768,768]{1,0:T(8,128)(2,1)}, u32[]{:S(2)}, u32[]{:S(2)}) collective-permute-start(bf16[768,768]{1,0:T(8,128)(2,1)} %collective-permute-done.3), channel_id=1, source_target_pairs={{0,2},{2,0},{1,3},{3,1},{4,6},{6,4},{5,7},{7,5},{8,10},{10,8},{9,1... | collective-permute-start | bytes 3538952 | tf_op jit(solution)/shard_map/ppermute | solution.py:691
  157.7 28.9 %collective-permute-start.1 = (bf16[384,1536]{1,0:T(8,128)(2,1)S(1)}, bf16[384,1536]{1,0:T(8,128)(2,1)S(1)}, u32[]{:S(2)}, u32[]{:S(2)}) collective-permute-start(bf16[384,1536]{1,0:T(8,128)(2,1)S(1)} %convolution_convert_fusion), channel_id=1, source_target_pairs={{0,1},{1,0},{2,3},{3,2},{4,5},{5,4},{6,7},{7,6},{8,9},{9,8},{10,11... | collective-permute-start | bytes 3538952 | tf_op jit(solution)/shard_map/ppermute | solution.py:688
  162.2 33.8 %collective-permute-start.5 = (bf16[144,1536]{1,0:T(8,128)(2,1)S(1)}, bf16[144,1536]{1,0:T(8,128)(2,1)S(1)}, u32[]{:S(2)}, u32[]{:S(2)}) collective-permute-start(bf16[144,1536]{1,0:T(8,128)(2,1)S(1)} %fusion.29.kv_own), channel_id=1, source_target_pairs={{0,1},{1,0},{2,3},{3,2},{4,5},{5,4},{6,7},{7,6},{8,9},{9,8},{10,11... | collective-permute-start | bytes 1327112 | tf_op jit(solution)/shard_map/ppermute | solution.py:688
  163.2 57.5 %collective-permute-start.6 = (bf16[768,768]{1,0:T(8,128)(2,1)}, bf16[768,768]{1,0:T(8,128)(2,1)}, u32[]{:S(2)}, u32[]{:S(2)}) collective-permute-start(bf16[768,768]{1,0:T(8,128)(2,1)} %get-tuple-element.384), channel_id=1, source_target_pairs={{0,1},{1,0},{2,3},{3,2},{4,5},{5,4},{6,7},{7,6},{8,9},{9,8},{10,11... | collective-permute-start | bytes 3538952 | tf_op jit(solution)/shard_map/ppermute | solution.py:688
  220.7 3.1 collective-permute-start.7
  228.4 29.5 %collective-permute-start.8 = (bf16[384,1536]{1,0:T(8,128)(2,1)S(1)}, bf16[384,1536]{1,0:T(8,128)(2,1)S(1)}, u32[]{:S(2)}, u32[]{:S(2)}) collective-permute-start(bf16[384,1536]{1,0:T(8,128)(2,1)S(1)} %multiply_convert_fusion.refs_0_), channel_id=1, source_target_pairs={{0,1},{1,0},{2,3},{3,2},{4,5},{5,4},{6,7},{7,6},{8,9},{9,8},{10,11... | collective-permute-start | bytes 3538952 | tf_op jit(solution)/shard_map/ppermute | solution.py:688
  229.6 28.3 %collective-permute-start.10 = (bf16[144,1536]{1,0:T(8,128)(2,1)S(1)}, bf16[144,1536]{1,0:T(8,128)(2,1)}, u32[]{:S(2)}, u32[]{:S(2)}) collective-permute-start(bf16[144,1536]{1,0:T(8,128)(2,1)S(1)} %pad.9.refs_0_), channel_id=1, source_target_pairs={{0,2},{2,0},{1,3},{3,1},{4,6},{6,4},{5,7},{7,5},{8,10},{10,8},{9,1... | collective-permute-start | bytes 1327112 | tf_op jit(solution)/shard_map/ppermute | solution.py:691
  233.2 24.7 %collective-permute-start.9 = (bf16[768,384]{1,0:T(8,128)(2,1)}, bf16[768,384]{1,0:T(8,128)(2,1)S(1)}, u32[]{:S(2)}, u32[]{:S(2)}) collective-permute-start(bf16[768,384]{1,0:T(8,128)(2,1)} %shard_map.282), channel_id=1, source_target_pairs={{0,2},{2,0},{1,3},{3,1},{4,6},{6,4},{5,7},{7,5},{8,10},{10,8},{9,1... | collective-permute-start | bytes 1769480 | tf_op jit(solution)/shard_map/ppermute | solution.py:691
  235.5 21.1 %collective-permute-start.15 = (f32[8,128]{1,0:T(8,128)S(1)}, f32[8,128]{1,0:T(8,128)S(1)}, u32[]{:S(2)}, u32[]{:S(2)}) collective-permute-start(f32[8,128]{1,0:T(8,128)S(1)} %broadcast_in_dim.11), channel_id=1, source_target_pairs={{0,1},{1,0},{2,3},{3,2},{4,5},{5,4},{6,7},{7,6},{8,9},{9,8},{10,11... | collective-permute-start | bytes 12296 | tf_op jit(solution)/shard_map/ppermute | solution.py:688
  257.8 53.8 %collective-permute-start.14 = (bf16[384,1536]{1,0:T(8,128)(2,1)}, bf16[384,1536]{1,0:T(8,128)(2,1)}, u32[]{:S(2)}, u32[]{:S(2)}) collective-permute-start(bf16[384,1536]{1,0:T(8,128)(2,1)} %multiply_convert_fusion.1.refs_0_), channel_id=1, source_target_pairs={{0,2},{2,0},{1,3},{3,1},{4,6},{6,4},{5,7},{7,5},{8,10},{10,8},{9,1... | collective-permute-start | bytes 3538952 | tf_op jit(solution)/shard_map/ppermute | solution.py:691
  261.3 50.3 %collective-permute-start.12 = (bf16[768,1536]{1,0:T(8,128)(2,1)}, bf16[768,1536]{1,0:T(8,128)(2,1)S(1)}, u32[]{:S(2)}, u32[]{:S(2)}) collective-permute-start(bf16[768,1536]{1,0:T(8,128)(2,1)} %pad_maximum_fusion.3), channel_id=1, source_target_pairs={{0,2},{2,0},{1,3},{3,1},{4,6},{6,4},{5,7},{7,5},{8,10},{10,8},{9,1... | collective-permute-start | bytes 7077896 | tf_op jit(solution)/shard_map/ppermute | solution.py:691
  294.5 37.0 %collective-permute-start.13 = (bf16[768,1536]{1,0:T(8,128)(2,1)}, bf16[768,1536]{1,0:T(8,128)(2,1)}, u32[]{:S(2)}, u32[]{:S(2)}) collective-permute-start(bf16[768,1536]{1,0:T(8,128)(2,1)} %shard_map.284), channel_id=1, source_target_pairs={{0,2},{2,0},{1,3},{3,1},{4,6},{6,4},{5,7},{7,5},{8,10},{10,8},{9,1... | collective-permute-start | bytes 7077896 | tf_op jit(solution)/shard_map/ppermute | solution.py:691
  303.1 28.3 %collective-permute-start.11 = (bf16[384,1536]{1,0:T(8,128)(2,1)S(1)}, bf16[384,1536]{1,0:T(8,128)(2,1)S(1)}, u32[]{:S(2)}, u32[]{:S(2)}) collective-permute-start(bf16[384,1536]{1,0:T(8,128)(2,1)S(1)} %fusion.26), channel_id=1, source_target_pairs={{0,1},{1,0},{2,3},{3,2},{4,5},{5,4},{6,7},{7,6},{8,9},{9,8},{10,11... | collective-permute-start | bytes 3538952 | tf_op jit(solution)/shard_map/ppermute | solution.py:688
  335.4 28.6 %collective-permute-start.17 = (bf16[384,1536]{1,0:T(8,128)(2,1)S(1)}, bf16[384,1536]{1,0:T(8,128)(2,1)S(1)}, u32[]{:S(2)}, u32[]{:S(2)}) collective-permute-start(bf16[384,1536]{1,0:T(8,128)(2,1)S(1)} %get-tuple-element.380.g_in.refs_0_), channel_id=1, source_target_pairs={{0,2},{2,0},{1,3},{3,1},{4,6},{6,4},{5,7},{7,5},{8,10},{10,8},{9,1... | collective-permute-start | bytes 3538952 | tf_op jit(solution)/shard_map/ppermute | solution.py:691
  335.4 28.6 %collective-permute-start.16 = (bf16[384,1536]{1,0:T(8,128)(2,1)S(1)}, bf16[384,1536]{1,0:T(8,128)(2,1)S(1)}, u32[]{:S(2)}, u32[]{:S(2)}) collective-permute-start(bf16[384,1536]{1,0:T(8,128)(2,1)S(1)} %get-tuple-element.380.g_in.refs_0_), channel_id=1, source_target_pairs={{0,1},{1,0},{2,3},{3,2},{4,5},{5,4},{6,7},{7,6},{8,9},{9,8},{10,11... | collective-permute-start | bytes 3538952 | tf_op jit(solution)/shard_map/ppermute | solution.py:688
  366.1 13.3 %collective-permute-start.19 = (bf16[2,384,1536]{2,1,0:T(8,128)(2,1)}, bf16[2,384,1536]{2,1,0:T(8,128)(2,1)S(1)}, u32[]{:S(2)}, u32[]{:S(2)}) collective-permute-start(bf16[2,384,1536]{2,1,0:T(8,128)(2,1)} %get-tuple-element.188), channel_id=1, source_target_pairs={{0,2},{2,0},{1,3},{3,1},{4,6},{6,4},{5,7},{7,5},{8,10},{10,8},{9,1... | collective-permute-start | bytes 7077896 | tf_op jit(solution)/shard_map/ppermute | solution.py:691
  366.6 12.7 %collective-permute-start.18 = (bf16[384,1536]{1,0:T(8,128)(2,1)}, bf16[384,1536]{1,0:T(8,128)(2,1)}, u32[]{:S(2)}, u32[]{:S(2)}) collective-permute-start(bf16[384,1536]{1,0:T(8,128)(2,1)} %copy-done.24), channel_id=1, source_target_pairs={{0,2},{2,0},{1,3},{3,1},{4,6},{6,4},{5,7},{7,5},{8,10},{10,8},{9,1... | collective-permute-start | bytes 3538952 | tf_op jit(solution)/shard_map/ppermute | solution.py:691
  380.3 16.7 %collective-permute-start.20 = (bf16[384,768]{1,0:T(8,128)(2,1)}, bf16[384,768]{1,0:T(8,128)(2,1)S(1)}, u32[]{:S(2)}, u32[]{:S(2)}) collective-permute-start(bf16[384,768]{1,0:T(8,128)(2,1)} %slice.224), channel_id=1, source_target_pairs={{0,1},{1,0},{2,3},{3,2},{4,5},{5,4},{6,7},{7,6},{8,9},{9,8},{10,11... | collective-permute-start | bytes 1769480 | tf_op jit(solution)/shard_map/ppermute | solution.py:688
  397.8 20.3 %collective-permute-start.21 = (bf16[2,384,1536]{2,1,0:T(8,128)(2,1)}, bf16[2,384,1536]{2,1,0:T(8,128)(2,1)S(1)}, u32[]{:S(2)}, u32[]{:S(2)}) collective-permute-start(bf16[2,384,1536]{2,1,0:T(8,128)(2,1)} %get-tuple-element.199), channel_id=1, source_target_pairs={{0,2},{2,0},{1,3},{3,1},{4,6},{6,4},{5,7},{7,5},{8,10},{10,8},{9,1... | collective-permute-start | bytes 7077896 | tf_op jit(solution)/shard_map/ppermute | solution.py:691
  397.8 37.4 %collective-permute-start.23 = (bf16[768,896]{1,0:T(8,128)(2,1)}, bf16[768,896]{1,0:T(8,128)(2,1)}, u32[]{:S(2)}, u32[]{:S(2)}) collective-permute-start(bf16[768,896]{1,0:T(8,128)(2,1)} %get-tuple-element.209), channel_id=1, source_target_pairs={{0,4},{4,0},{1,5},{5,1},{2,6},{6,2},{3,7},{7,3},{8,12},{12,8},{9,1... | collective-permute-start | bytes 4128776 | tf_op jit(solution)/shard_map/ppermute | solution.py:694
  402.7 15.4 %collective-permute-start.22 = (bf16[768,384]{1,0:T(8,128)(2,1)}, bf16[768,384]{1,0:T(8,128)(2,1)S(1)}, u32[]{:S(2)}, u32[]{:S(2)}) collective-permute-start(bf16[768,384]{1,0:T(8,128)(2,1)} %shard_map.290), channel_id=1, source_target_pairs={{0,2},{2,0},{1,3},{3,1},{4,6},{6,4},{5,7},{7,5},{8,10},{10,8},{9,1... | collective-permute-start | bytes 1769480 | tf_op jit(solution)/shard_map/ppermute | solution.py:691
  402.9 52.1 %collective-permute-start.25 = (bf16[384,1536]{1,0:T(8,128)(2,1)}, bf16[384,1536]{1,0:T(8,128)(2,1)}, u32[]{:S(2)}, u32[]{:S(2)}) collective-permute-start(bf16[384,1536]{1,0:T(8,128)(2,1)} %multiply_convert_fusion.1.refs_0_), channel_id=1, source_target_pairs={{0,1},{1,0},{2,3},{3,2},{4,5},{5,4},{6,7},{7,6},{8,9},{9,8},{10,11... | collective-permute-start | bytes 3538952 | tf_op jit(solution)/shard_map/ppermute | solution.py:688
  418.1 41.2 %collective-permute-start.26 = (bf16[384,1536]{1,0:T(8,128)(2,1)}, bf16[384,1536]{1,0:T(8,128)(2,1)}, u32[]{:S(2)}, u32[]{:S(2)}) collective-permute-start(bf16[384,1536]{1,0:T(8,128)(2,1)} %shard_map.289), channel_id=1, source_target_pairs={{0,1},{1,0},{2,3},{3,2},{4,5},{5,4},{6,7},{7,6},{8,9},{9,8},{10,11... | collective-permute-start | bytes 3538952 | tf_op jit(solution)/shard_map/ppermute | solution.py:688
  435.2 24.2 %collective-permute-start.24 = (bf16[768,640]{1,0:T(8,128)(2,1)}, bf16[768,640]{1,0:T(8,128)(2,1)S(1)}, u32[]{:S(2)}, u32[]{:S(2)}) collective-permute-start(bf16[768,640]{1,0:T(8,128)(2,1)} %get-tuple-element.219), channel_id=1, source_target_pairs={{0,4},{4,0},{1,5},{5,1},{2,6},{6,2},{3,7},{7,3},{8,12},{12,8},{9,1... | collective-permute-start | bytes 2949128 | tf_op jit(solution)/shard_map/ppermute | solution.py:694
  459.4 83.0 %reduce-scatter.11.cloned.1.call-start = ((), (), s32[]{:S(2)}) async-start(), calls=%async_computation.11 | async-start | bytes 1228800 | tf_op jit(solution)/shard_map/reduce_scatter | solution.py:831
  459.5 48.7 %collective-permute-start.29 = (bf16[768,1408]{1,0:T(8,128)(2,1)}, bf16[768,1408]{1,0:T(8,128)(2,1)}, u32[]{:S(2)}, u32[]{:S(2)}) collective-permute-start(bf16[768,1408]{1,0:T(8,128)(2,1)} %get-tuple-element.235), channel_id=1, source_target_pairs={{0,4},{4,0},{1,5},{5,1},{2,6},{6,2},{3,7},{7,3},{8,12},{12,8},{9,1... | collective-permute-start | bytes 6488072 | tf_op jit(solution)/shard_map/ppermute | solution.py:694
  464.1 143.1 %reduce-scatter.13.cloned.1.call-start = ((), (), s32[]{:S(2)}) async-start(), calls=%async_computation.12 | async-start | bytes 2703360 | tf_op jit(solution)/shard_map/reduce_scatter | solution.py:831
  471.1 34.9 %collective-permute-start.28 = (bf16[384,1536]{1,0:T(8,128)(2,1)}, bf16[384,1536]{1,0:T(8,128)(2,1)S(1)}, u32[]{:S(2)}, u32[]{:S(2)}) collective-permute-start(bf16[384,1536]{1,0:T(8,128)(2,1)} %get-tuple-element.241.g_in.refs_0_), channel_id=1, source_target_pairs={{0,2},{2,0},{1,3},{3,1},{4,6},{6,4},{5,7},{7,5},{8,10},{10,8},{9,1... | collective-permute-start | bytes 3538952 | tf_op jit(solution)/shard_map/ppermute | solution.py:691
  471.1 34.8 %collective-permute-start.27 = (bf16[384,1536]{1,0:T(8,128)(2,1)}, bf16[384,1536]{1,0:T(8,128)(2,1)}, u32[]{:S(2)}, u32[]{:S(2)}) collective-permute-start(bf16[384,1536]{1,0:T(8,128)(2,1)} %get-tuple-element.241.g_in.refs_0_), channel_id=1, source_target_pairs={{0,1},{1,0},{2,3},{3,2},{4,5},{5,4},{6,7},{7,6},{8,9},{9,8},{10,11... | collective-permute-start | bytes 3538952 | tf_op jit(solution)/shard_map/ppermute | solution.py:688
  512.7 124.4 %reduce-scatter.15.cloned.1.call-start = ((), (), s32[]{:S(2)}) async-start(), calls=%async_computation.13 | async-start | bytes 1474560 | tf_op jit(solution)/shard_map/reduce_scatter | solution.py:831
  512.7 3.3 collective-permute-start.33
  512.8 28.6 %collective-permute-start.31 = (bf16[768,768]{1,0:T(8,128)(2,1)}, bf16[768,768]{1,0:T(8,128)(2,1)S(1)}, u32[]{:S(2)}, u32[]{:S(2)}) collective-permute-start(bf16[768,768]{1,0:T(8,128)(2,1)} %get-tuple-element.240), channel_id=1, source_target_pairs={{0,4},{4,0},{1,5},{5,1},{2,6},{6,2},{3,7},{7,3},{8,12},{12,8},{9,1... | collective-permute-start | bytes 3538952 | tf_op jit(solution)/shard_map/ppermute | solution.py:694
  513.5 27.9 %collective-permute-start.32 = (bf16[384,1536]{1,0:T(8,128)(2,1)S(1)}, bf16[384,1536]{1,0:T(8,128)(2,1)}, u32[]{:S(2)}, u32[]{:S(2)}) collective-permute-start(bf16[384,1536]{1,0:T(8,128)(2,1)S(1)} %copy-done.18), channel_id=1, source_target_pairs={{0,2},{2,0},{1,3},{3,1},{4,6},{6,4},{5,7},{7,5},{8,10},{10,8},{9,1... | collective-permute-start | bytes 3538952 | tf_op jit(solution)/shard_map/ppermute | solution.py:691
  513.6 28.2 %collective-permute-start.30 = (bf16[384,1536]{1,0:T(8,128)(2,1)S(1)}, bf16[384,1536]{1,0:T(8,128)(2,1)S(1)}, u32[]{:S(2)}, u32[]{:S(2)}) collective-permute-start(bf16[384,1536]{1,0:T(8,128)(2,1)S(1)} %copy-done.18), channel_id=1, source_target_pairs={{0,1},{1,0},{2,3},{3,2},{4,5},{5,4},{6,7},{7,6},{8,9},{9,8},{10,11... | collective-permute-start | bytes 3538952 | tf_op jit(solution)/shard_map/ppermute | solution.py:688
  542.4 3.8 collective-permute-start.34
  546.2 124.1 %reduce-scatter.17.cloned.1.call-start = ((), (), s32[]{:S(2)}) async-start(), calls=%async_computation.14 | async-start | bytes 2457600 | tf_op jit(solution)/shard_map/reduce_scatter | solution.py:831
  558.3 48.8 %collective-permute-start.37 = (bf16[768,1280]{1,0:T(8,128)(2,1)}, bf16[768,1280]{1,0:T(8,128)(2,1)S(1)}, u32[]{:S(2)}, u32[]{:S(2)}) collective-permute-start(bf16[768,1280]{1,0:T(8,128)(2,1)} %shard_map.304), channel_id=1, source_target_pairs={{0,4},{4,0},{1,5},{5,1},{2,6},{6,2},{3,7},{7,3},{8,12},{12,8},{9,1... | collective-permute-start | bytes 5898248 | tf_op jit(solution)/shard_map/ppermute | solution.py:694
  560.5 46.6 %collective-permute-start.35 = (bf16[384,768]{1,0:T(8,128)(2,1)}, bf16[384,768]{1,0:T(8,128)(2,1)S(1)}, u32[]{:S(2)}, u32[]{:S(2)}) collective-permute-start(bf16[384,768]{1,0:T(8,128)(2,1)} %slice.225), channel_id=1, source_target_pairs={{0,1},{1,0},{2,3},{3,2},{4,5},{5,4},{6,7},{7,6},{8,9},{9,8},{10,11... | collective-permute-start | bytes 1769480 | tf_op jit(solution)/shard_map/ppermute | solution.py:688
  561.6 45.5 %collective-permute-start.36 = (bf16[144,1536]{1,0:T(8,128)(2,1)S(1)}, bf16[144,1536]{1,0:T(8,128)(2,1)S(1)}, u32[]{:S(2)}, u32[]{:S(2)}) collective-permute-start(bf16[144,1536]{1,0:T(8,128)(2,1)S(1)} %get-tuple-element.400), channel_id=1, source_target_pairs={{0,1},{1,0},{2,3},{3,2},{4,5},{5,4},{6,7},{7,6},{8,9},{9,8},{10,11... | collective-permute-start | bytes 1327112 | tf_op jit(solution)/shard_map/ppermute | solution.py:688
  612.8 102.2 %reduce-scatter.19.cloned.1.call-start = ((), (), s32[]{:S(2)}) async-start(), calls=%async_computation.15 | async-start | bytes 737280 | tf_op jit(solution)/shard_map/reduce_scatter | solution.py:831
  612.8 4.0 collective-permute-start.38
  612.9 16.5 %collective-permute-start.39 = (bf16[768,384]{1,0:T(8,128)(2,1)}, bf16[768,384]{1,0:T(8,128)(2,1)S(1)}, u32[]{:S(2)}, u32[]{:S(2)}) collective-permute-start(bf16[768,384]{1,0:T(8,128)(2,1)} %get-tuple-element.283), channel_id=1, source_target_pairs={{0,4},{4,0},{1,5},{5,1},{2,6},{6,2},{3,7},{7,3},{8,12},{12,8},{9,1... | collective-permute-start | bytes 1769480 | tf_op jit(solution)/shard_map/ppermute | solution.py:694
  629.4 40.9 %collective-permute-start.43 = (bf16[768,1152]{1,0:T(8,128)(2,1)}, bf16[768,1152]{1,0:T(8,128)(2,1)S(1)}, u32[]{:S(2)}, u32[]{:S(2)}) collective-permute-start(bf16[768,1152]{1,0:T(8,128)(2,1)} %get-tuple-element.287), channel_id=1, source_target_pairs={{0,4},{4,0},{1,5},{5,1},{2,6},{6,2},{3,7},{7,3},{8,12},{12,8},{9,1... | collective-permute-start | bytes 5308424 | tf_op jit(solution)/shard_map/ppermute | solution.py:694
  637.1 6.2 collective-permute-start.42
  640.5 107.2 %reduce-scatter.21.cloned.1.call-start = ((), (), s32[]{:S(2)}) async-start(), calls=%async_computation.16 | async-start | bytes 2211840 | tf_op jit(solution)/shard_map/reduce_scatter | solution.py:831
  640.6 2.7 collective-permute-start.41
  675.6 84.5 %reduce-scatter.23.cloned.1.call-start = ((), (), s32[]{:S(2)}) async-start(), calls=%async_computation.17 | async-start | bytes 2211840 | tf_op jit(solution)/shard_map/reduce_scatter | solution.py:831
  676.6 27.7 %collective-permute-start.45 = (bf16[384,1536]{1,0:T(8,128)(2,1)}, bf16[384,1536]{1,0:T(8,128)(2,1)}, u32[]{:S(2)}, u32[]{:S(2)}) collective-permute-start(bf16[384,1536]{1,0:T(8,128)(2,1)} %get-tuple-element.308), channel_id=1, source_target_pairs={{0,1},{1,0},{2,3},{3,2},{4,5},{5,4},{6,7},{7,6},{8,9},{9,8},{10,11... | collective-permute-start | bytes 3538952 | tf_op jit(solution)/shard_map/ppermute | solution.py:688
  677.2 40.0 %collective-permute-start.44 = (bf16[768,1152]{1,0:T(8,128)(2,1)S(1)}, bf16[768,1152]{1,0:T(8,128)(2,1)}, u32[]{:S(2)}, u32[]{:S(2)}) collective-permute-start(bf16[768,1152]{1,0:T(8,128)(2,1)S(1)} %copy-done.33), channel_id=1, source_target_pairs={{0,4},{4,0},{1,5},{5,1},{2,6},{6,2},{3,7},{7,3},{8,12},{12,8},{9,1... | collective-permute-start | bytes 5308424 | tf_op jit(solution)/shard_map/ppermute | solution.py:694
  721.7 3.8 collective-permute-start.46
  722.9 9.0 %collective-permute-start.55 = (bf16[96,384]{1,0:T(8,128)(2,1)S(1)}, bf16[96,384]{1,0:T(8,128)(2,1)S(1)}, u32[]{:S(2)}, u32[]{:S(2)}) collective-permute-start(bf16[96,384]{1,0:T(8,128)(2,1)S(1)} %constant_dynamic-slice_fusion.2), channel_id=1, source_target_pairs={{0,2},{2,0},{1,3},{3,1},{4,6},{6,4},{5,7},{7,5},{8,10},{10,8},{9,1... | collective-permute-start | bytes 221192 | tf_op jit(solution)/shard_map/ppermute | solution.py:691
  723.0 10.5 %collective-permute-start.53 = (bf16[96,384]{1,0:T(8,128)(2,1)S(1)}, bf16[96,384]{1,0:T(8,128)(2,1)S(1)}, u32[]{:S(2)}, u32[]{:S(2)}) collective-permute-start(bf16[96,384]{1,0:T(8,128)(2,1)S(1)} %constant_dynamic-slice_fusion.4), channel_id=1, source_target_pairs={{0,2},{2,0},{1,3},{3,1},{4,6},{6,4},{5,7},{7,5},{8,10},{10,8},{9,1... | collective-permute-start | bytes 221192 | tf_op jit(solution)/shard_map/ppermute | solution.py:691
  725.7 20.8 %collective-permute-start.56 = (bf16[96,1536]{1,0:T(8,128)(2,1)S(1)}, bf16[96,1536]{1,0:T(8,128)(2,1)S(1)}, u32[]{:S(2)}, u32[]{:S(2)}) collective-permute-start(bf16[96,1536]{1,0:T(8,128)(2,1)S(1)} %fusion.55), channel_id=1, source_target_pairs={{0,2},{2,0},{1,3},{3,1},{4,6},{6,4},{5,7},{7,5},{8,10},{10,8},{9,1... | collective-permute-start | bytes 884744 | tf_op jit(solution)/shard_map/ppermute | solution.py:691
  726.8 3.9 collective-permute-start.48
  727.7 17.6 %collective-permute-start.57 = (bf16[96,1536]{1,0:T(8,128)(2,1)S(1)}, bf16[96,1536]{1,0:T(8,128)(2,1)S(1)}, u32[]{:S(2)}, u32[]{:S(2)}) collective-permute-start(bf16[96,1536]{1,0:T(8,128)(2,1)S(1)} %fusion.57), channel_id=1, source_target_pairs={{0,2},{2,0},{1,3},{3,1},{4,6},{6,4},{5,7},{7,5},{8,10},{10,8},{9,1... | collective-permute-start | bytes 884744 | tf_op jit(solution)/shard_map/ppermute | solution.py:691
  730.7 18.1 %collective-permute-start.51 = (bf16[130,1536]{1,0:T(8,128)(2,1)S(1)}, bf16[130,1536]{1,0:T(8,128)(2,1)S(1)}, u32[]{:S(2)}, u32[]{:S(2)}) collective-permute-start(bf16[130,1536]{1,0:T(8,128)(2,1)S(1)} %slice.397), channel_id=1, source_target_pairs={{0,1},{1,0},{2,3},{3,2},{4,5},{5,4},{6,7},{7,6},{8,9},{9,8},{10,11... | collective-permute-start | bytes 1198088 | tf_op jit(solution)/shard_map/ppermute | solution.py:688
  731.9 5.3 collective-permute-start.49
  737.3 6.2 collective-permute-start.50
  (75 other events, 532.3 us)
Sparse Core Ops, SparseCore 0:
  14.9 103.4 all-gather.2
  120.0 143.9 all-gather.4
  459.5 30.5 reduce-scatter.8
  492.4 24.9 reduce-scatter.10
  520.1 43.5 reduce-scatter.12
  566.0 28.5 reduce-scatter.14
  612.9 39.8 reduce-scatter.16
  655.2 21.1 reduce-scatter.18
  678.8 36.8 reduce-scatter.20
  721.7 38.4 reduce-scatter.22

commit v5 on v4

--- a/solution.py
+++ b/solution.py
@@ -21,9 +21,9 @@
 DOWN_PIECES = (896, 640)
 GATE_PIECES = (1408, 128)
 UP_PIECES = (768, 768)
-PULL_ROWS = 256
-NORM_ROWS = 128
-FEED_COLUMNS = 512
+PULL_ROWS = 512
+NORM_ROWS = 192
+FEED_COLUMNS = 768
 SMALL_COST = pl.CostEstimate(flops=1 << 20, bytes_accessed=1 << 14, transcendentals=0)
 
 

time: 782 us -> 779 us (level)
  Pallas kernels: 318 us -> 309 us
  transfers between devices with their start and end apart: 69 -> 69, of which waited for: 26 -> 27; matrix products, arithmetic and copies ran while one was open for 15% -> 15% of each run, Pallas kernels for 41% -> 40%
where the time goes in v5:
time: 779 us; the launch traced here: 771 us
  Pallas kernels  309 us (40%)
  waiting for transfers between devices  256 us (33%)
  matrix products  78.7 us (10%)
  starting transfers between devices  42.9 us (6%)
  local copies, waits for them, and re-layouts  34.9 us (4%)
  other arithmetic  29.4 us (4%)
  between operations  20.1 us (3%)
    ppermute x18, waiting for transfers between devices, to_peer(): return lax.ppermute(values, 'tensor', swap)  114 us
    pallas_call x8, Pallas kernels, weight_grad(): pl.pallas_call(functools.partial(weight_grad_kernel, len(parts), pieces,...  86.8 us
    dot_general x13, matrix products, dot(): lax.dot_general(left, right, (((left_dim,), (right_dim,)), ((), ())), pre...  78.7 us
    all_gather x2, waiting for transfers between devices, gather(): return lax.all_gather(values, dp_axes, axis=0, tiled=True)  71.7 us
    pallas_call x1, Pallas kernels, self_back(): pl.pallas_call(self_back_kernel, grid_spec=pltpu.PrefetchScalarGridSpec(n...  43.8 us
    ppermute x8, waiting for transfers between devices, to_near(): return lax.ppermute(values, 'near', swap)  39.8 us
    pallas_call x9, Pallas kernels, near_sum(): pl.pallas_call(near_sum_kernel, grid=(rows // block,), in_specs=[spec(par...  33.7 us
    pallas_call x2, Pallas kernels, pull(): pl.pallas_call(pull_kernel, grid=(depth // PULL_ROWS,), in_specs=[whole,...  26.7 us
  transfers between devices with their start and end apart: 69, of which 27 were waited for; matrix products, arithmetic and copies ran while one was open for 15% of the time, Pallas kernels for 40%

profile of v5, /device:TPU:0, one launch (start us, length us, event | category | flops | bytes accessed | tf_op | source)
XLA Modules:
  0.0 771.4 jit_solution(7672154210291179279)
XLA Ops:
  16.0 3.1 shard_map.283
  19.1 3.0 collective-permute-start
  25.9 22.2 %collective-permute-done = bf16[384,1536]{1,0:T(8,128)(2,1)S(1)} collective-permute-done((bf16[384,1536]{1,0:T(8,128)(2,1)S(1)}, bf16[384,1536]{1,0:T(8,128)(2,1)S(1)}, u32[]{:S(2)}, u32[]{:S(2)}) %collective-permute-start) | collective-permute-done | bytes 1179680 | tf_op jit(solution)/shard_map/ppermute | solution.py:688
  48.8 69.6 %all-gather.3.cloned.1.call-done.own_w.out_w.qkv_w = bf16[1536,6272]{1,0:T(8,128)(2,1)} async-done(((bf16[96,6272]{1,0:T(8,128)(2,1)}), bf16[1536,6272]{1,0:T(8,128)(2,1)}) %all-gather.3.cloned.1.call-update) | async-done | bytes 19267600 | tf_op jit(solution)/shard_map/all_gather | solution.py:697
  119.6 3.2 constant_dynamic-slice_fusion.6
  126.5 12.3 %fusion.13.qkv = f32[768,2304]{1,0:T(8,128)} fusion(bf16[1536,6272]{1,0:T(8,128)(2,1)} %all-gather.3.cloned.1.call-done.own_w.out_w.qkv_w, bf16[384,1536]{1,0:T(8,128)(2,1)S(1)} %get-tuple-element.443, bf16[384,1536]{1,0:T(8,128)(2,1)S(1)} %get-tuple-element.442), kind=kOutput, calls=%fused_computation.15 | convolution fusion | flops 5440536576 | bytes 16515072 | tf_op jit(solution)/shard_map/dot_general | solution.py:31
  138.8 15.5 %shard_map.280 = (bf16[768,768]{1,0:T(8,128)(2,1)}, bf16[768,768]{1,0:T(8,128)(2,1)}, bf16[768,768]{1,0:T(8,128)(2,1)}, bf16[768,768]{1,0:T(8,128)(2,1)}, f32[6,2,768]{2,1,0:T(2,128)}) custom-call(f32[768,2304]{1,0:T(8,128)} %fusion.13.qkv, f32[768,128]{1,0:T(8,128)} %get-tuple-element.449.cos_in, f32[768,128]{1,0:T(8,128)} %get-tuple-element.450.sin_in), custom_call_target="tpu_custom_call" | custom-call | flops 1048576 | bytes 16384 | tf_op jit(solution)/shard_map/pallas_call | solution.py:186
  154.6 3.0 convolution_convert_fusion
  158.8 3.3 fusion.29.kv_own
  170.7 15.8 %collective-permute-done.1 = bf16[384,1536]{1,0:T(8,128)(2,1)S(1)} collective-permute-done((bf16[384,1536]{1,0:T(8,128)(2,1)S(1)}, bf16[384,1536]{1,0:T(8,128)(2,1)S(1)}, u32[]{:S(2)}, u32[]{:S(2)}) %collective-permute-start.1) | collective-permute-done | bytes 1179680 | tf_op jit(solution)/shard_map/ppermute | solution.py:688
  188.8 7.2 collective-permute-done.5.kv_peer
  196.0 3.3 convolution_convert_fusion.1.q_peer
  199.3 4.0 fusion.48.q_own
  203.3 12.0 %shard_map.281 = (bf16[384,1536]{1,0:T(8,128)(2,1)}, f32[12,2,384]{2,1,0:T(2,128)}) custom-call(bf16[384,768]{1,0:T(8,128)(2,1)} %fusion.48.q_own, bf16[384,768]{1,0:T(8,128)(2,1)} %convolution_convert_fusion.1.q_peer, bf16[144,1536]{1,0:T(8,128)(2,1)} %copy-done.37, bf16[144,1536]{1,0:T(8,128)(2,1)} %copy-done.38), custom_call_target="tpu_custom_call" | custom-call | flops 1048576 | bytes 16384 | tf_op jit(solution)/shard_map/pallas_call | solution.py:270
  215.3 5.4 collective-permute-done.6
  220.7 3.0 convolution_add_fusion.1
  236.5 20.2 %collective-permute-done.15 = f32[8,128]{1,0:T(8,128)S(1)} collective-permute-done((f32[8,128]{1,0:T(8,128)S(1)}, f32[8,128]{1,0:T(8,128)S(1)}, u32[]{:S(2)}, u32[]{:S(2)}) %collective-permute-start.15) | collective-permute-done | bytes 4128 | tf_op jit(solution)/shard_map/ppermute | solution.py:688
  264.0 11.5 %fusion.15.gate_in = bf16[768,3072]{1,0:T(8,128)(2,1)S(1)} fusion(bf16[1536,9216]{1,0:T(8,128)(2,1)} %all-gather.5.cloned.1.call-done.weights, bf16[384,1536]{1,0:T(8,128)(2,1)} %copy-done.8, bf16[384,1536]{1,0:T(8,128)(2,1)S(1)} %multiply_convert_fusion.refs_0_), kind=kOutput, calls=%fused_computation.17 | convolution fusion | flops 7254835200 | bytes 16515072 | tf_op jit(solution)/shard_map/dot_general | solution.py:31
  275.5 14.9 %fusion.64 = (bf16[768,3072]{1,0:T(8,128)(2,1)}, bf16[768,3072]{1,0:T(8,128)(2,1)}) fusion(bf16[768,3072]{1,0:T(8,128)(2,1)S(1)} %fusion.15.gate_in, bf16[1536,9216]{1,0:T(8,128)(2,1)} %all-gather.5.cloned.1.call-done.weights, bf16[384,1536]{1,0:T(8,128)(2,1)S(1)} %copy-done.9, bf16[384,1536]{1,0:T(8,128)(2,1)S(1)} %multiply_convert_fusion.refs_0_), kind=kOutput, calls=%fused_computation.179 | convolution fusion | flops 7271350272 | bytes 25952256 | tf_op jit(solution)/shard_map/dot_general | solution.py:31
  290.5 4.0 shard_map.284
  294.7 8.4 %fusion.26 = bf16[384,1536]{1,0:T(8,128)(2,1)S(1)} fusion(bf16[1536,9216]{1,0:T(8,128)(2,1)} %all-gather.5.cloned.1.call-done.weights, bf16[768,3072]{1,0:T(8,128)(2,1)} %get-tuple-element.387.refs_0_.refs_1_.refs_3_), kind=kOutput, calls=%fused_computation.34 | convolution fusion | flops 3624468480 | bytes 12976128 | tf_op jit(solution)/shard_map/dot_general | solution.py:31
  305.1 6.8 fusion.11
  312.0 19.5 %collective-permute-done.11 = bf16[384,1536]{1,0:T(8,128)(2,1)S(1)} collective-permute-done((bf16[384,1536]{1,0:T(8,128)(2,1)S(1)}, bf16[384,1536]{1,0:T(8,128)(2,1)S(1)}, u32[]{:S(2)}, u32[]{:S(2)}) %collective-permute-start.11) | collective-permute-done | bytes 1179680 | tf_op jit(solution)/shard_map/ppermute | solution.py:688
  337.1 11.7 %shard_map.285 = (bf16[384,3072]{1,0:T(8,128)(2,1)}, bf16[384,3072]{1,0:T(8,128)(2,1)}, bf16[2,384,1536]{2,1,0:T(8,128)(2,1)}) custom-call(s32[2]{0:T(128)} %pad_add_fusion.places, bf16[384,1536]{1,0:T(8,128)(2,1)} %copy-done.10, bf16[1536,9216]{1,0:T(8,128)(2,1)} %all-gather.5.cloned.1.call-done.weights, bf16[768,3072]{1,0:T(8,128)(2,1)} %copy-done.5, ...), custom_call_target="tpu_custom_call" | custom-call | flops 1048576 | bytes 16384 | tf_op jit(solution)/shard_map/pallas_call | solution.py:376
  348.8 13.4 %shard_map.286.refs_0_ = f32[384,1536]{1,0:T(8,128)} custom-call(bf16[384,3072]{1,0:T(8,128)(2,1)} %get-tuple-element.197.gate_in.refs_1_, bf16[384,3072]{1,0:T(8,128)(2,1)} %get-tuple-element.182.up_in.refs_1_, bf16[1536,9216]{1,0:T(8,128)(2,1)} %all-gather.5.cloned.1.call-done.weights), custom_call_target="tpu_custom_call" | custom-call | flops 1048576 | bytes 16384 | tf_op jit(solution)/shard_map/pallas_call | solution.py:606
  365.3 11.6 %shard_map.287 = (bf16[384,3072]{1,0:T(8,128)(2,1)}, bf16[384,3072]{1,0:T(8,128)(2,1)}, bf16[2,384,1536]{2,1,0:T(8,128)(2,1)}) custom-call(s32[2]{0:T(128)} %pad_add_fusion.places, bf16[384,1536]{1,0:T(8,128)(2,1)} %copy-done.24, bf16[1536,9216]{1,0:T(8,128)(2,1)} %all-gather.5.cloned.1.call-done.weights, bf16[768,3072]{1,0:T(8,128)(2,1)} %copy-done.5, ...), custom_call_target="tpu_custom_call" | custom-call | flops 1048576 | bytes 16384 | tf_op jit(solution)/shard_map/pallas_call | solution.py:376
  379.7 15.7 %shard_map.288 = (bf16[768,896]{1,0:T(8,128)(2,1)}, bf16[768,640]{1,0:T(8,128)(2,1)}, bf16[768,896]{1,0:T(8,128)(2,1)}, bf16[768,640]{1,0:T(8,128)(2,1)}) custom-call(s32[2]{0:T(128)} %pad_add_fusion.places, bf16[384,1536]{1,0:T(8,128)(2,1)} %copy-done.10, bf16[768,3072]{1,0:T(8,128)(2,1)} %get-tuple-element.387.refs_0_.refs_1_.refs_3_, ...), custom_call_target="tpu_custom_call" | custom-call | flops 1048576 | bytes 16384 | tf_op jit(solution)/shard_map/pallas_call | solution.py:456
  402.4 13.3 %shard_map.289 = bf16[384,1536]{1,0:T(8,128)(2,1)} custom-call(bf16[384,3072]{1,0:T(8,128)(2,1)} %get-tuple-element.202.gate_in.refs_3_, bf16[384,3072]{1,0:T(8,128)(2,1)} %get-tuple-element.211.up_in.refs_3_, bf16[1536,9216]{1,0:T(8,128)(2,1)} %all-gather.5.cloned.1.call-done.weights), custom_call_target="tpu_custom_call" | custom-call | flops 1048576 | bytes 16384 | tf_op jit(solution)/shard_map/pallas_call | solution.py:606
  417.2 15.7 %shard_map.291 = (bf16[768,1408]{1,0:T(8,128)(2,1)}, bf16[768,128]{1,0:T(8,128)(2,1)}, bf16[768,1408]{1,0:T(8,128)(2,1)}, bf16[768,128]{1,0:T(8,128)(2,1)}) custom-call(s32[2]{0:T(128)} %pad_add_fusion.places, bf16[384,1536]{1,0:T(8,128)(2,1)} %copy-done.6, bf16[384,3072]{1,0:T(8,128)(2,1)} %get-tuple-element.197.gate_in.refs_1_, ...), custom_call_target="tpu_custom_call" | custom-call | flops 1048576 | bytes 16384 | tf_op jit(solution)/shard_map/pallas_call | solution.py:456
  433.2 3.9 shard_map.293
  437.1 15.7 %shard_map.292 = (bf16[768,768]{1,0:T(8,128)(2,1)}, bf16[768,768]{1,0:T(8,128)(2,1)}, bf16[768,768]{1,0:T(8,128)(2,1)}, bf16[768,768]{1,0:T(8,128)(2,1)}) custom-call(s32[2]{0:T(128)} %pad_add_fusion.places, bf16[384,1536]{1,0:T(8,128)(2,1)} %copy-done.6, bf16[384,3072]{1,0:T(8,128)(2,1)} %get-tuple-element.182.up_in.refs_1_, bf16[384,1536]{1,0:T(8,128)(2,1)} %copy-done.8, ...), custom_call_target="tpu_custom_call" | custom-call | flops 1048576 | bytes 16384 | tf_op jit(solution)/shard_map/pallas_call | solution.py:456
  452.8 4.2 collective-permute-done.24.refs_1_
  457.9 3.7 shard_map.299
  461.7 5.8 shard_map.294
  470.7 5.5 shard_map.295
  476.3 13.2 %shard_map.296 = (bf16[384,1536]{1,0:T(8,128)(2,1)}, bf16[144,3072]{1,0:T(8,128)(2,1)}) custom-call(bf16[384,768]{1,0:T(8,128)(2,1)} %fusion.48.q_own, bf16[384,768]{1,0:T(8,128)(2,1)} %convolution_convert_fusion.1.q_peer, bf16[384,768]{1,0:T(8,128)(2,1)} %get-tuple-element.223.g_own, bf16[384,768]{1,0:T(8,128)(2,1)} %get-tuple-element.224.g_peer, ...), custom_call_target="tpu_custom_call" | custom-call | flops 1048576 | bytes 16384 | tf_op jit(solution)/shard_map/pallas_call | solution.py:270
  489.4 5.9 shard_map.297.refs_0_
  495.4 5.4 shard_map.298
  500.8 4.8 collective-permute-done.29.refs_1_
  505.6 4.5 shard_map.300
  513.4 7.7 shard_map.301
  521.1 17.8 %collective-permute-done.31.refs_1_ = bf16[768,768]{1,0:T(8,128)(2,1)S(1)} collective-permute-done((bf16[768,768]{1,0:T(8,128)(2,1)}, bf16[768,768]{1,0:T(8,128)(2,1)S(1)}, u32[]{:S(2)}, u32[]{:S(2)}) %collective-permute-start.31) | collective-permute-done | bytes 1179680 | tf_op jit(solution)/shard_map/ppermute | solution.py:694
  539.9 3.7 shard_map.302
  544.8 7.5 shard_map.303
  552.3 3.1 shard_map.304
  560.4 43.8 %shard_map.305 = (bf16[768,2304]{1,0:T(8,128)(2,1)}, bf16[768,1152]{1,0:T(8,128)(2,1)}, f32[384,1536]{1,0:T(8,128)}, bf16[384,1536]{1,0:T(8,128)(2,1)}) custom-call(s32[2]{0:T(128)} %pad_add_fusion.places, bf16[768,768]{1,0:T(8,128)(2,1)} %get-tuple-element.250.q_in, bf16[768,768]{1,0:T(8,128)(2,1)} %get-tuple-element.251.k_in, ...), custom_call_target="tpu_custom_call" | custom-call | flops 1048576 | bytes 16384 | tf_op jit(solution)/shard_map/pallas_call | solution.py:220
  605.6 4.3 shard_map.306
  610.8 3.1 collective-permute-done.38.refs_3_
  615.1 11.3 %shard_map.307 = (bf16[768,1152]{1,0:T(8,128)(2,1)}, bf16[768,1152]{1,0:T(8,128)(2,1)}) custom-call(s32[2]{0:T(128)} %pad_add_fusion.places, bf16[768,1536]{1,0:T(8,128)(2,1)} %copy-done.16, bf16[768,2304]{1,0:T(8,128)(2,1)} %get-tuple-element.272.refs_1_, bf16[768,1536]{1,0:T(8,128)(2,1)} %collective-permute-done.2.refs_2_, bf16[768,1152]{1,0:T(8,128)(2,1)} %copy-done.34), custom_call_target="tpu_custom_call" | custom-call | flops 1048576 | bytes 16384 | tf_op jit(solution)/shard_map/pallas_call | solution.py:456
  634.3 3.4 shard_map.308
  642.4 7.7 %shard_map.312 = (bf16[768,384]{1,0:T(8,128)(2,1)}, bf16[768,384]{1,0:T(8,128)(2,1)}) custom-call(s32[2]{0:T(128)} %pad_add_fusion.places, bf16[384,1536]{1,0:T(8,128)(2,1)} %multiply_convert_fusion.1.refs_0_, bf16[384,1536]{1,0:T(8,128)(2,1)} %get-tuple-element.248.g_in.refs_0_.refs_1_, bf16[384,1536]{1,0:T(8,128)(2,1)} %collective-permute-done.25.refs_2_, ...), custom_call_target="tpu_custom_call" | custom-call | flops 1048576 | bytes 16384 | tf_op jit(solution)/shard_map/pallas_call | solution.py:456
  650.1 5.6 shard_map.313
  655.7 2.8 shard_map.314
  658.6 8.8 %collective-permute-done.43.refs_1_ = bf16[768,1152]{1,0:T(8,128)(2,1)S(1)} collective-permute-done((bf16[768,1152]{1,0:T(8,128)(2,1)}, bf16[768,1152]{1,0:T(8,128)(2,1)S(1)}, u32[]{:S(2)}, u32[]{:S(2)}) %collective-permute-start.43) | collective-permute-done | bytes 1769504 | tf_op jit(solution)/shard_map/ppermute | solution.py:694
  668.6 4.1 shard_map.315
  679.1 22.2 %collective-permute-done.45.refs_1_ = bf16[384,1536]{1,0:T(8,128)(2,1)} collective-permute-done((bf16[384,1536]{1,0:T(8,128)(2,1)}, bf16[384,1536]{1,0:T(8,128)(2,1)}, u32[]{:S(2)}, u32[]{:S(2)}) %collective-permute-start.45) | collective-permute-done | bytes 1179680 | tf_op jit(solution)/shard_map/ppermute | solution.py:688
  701.4 4.0 fusion.18
  705.4 5.5 shard_map.316
  711.0 4.2 collective-permute-done.44.refs_2_
  715.2 4.2 shard_map.317
  725.8 2.8 collective-permute-done.48
  731.8 3.1 collective-permute-done.49
  736.9 4.1 collective-permute-done.50
  748.5 9.3 %reduce-scatter.23.cloned.1.call-done = bf16[192,1152]{1,0:T(8,128)(2,1)} async-done(((bf16[768,1152]{1,0:T(8,128)(2,1)}), bf16[192,1152]{1,0:T(8,128)(2,1)}) %reduce-scatter.23.cloned.1.call-update) | async-done | bytes 442384 | tf_op jit(solution)/shard_map/reduce_scatter | solution.py:831
  (379 shorter events, 131.6 us)
Async XLA Ops:
  7.2 111.2 %all-gather.3.cloned.1.call-start = ((), (), s32[]{:S(2)}) async-start(), calls=%async_computation.8 | async-start | bytes 20471808 | tf_op jit(solution)/shard_map/all_gather | solution.py:697
  14.7 249.2 %all-gather.5.cloned.1.call-start = ((), (), s32[]{:S(2)}) async-start(), calls=%async_computation.9 | async-start | bytes 30081024 | tf_op jit(solution)/shard_map/all_gather | solution.py:697
  19.0 486.6 %reduce-scatter.9.cloned.1.call-start = ((), (), s32[]{:S(2)}) async-start(), calls=%async_computation.10 | async-start | bytes 1720320 | tf_op jit(solution)/shard_map/reduce_scatter | solution.py:831
  19.1 29.0 %collective-permute-start = (bf16[384,1536]{1,0:T(8,128)(2,1)S(1)}, bf16[384,1536]{1,0:T(8,128)(2,1)S(1)}, u32[]{:S(2)}, u32[]{:S(2)}) collective-permute-start(bf16[384,1536]{1,0:T(8,128)(2,1)S(1)} %bitcast.35), channel_id=1, source_target_pairs={{0,1},{1,0},{2,3},{3,2},{4,5},{5,4},{6,7},{7,6},{8,9},{9,8},{10,11... | collective-permute-start | bytes 3538952 | tf_op jit(solution)/shard_map/ppermute | solution.py:688
  122.8 31.5 %collective-permute-start.3 = (bf16[768,768]{1,0:T(8,128)(2,1)}, bf16[768,768]{1,0:T(8,128)(2,1)}, u32[]{:S(2)}, u32[]{:S(2)}) collective-permute-start(bf16[768,768]{1,0:T(8,128)(2,1)} %get-tuple-element.385), channel_id=1, source_target_pairs={{0,1},{1,0},{2,3},{3,2},{4,5},{5,4},{6,7},{7,6},{8,9},{9,8},{10,11... | collective-permute-start | bytes 3538952 | tf_op jit(solution)/shard_map/ppermute | solution.py:688
  126.4 60.1 %collective-permute-start.2 = (bf16[768,1536]{1,0:T(8,128)(2,1)S(1)}, bf16[768,1536]{1,0:T(8,128)(2,1)}, u32[]{:S(2)}, u32[]{:S(2)}) collective-permute-start(bf16[768,1536]{1,0:T(8,128)(2,1)S(1)} %pad_maximum_fusion.refs_0_), channel_id=1, source_target_pairs={{0,2},{2,0},{1,3},{3,1},{4,6},{6,4},{5,7},{7,5},{8,10},{10,8},{9,1... | collective-permute-start | bytes 7077896 | tf_op jit(solution)/shard_map/ppermute | solution.py:691
  154.3 12.8 %collective-permute-start.4 = (bf16[768,768]{1,0:T(8,128)(2,1)}, bf16[768,768]{1,0:T(8,128)(2,1)}, u32[]{:S(2)}, u32[]{:S(2)}) collective-permute-start(bf16[768,768]{1,0:T(8,128)(2,1)} %collective-permute-done.3), channel_id=1, source_target_pairs={{0,2},{2,0},{1,3},{3,1},{4,6},{6,4},{5,7},{7,5},{8,10},{10,8},{9,1... | collective-permute-start | bytes 3538952 | tf_op jit(solution)/shard_map/ppermute | solution.py:691
  157.6 28.9 %collective-permute-start.1 = (bf16[384,1536]{1,0:T(8,128)(2,1)S(1)}, bf16[384,1536]{1,0:T(8,128)(2,1)S(1)}, u32[]{:S(2)}, u32[]{:S(2)}) collective-permute-start(bf16[384,1536]{1,0:T(8,128)(2,1)S(1)} %convolution_convert_fusion), channel_id=1, source_target_pairs={{0,1},{1,0},{2,3},{3,2},{4,5},{5,4},{6,7},{7,6},{8,9},{9,8},{10,11... | collective-permute-start | bytes 3538952 | tf_op jit(solution)/shard_map/ppermute | solution.py:688
  162.2 33.8 %collective-permute-start.5 = (bf16[144,1536]{1,0:T(8,128)(2,1)S(1)}, bf16[144,1536]{1,0:T(8,128)(2,1)S(1)}, u32[]{:S(2)}, u32[]{:S(2)}) collective-permute-start(bf16[144,1536]{1,0:T(8,128)(2,1)S(1)} %fusion.29.kv_own), channel_id=1, source_target_pairs={{0,1},{1,0},{2,3},{3,2},{4,5},{5,4},{6,7},{7,6},{8,9},{9,8},{10,11... | collective-permute-start | bytes 1327112 | tf_op jit(solution)/shard_map/ppermute | solution.py:688
  163.2 57.5 %collective-permute-start.6 = (bf16[768,768]{1,0:T(8,128)(2,1)}, bf16[768,768]{1,0:T(8,128)(2,1)}, u32[]{:S(2)}, u32[]{:S(2)}) collective-permute-start(bf16[768,768]{1,0:T(8,128)(2,1)} %get-tuple-element.384), channel_id=1, source_target_pairs={{0,1},{1,0},{2,3},{3,2},{4,5},{5,4},{6,7},{7,6},{8,9},{9,8},{10,11... | collective-permute-start | bytes 3538952 | tf_op jit(solution)/shard_map/ppermute | solution.py:688
  220.7 3.1 collective-permute-start.7
  228.4 29.5 %collective-permute-start.8 = (bf16[384,1536]{1,0:T(8,128)(2,1)S(1)}, bf16[384,1536]{1,0:T(8,128)(2,1)S(1)}, u32[]{:S(2)}, u32[]{:S(2)}) collective-permute-start(bf16[384,1536]{1,0:T(8,128)(2,1)S(1)} %multiply_convert_fusion.refs_0_), channel_id=1, source_target_pairs={{0,1},{1,0},{2,3},{3,2},{4,5},{5,4},{6,7},{7,6},{8,9},{9,8},{10,11... | collective-permute-start | bytes 3538952 | tf_op jit(solution)/shard_map/ppermute | solution.py:688
  229.6 28.3 %collective-permute-start.10 = (bf16[144,1536]{1,0:T(8,128)(2,1)S(1)}, bf16[144,1536]{1,0:T(8,128)(2,1)}, u32[]{:S(2)}, u32[]{:S(2)}) collective-permute-start(bf16[144,1536]{1,0:T(8,128)(2,1)S(1)} %pad.9.refs_0_), channel_id=1, source_target_pairs={{0,2},{2,0},{1,3},{3,1},{4,6},{6,4},{5,7},{7,5},{8,10},{10,8},{9,1... | collective-permute-start | bytes 1327112 | tf_op jit(solution)/shard_map/ppermute | solution.py:691
  233.2 24.7 %collective-permute-start.9 = (bf16[768,384]{1,0:T(8,128)(2,1)}, bf16[768,384]{1,0:T(8,128)(2,1)S(1)}, u32[]{:S(2)}, u32[]{:S(2)}) collective-permute-start(bf16[768,384]{1,0:T(8,128)(2,1)} %shard_map.282), channel_id=1, source_target_pairs={{0,2},{2,0},{1,3},{3,1},{4,6},{6,4},{5,7},{7,5},{8,10},{10,8},{9,1... | collective-permute-start | bytes 1769480 | tf_op jit(solution)/shard_map/ppermute | solution.py:691
  235.5 21.2 %collective-permute-start.15 = (f32[8,128]{1,0:T(8,128)S(1)}, f32[8,128]{1,0:T(8,128)S(1)}, u32[]{:S(2)}, u32[]{:S(2)}) collective-permute-start(f32[8,128]{1,0:T(8,128)S(1)} %broadcast_in_dim.11), channel_id=1, source_target_pairs={{0,1},{1,0},{2,3},{3,2},{4,5},{5,4},{6,7},{7,6},{8,9},{9,8},{10,11... | collective-permute-start | bytes 12296 | tf_op jit(solution)/shard_map/ppermute | solution.py:688
  257.8 54.1 %collective-permute-start.14 = (bf16[384,1536]{1,0:T(8,128)(2,1)}, bf16[384,1536]{1,0:T(8,128)(2,1)}, u32[]{:S(2)}, u32[]{:S(2)}) collective-permute-start(bf16[384,1536]{1,0:T(8,128)(2,1)} %multiply_convert_fusion.1.refs_0_), channel_id=1, source_target_pairs={{0,2},{2,0},{1,3},{3,1},{4,6},{6,4},{5,7},{7,5},{8,10},{10,8},{9,1... | collective-permute-start | bytes 3538952 | tf_op jit(solution)/shard_map/ppermute | solution.py:691
  261.3 50.6 %collective-permute-start.12 = (bf16[768,1536]{1,0:T(8,128)(2,1)}, bf16[768,1536]{1,0:T(8,128)(2,1)S(1)}, u32[]{:S(2)}, u32[]{:S(2)}) collective-permute-start(bf16[768,1536]{1,0:T(8,128)(2,1)} %pad_maximum_fusion.3), channel_id=1, source_target_pairs={{0,2},{2,0},{1,3},{3,1},{4,6},{6,4},{5,7},{7,5},{8,10},{10,8},{9,1... | collective-permute-start | bytes 7077896 | tf_op jit(solution)/shard_map/ppermute | solution.py:691
  294.5 37.0 %collective-permute-start.13 = (bf16[768,1536]{1,0:T(8,128)(2,1)}, bf16[768,1536]{1,0:T(8,128)(2,1)}, u32[]{:S(2)}, u32[]{:S(2)}) collective-permute-start(bf16[768,1536]{1,0:T(8,128)(2,1)} %shard_map.284), channel_id=1, source_target_pairs={{0,2},{2,0},{1,3},{3,1},{4,6},{6,4},{5,7},{7,5},{8,10},{10,8},{9,1... | collective-permute-start | bytes 7077896 | tf_op jit(solution)/shard_map/ppermute | solution.py:691
  303.1 28.4 %collective-permute-start.11 = (bf16[384,1536]{1,0:T(8,128)(2,1)S(1)}, bf16[384,1536]{1,0:T(8,128)(2,1)S(1)}, u32[]{:S(2)}, u32[]{:S(2)}) collective-permute-start(bf16[384,1536]{1,0:T(8,128)(2,1)S(1)} %fusion.26), channel_id=1, source_target_pairs={{0,1},{1,0},{2,3},{3,2},{4,5},{5,4},{6,7},{7,6},{8,9},{9,8},{10,11... | collective-permute-start | bytes 3538952 | tf_op jit(solution)/shard_map/ppermute | solution.py:688
  335.4 26.9 %collective-permute-start.17 = (bf16[384,1536]{1,0:T(8,128)(2,1)S(1)}, bf16[384,1536]{1,0:T(8,128)(2,1)S(1)}, u32[]{:S(2)}, u32[]{:S(2)}) collective-permute-start(bf16[384,1536]{1,0:T(8,128)(2,1)S(1)} %get-tuple-element.380.g_in.refs_0_), channel_id=1, source_target_pairs={{0,2},{2,0},{1,3},{3,1},{4,6},{6,4},{5,7},{7,5},{8,10},{10,8},{9,1... | collective-permute-start | bytes 3538952 | tf_op jit(solution)/shard_map/ppermute | solution.py:691
  335.4 28.4 %collective-permute-start.16 = (bf16[384,1536]{1,0:T(8,128)(2,1)S(1)}, bf16[384,1536]{1,0:T(8,128)(2,1)S(1)}, u32[]{:S(2)}, u32[]{:S(2)}) collective-permute-start(bf16[384,1536]{1,0:T(8,128)(2,1)S(1)} %get-tuple-element.380.g_in.refs_0_), channel_id=1, source_target_pairs={{0,1},{1,0},{2,3},{3,2},{4,5},{5,4},{6,7},{7,6},{8,9},{9,8},{10,11... | collective-permute-start | bytes 3538952 | tf_op jit(solution)/shard_map/ppermute | solution.py:688
  364.8 12.1 %collective-permute-start.19 = (bf16[2,384,1536]{2,1,0:T(8,128)(2,1)}, bf16[2,384,1536]{2,1,0:T(8,128)(2,1)S(1)}, u32[]{:S(2)}, u32[]{:S(2)}) collective-permute-start(bf16[2,384,1536]{2,1,0:T(8,128)(2,1)} %get-tuple-element.188), channel_id=1, source_target_pairs={{0,2},{2,0},{1,3},{3,1},{4,6},{6,4},{5,7},{7,5},{8,10},{10,8},{9,1... | collective-permute-start | bytes 7077896 | tf_op jit(solution)/shard_map/ppermute | solution.py:691
  365.1 11.8 %collective-permute-start.18 = (bf16[384,1536]{1,0:T(8,128)(2,1)}, bf16[384,1536]{1,0:T(8,128)(2,1)}, u32[]{:S(2)}, u32[]{:S(2)}) collective-permute-start(bf16[384,1536]{1,0:T(8,128)(2,1)} %copy-done.24), channel_id=1, source_target_pairs={{0,2},{2,0},{1,3},{3,1},{4,6},{6,4},{5,7},{7,5},{8,10},{10,8},{9,1... | collective-permute-start | bytes 3538952 | tf_op jit(solution)/shard_map/ppermute | solution.py:691
  377.9 17.4 %collective-permute-start.20 = (bf16[384,768]{1,0:T(8,128)(2,1)}, bf16[384,768]{1,0:T(8,128)(2,1)S(1)}, u32[]{:S(2)}, u32[]{:S(2)}) collective-permute-start(bf16[384,768]{1,0:T(8,128)(2,1)} %slice.224), channel_id=1, source_target_pairs={{0,1},{1,0},{2,3},{3,2},{4,5},{5,4},{6,7},{7,6},{8,9},{9,8},{10,11... | collective-permute-start | bytes 1769480 | tf_op jit(solution)/shard_map/ppermute | solution.py:688
  396.2 19.5 %collective-permute-start.21 = (bf16[2,384,1536]{2,1,0:T(8,128)(2,1)}, bf16[2,384,1536]{2,1,0:T(8,128)(2,1)S(1)}, u32[]{:S(2)}, u32[]{:S(2)}) collective-permute-start(bf16[2,384,1536]{2,1,0:T(8,128)(2,1)} %get-tuple-element.199), channel_id=1, source_target_pairs={{0,2},{2,0},{1,3},{3,1},{4,6},{6,4},{5,7},{7,5},{8,10},{10,8},{9,1... | collective-permute-start | bytes 7077896 | tf_op jit(solution)/shard_map/ppermute | solution.py:691
  396.4 36.5 %collective-permute-start.23 = (bf16[768,896]{1,0:T(8,128)(2,1)}, bf16[768,896]{1,0:T(8,128)(2,1)}, u32[]{:S(2)}, u32[]{:S(2)}) collective-permute-start(bf16[768,896]{1,0:T(8,128)(2,1)} %get-tuple-element.209), channel_id=1, source_target_pairs={{0,4},{4,0},{1,5},{5,1},{2,6},{6,2},{3,7},{7,3},{8,12},{12,8},{9,1... | collective-permute-start | bytes 4128776 | tf_op jit(solution)/shard_map/ppermute | solution.py:694
  401.8 13.9 %collective-permute-start.22 = (bf16[768,384]{1,0:T(8,128)(2,1)}, bf16[768,384]{1,0:T(8,128)(2,1)S(1)}, u32[]{:S(2)}, u32[]{:S(2)}) collective-permute-start(bf16[768,384]{1,0:T(8,128)(2,1)} %shard_map.290), channel_id=1, source_target_pairs={{0,2},{2,0},{1,3},{3,1},{4,6},{6,4},{5,7},{7,5},{8,10},{10,8},{9,1... | collective-permute-start | bytes 1769480 | tf_op jit(solution)/shard_map/ppermute | solution.py:691
  401.8 50.9 %collective-permute-start.25 = (bf16[384,1536]{1,0:T(8,128)(2,1)}, bf16[384,1536]{1,0:T(8,128)(2,1)}, u32[]{:S(2)}, u32[]{:S(2)}) collective-permute-start(bf16[384,1536]{1,0:T(8,128)(2,1)} %multiply_convert_fusion.1.refs_0_), channel_id=1, source_target_pairs={{0,1},{1,0},{2,3},{3,2},{4,5},{5,4},{6,7},{7,6},{8,9},{9,8},{10,11... | collective-permute-start | bytes 3538952 | tf_op jit(solution)/shard_map/ppermute | solution.py:688
  415.7 41.2 %collective-permute-start.26 = (bf16[384,1536]{1,0:T(8,128)(2,1)}, bf16[384,1536]{1,0:T(8,128)(2,1)}, u32[]{:S(2)}, u32[]{:S(2)}) collective-permute-start(bf16[384,1536]{1,0:T(8,128)(2,1)} %shard_map.289), channel_id=1, source_target_pairs={{0,1},{1,0},{2,3},{3,2},{4,5},{5,4},{6,7},{7,6},{8,9},{9,8},{10,11... | collective-permute-start | bytes 3538952 | tf_op jit(solution)/shard_map/ppermute | solution.py:688
  432.9 24.0 %collective-permute-start.24 = (bf16[768,640]{1,0:T(8,128)(2,1)}, bf16[768,640]{1,0:T(8,128)(2,1)S(1)}, u32[]{:S(2)}, u32[]{:S(2)}) collective-permute-start(bf16[768,640]{1,0:T(8,128)(2,1)} %get-tuple-element.219), channel_id=1, source_target_pairs={{0,4},{4,0},{1,5},{5,1},{2,6},{6,2},{3,7},{7,3},{8,12},{12,8},{9,1... | collective-permute-start | bytes 2949128 | tf_op jit(solution)/shard_map/ppermute | solution.py:694
  457.0 82.9 %reduce-scatter.11.cloned.1.call-start = ((), (), s32[]{:S(2)}) async-start(), calls=%async_computation.11 | async-start | bytes 1228800 | tf_op jit(solution)/shard_map/reduce_scatter | solution.py:831
  457.0 48.6 %collective-permute-start.29 = (bf16[768,1408]{1,0:T(8,128)(2,1)}, bf16[768,1408]{1,0:T(8,128)(2,1)}, u32[]{:S(2)}, u32[]{:S(2)}) collective-permute-start(bf16[768,1408]{1,0:T(8,128)(2,1)} %get-tuple-element.235), channel_id=1, source_target_pairs={{0,4},{4,0},{1,5},{5,1},{2,6},{6,2},{3,7},{7,3},{8,12},{12,8},{9,1... | collective-permute-start | bytes 6488072 | tf_op jit(solution)/shard_map/ppermute | solution.py:694
  461.6 142.6 %reduce-scatter.13.cloned.1.call-start = ((), (), s32[]{:S(2)}) async-start(), calls=%async_computation.12 | async-start | bytes 2703360 | tf_op jit(solution)/shard_map/reduce_scatter | solution.py:831
  467.5 33.3 %collective-permute-start.28 = (bf16[384,1536]{1,0:T(8,128)(2,1)}, bf16[384,1536]{1,0:T(8,128)(2,1)S(1)}, u32[]{:S(2)}, u32[]{:S(2)}) collective-permute-start(bf16[384,1536]{1,0:T(8,128)(2,1)} %get-tuple-element.241.g_in.refs_0_), channel_id=1, source_target_pairs={{0,2},{2,0},{1,3},{3,1},{4,6},{6,4},{5,7},{7,5},{8,10},{10,8},{9,1... | collective-permute-start | bytes 3538952 | tf_op jit(solution)/shard_map/ppermute | solution.py:691
  467.5 33.3 %collective-permute-start.27 = (bf16[384,1536]{1,0:T(8,128)(2,1)}, bf16[384,1536]{1,0:T(8,128)(2,1)}, u32[]{:S(2)}, u32[]{:S(2)}) collective-permute-start(bf16[384,1536]{1,0:T(8,128)(2,1)} %get-tuple-element.241.g_in.refs_0_), channel_id=1, source_target_pairs={{0,1},{1,0},{2,3},{3,2},{4,5},{5,4},{6,7},{7,6},{8,9},{9,8},{10,11... | collective-permute-start | bytes 3538952 | tf_op jit(solution)/shard_map/ppermute | solution.py:688
  510.1 124.2 %reduce-scatter.15.cloned.1.call-start = ((), (), s32[]{:S(2)}) async-start(), calls=%async_computation.13 | async-start | bytes 1474560 | tf_op jit(solution)/shard_map/reduce_scatter | solution.py:831
  510.2 3.3 collective-permute-start.33
  510.3 28.6 %collective-permute-start.31 = (bf16[768,768]{1,0:T(8,128)(2,1)}, bf16[768,768]{1,0:T(8,128)(2,1)S(1)}, u32[]{:S(2)}, u32[]{:S(2)}) collective-permute-start(bf16[768,768]{1,0:T(8,128)(2,1)} %get-tuple-element.240), channel_id=1, source_target_pairs={{0,4},{4,0},{1,5},{5,1},{2,6},{6,2},{3,7},{7,3},{8,12},{12,8},{9,1... | collective-permute-start | bytes 3538952 | tf_op jit(solution)/shard_map/ppermute | solution.py:694
  510.7 28.2 %collective-permute-start.32 = (bf16[384,1536]{1,0:T(8,128)(2,1)S(1)}, bf16[384,1536]{1,0:T(8,128)(2,1)}, u32[]{:S(2)}, u32[]{:S(2)}) collective-permute-start(bf16[384,1536]{1,0:T(8,128)(2,1)S(1)} %copy-done.18), channel_id=1, source_target_pairs={{0,2},{2,0},{1,3},{3,1},{4,6},{6,4},{5,7},{7,5},{8,10},{10,8},{9,1... | collective-permute-start | bytes 3538952 | tf_op jit(solution)/shard_map/ppermute | solution.py:691
  510.9 28.2 %collective-permute-start.30 = (bf16[384,1536]{1,0:T(8,128)(2,1)S(1)}, bf16[384,1536]{1,0:T(8,128)(2,1)S(1)}, u32[]{:S(2)}, u32[]{:S(2)}) collective-permute-start(bf16[384,1536]{1,0:T(8,128)(2,1)S(1)} %copy-done.18), channel_id=1, source_target_pairs={{0,1},{1,0},{2,3},{3,2},{4,5},{5,4},{6,7},{7,6},{8,9},{9,8},{10,11... | collective-permute-start | bytes 3538952 | tf_op jit(solution)/shard_map/ppermute | solution.py:688
  539.9 3.8 collective-permute-start.34
  543.6 123.8 %reduce-scatter.17.cloned.1.call-start = ((), (), s32[]{:S(2)}) async-start(), calls=%async_computation.14 | async-start | bytes 2457600 | tf_op jit(solution)/shard_map/reduce_scatter | solution.py:831
  555.4 48.9 %collective-permute-start.37 = (bf16[768,1280]{1,0:T(8,128)(2,1)}, bf16[768,1280]{1,0:T(8,128)(2,1)S(1)}, u32[]{:S(2)}, u32[]{:S(2)}) collective-permute-start(bf16[768,1280]{1,0:T(8,128)(2,1)} %shard_map.304), channel_id=1, source_target_pairs={{0,4},{4,0},{1,5},{5,1},{2,6},{6,2},{3,7},{7,3},{8,12},{12,8},{9,1... | collective-permute-start | bytes 5898248 | tf_op jit(solution)/shard_map/ppermute | solution.py:694
  557.5 46.7 %collective-permute-start.35 = (bf16[384,768]{1,0:T(8,128)(2,1)}, bf16[384,768]{1,0:T(8,128)(2,1)S(1)}, u32[]{:S(2)}, u32[]{:S(2)}) collective-permute-start(bf16[384,768]{1,0:T(8,128)(2,1)} %slice.225), channel_id=1, source_target_pairs={{0,1},{1,0},{2,3},{3,2},{4,5},{5,4},{6,7},{7,6},{8,9},{9,8},{10,11... | collective-permute-start | bytes 1769480 | tf_op jit(solution)/shard_map/ppermute | solution.py:688
  560.0 44.3 %collective-permute-start.36 = (bf16[144,1536]{1,0:T(8,128)(2,1)S(1)}, bf16[144,1536]{1,0:T(8,128)(2,1)S(1)}, u32[]{:S(2)}, u32[]{:S(2)}) collective-permute-start(bf16[144,1536]{1,0:T(8,128)(2,1)S(1)} %get-tuple-element.400), channel_id=1, source_target_pairs={{0,1},{1,0},{2,3},{3,2},{4,5},{5,4},{6,7},{7,6},{8,9},{9,8},{10,11... | collective-permute-start | bytes 1327112 | tf_op jit(solution)/shard_map/ppermute | solution.py:688
  609.9 101.1 %reduce-scatter.19.cloned.1.call-start = ((), (), s32[]{:S(2)}) async-start(), calls=%async_computation.15 | async-start | bytes 737280 | tf_op jit(solution)/shard_map/reduce_scatter | solution.py:831
  609.9 4.0 collective-permute-start.38
  610.0 16.5 %collective-permute-start.39 = (bf16[768,384]{1,0:T(8,128)(2,1)}, bf16[768,384]{1,0:T(8,128)(2,1)S(1)}, u32[]{:S(2)}, u32[]{:S(2)}) collective-permute-start(bf16[768,384]{1,0:T(8,128)(2,1)} %get-tuple-element.283), channel_id=1, source_target_pairs={{0,4},{4,0},{1,5},{5,1},{2,6},{6,2},{3,7},{7,3},{8,12},{12,8},{9,1... | collective-permute-start | bytes 1769480 | tf_op jit(solution)/shard_map/ppermute | solution.py:694
  626.5 40.9 %collective-permute-start.43 = (bf16[768,1152]{1,0:T(8,128)(2,1)}, bf16[768,1152]{1,0:T(8,128)(2,1)S(1)}, u32[]{:S(2)}, u32[]{:S(2)}) collective-permute-start(bf16[768,1152]{1,0:T(8,128)(2,1)} %get-tuple-element.287), channel_id=1, source_target_pairs={{0,4},{4,0},{1,5},{5,1},{2,6},{6,2},{3,7},{7,3},{8,12},{12,8},{9,1... | collective-permute-start | bytes 5308424 | tf_op jit(solution)/shard_map/ppermute | solution.py:694
  634.3 6.2 collective-permute-start.42
  637.8 107.6 %reduce-scatter.21.cloned.1.call-start = ((), (), s32[]{:S(2)}) async-start(), calls=%async_computation.16 | async-start | bytes 2211840 | tf_op jit(solution)/shard_map/reduce_scatter | solution.py:831
  637.8 2.7 collective-permute-start.41
  672.7 85.0 %reduce-scatter.23.cloned.1.call-start = ((), (), s32[]{:S(2)}) async-start(), calls=%async_computation.17 | async-start | bytes 2211840 | tf_op jit(solution)/shard_map/reduce_scatter | solution.py:831
  673.7 27.7 %collective-permute-start.45 = (bf16[384,1536]{1,0:T(8,128)(2,1)}, bf16[384,1536]{1,0:T(8,128)(2,1)}, u32[]{:S(2)}, u32[]{:S(2)}) collective-permute-start(bf16[384,1536]{1,0:T(8,128)(2,1)} %get-tuple-element.308), channel_id=1, source_target_pairs={{0,1},{1,0},{2,3},{3,2},{4,5},{5,4},{6,7},{7,6},{8,9},{9,8},{10,11... | collective-permute-start | bytes 3538952 | tf_op jit(solution)/shard_map/ppermute | solution.py:688
  675.4 39.8 %collective-permute-start.44 = (bf16[768,1152]{1,0:T(8,128)(2,1)S(1)}, bf16[768,1152]{1,0:T(8,128)(2,1)}, u32[]{:S(2)}, u32[]{:S(2)}) collective-permute-start(bf16[768,1152]{1,0:T(8,128)(2,1)S(1)} %copy-done.33), channel_id=1, source_target_pairs={{0,4},{4,0},{1,5},{5,1},{2,6},{6,2},{3,7},{7,3},{8,12},{12,8},{9,1... | collective-permute-start | bytes 5308424 | tf_op jit(solution)/shard_map/ppermute | solution.py:694
  719.6 3.8 collective-permute-start.46
  720.5 9.0 %collective-permute-start.55 = (bf16[96,384]{1,0:T(8,128)(2,1)S(1)}, bf16[96,384]{1,0:T(8,128)(2,1)S(1)}, u32[]{:S(2)}, u32[]{:S(2)}) collective-permute-start(bf16[96,384]{1,0:T(8,128)(2,1)S(1)} %constant_dynamic-slice_fusion.2), channel_id=1, source_target_pairs={{0,2},{2,0},{1,3},{3,1},{4,6},{6,4},{5,7},{7,5},{8,10},{10,8},{9,1... | collective-permute-start | bytes 221192 | tf_op jit(solution)/shard_map/ppermute | solution.py:691
  720.6 10.4 %collective-permute-start.53 = (bf16[96,384]{1,0:T(8,128)(2,1)S(1)}, bf16[96,384]{1,0:T(8,128)(2,1)S(1)}, u32[]{:S(2)}, u32[]{:S(2)}) collective-permute-start(bf16[96,384]{1,0:T(8,128)(2,1)S(1)} %constant_dynamic-slice_fusion.4), channel_id=1, source_target_pairs={{0,2},{2,0},{1,3},{3,1},{4,6},{6,4},{5,7},{7,5},{8,10},{10,8},{9,1... | collective-permute-start | bytes 221192 | tf_op jit(solution)/shard_map/ppermute | solution.py:691
  723.6 20.5 %collective-permute-start.56 = (bf16[96,1536]{1,0:T(8,128)(2,1)S(1)}, bf16[96,1536]{1,0:T(8,128)(2,1)S(1)}, u32[]{:S(2)}, u32[]{:S(2)}) collective-permute-start(bf16[96,1536]{1,0:T(8,128)(2,1)S(1)} %fusion.55), channel_id=1, source_target_pairs={{0,2},{2,0},{1,3},{3,1},{4,6},{6,4},{5,7},{7,5},{8,10},{10,8},{9,1... | collective-permute-start | bytes 884744 | tf_op jit(solution)/shard_map/ppermute | solution.py:691
  724.7 3.9 collective-permute-start.48
  725.7 17.2 %collective-permute-start.57 = (bf16[96,1536]{1,0:T(8,128)(2,1)S(1)}, bf16[96,1536]{1,0:T(8,128)(2,1)S(1)}, u32[]{:S(2)}, u32[]{:S(2)}) collective-permute-start(bf16[96,1536]{1,0:T(8,128)(2,1)S(1)} %fusion.57), channel_id=1, source_target_pairs={{0,2},{2,0},{1,3},{3,1},{4,6},{6,4},{5,7},{7,5},{8,10},{10,8},{9,1... | collective-permute-start | bytes 884744 | tf_op jit(solution)/shard_map/ppermute | solution.py:691
  728.6 17.9 %collective-permute-start.51 = (bf16[130,1536]{1,0:T(8,128)(2,1)S(1)}, bf16[130,1536]{1,0:T(8,128)(2,1)S(1)}, u32[]{:S(2)}, u32[]{:S(2)}) collective-permute-start(bf16[130,1536]{1,0:T(8,128)(2,1)S(1)} %slice.397), channel_id=1, source_target_pairs={{0,1},{1,0},{2,3},{3,2},{4,5},{5,4},{6,7},{7,6},{8,9},{9,8},{10,11... | collective-permute-start | bytes 1198088 | tf_op jit(solution)/shard_map/ppermute | solution.py:688
  729.5 5.4 collective-permute-start.49
  734.9 6.1 collective-permute-start.50
  (75 other events, 537.8 us)
Sparse Core Ops, SparseCore 0:
  14.9 103.4 all-gather.2
  120.0 143.9 all-gather.4
  457.1 31.2 reduce-scatter.8
  490.7 24.9 reduce-scatter.10
  518.4 43.5 reduce-scatter.12
  564.2 28.5 reduce-scatter.14
  610.0 40.7 reduce-scatter.16
  653.1 21.1 reduce-scatter.18
  676.7 36.8 reduce-scatter.20
  719.6 38.1 reduce-scatter.22
